TPU v7x, 128 devices: a whole 4x4x4 slice. The times are simulated.
128 devices in a mesh: section: 4 (over y_hi, core), rep: 32 (over y_lo, x, z).
Axes of the slice: x: 4, y: 4 (y_hi: 2, y_lo: 2; y = y_hi * 2 + y_lo), z: 4, core: 2. Of those that a mesh axis runs over, the one named last changes fastest.
Arguments:
- block_inputs: bfloat16 [2, 2, 32, 3072], P(None, None, 'rep'), may hold values from -6 to 6
- routes: int32 [2, 3, 2, 4], replicated, may hold values from 0 to 1
- cotangent: bfloat16 [2, 4, 32, 3072], P(None, None, 'rep'), may hold values from -6 to 6
- gossip_peer: int32 [4, 2], replicated, may hold values from 0 to 1, as said below
- w_in: bfloat16 [4, 3072, 24576], P('section', None, 'rep'), may hold values from -6 to 6
- w_out: bfloat16 [4, 24576, 3072], P('section', 'rep'), may hold values from -6 to 6
Outputs:
- new_in: bfloat16 [4, 3072, 24576], P('section', None, 'rep')
- new_out: bfloat16 [4, 24576, 3072], P('section', 'rep')
Inputs may be any that keep to these rules, and one draw needn't show every extreme that they name: `gossip_peer`: row s maps each replica to itself or to the other replica, the same way for the whole row; at least one row pairs the two replicas.
All inputs are finite; a program needn't handle non-finite values.
Results may differ from a plain program's by a relative error of at most 0.017.
Values may be sent and summed in bfloat16 or wider, within the bound.
A program may use at most 256 MiB of HBM per device.

v0:
```python
import jax
import jax.numpy as jnp
from jax import lax
from jax.sharding import PartitionSpec as P

EPSILON = 1e-06
GELU_SCALE = 0.7978845608028654
LEARNING = 8.0


def swapped(value, axis, apart):
    mask = 2**apart
    pairs = [(source, source ^ mask) for source in range(lax.axis_size(axis))]
    return lax.ppermute(value, axis, pairs)


def passed_along(value, axis, steps):
    count = lax.axis_size(axis)
    leading, last = (max(0, -steps), min(count, count - steps))
    return lax.ppermute(value, axis, [(source, source + steps) for source in range(leading, last)])


def gelu_parts(preact):
    inner = GELU_SCALE * (preact + 0.044715 * preact * preact * preact)
    tanh_val = jnp.tanh(inner)
    gelu_val = 0.5 * preact * (1.0 + tanh_val)
    slopes = 0.5 * (1.0 + tanh_val) + 0.5 * preact * (1.0 - tanh_val * tanh_val) * GELU_SCALE * (
        1.0 + 3.0 * 0.044715 * preact * preact
    )
    return (gelu_val, slopes)


def route_tables(routes, blocks):
    micro_count, bound_count, replicas, capacity = routes.shape
    slot_ids = jnp.arange(capacity, dtype=jnp.int32)
    replica_ids = jnp.arange(replicas, dtype=jnp.int32)
    live_now = jnp.broadcast_to(slot_ids[None, None, :] < blocks, (micro_count, replicas, capacity))
    link_list = []
    live_list = [live_now]
    for bound_idx in range(bound_count):
        target = jnp.where(live_now, routes[:, bound_idx], -1).reshape(
            micro_count, replicas * capacity
        )
        matches = (target[:, :, None] == replica_ids[None, None, :]).astype(jnp.int32)
        before = jnp.cumsum(matches, axis=1) - matches
        position = jnp.sum(matches * before, axis=2)
        link_table = matches[:, :, :, None] * (
            position[:, :, None, None] == slot_ids[None, None, None, :]
        ).astype(jnp.int32)
        link_table = link_table.reshape(micro_count, replicas, capacity, replicas, capacity)
        link_list.append(link_table.astype(jnp.float32))
        live_now = jnp.sum(link_table, axis=(1, 2)) > 0
        live_list.append(live_now)
    return (link_list, live_list)


def share_sum(partial_value, shard_idx, group_bits):
    current = partial_value
    for bit_pos in reversed(range(group_bits)):
        half_size = current.shape[0] // 2
        upper_bit = jnp.bitwise_and(jnp.right_shift(shard_idx, bit_pos), 1) == 1
        kept_half = jnp.where(upper_bit, current[half_size:], current[:half_size])
        sent_half = jnp.where(upper_bit, current[:half_size], current[half_size:])
        current = kept_half + swapped(sent_half.astype(jnp.bfloat16), "rep", bit_pos).astype(
            sent_half.dtype
        )
    return current[0]


def gather_rows(row_piece, shard_idx, group_bits):
    current = row_piece[None]
    for bit_pos in range(group_bits):
        partner_rows = swapped(current, "rep", bit_pos)
        upper_bit = jnp.bitwise_and(jnp.right_shift(shard_idx, bit_pos), 1) == 1
        current = jnp.where(
            upper_bit,
            jnp.concatenate([partner_rows, current], axis=0),
            jnp.concatenate([current, partner_rows], axis=0),
        )
    return current


def layer_front(flat_rows, weight_in, scale_in):
    widened = flat_rows.astype(jnp.float32)
    inverse = lax.rsqrt(jnp.mean(widened * widened, axis=-1, keepdims=True) + EPSILON)
    normed = (widened * inverse).astype(jnp.bfloat16)
    preact = jnp.dot(normed, weight_in, preferred_element_type=jnp.float32) * scale_in
    return (widened, inverse, normed, preact)


def own_part(flat_array, layout, shard_idx):
    return lax.dynamic_index_in_dim(flat_array.reshape(layout), shard_idx, 0, keepdims=False)


def layer_rest(widened, preact, weight_out, scale_out, layout, shard_idx, group_bits):
    gelu_val, slopes = gelu_parts(preact)
    activated = gelu_val.astype(jnp.bfloat16)
    partial_value = jnp.dot(activated, weight_out, preferred_element_type=jnp.float32) * scale_out
    summed = share_sum(partial_value.reshape(layout), shard_idx, group_bits)
    return (own_part(widened, layout, shard_idx) + summed).astype(jnp.bfloat16)


def layer_backward(
    inputs,
    normed,
    preact,
    weight_in,
    weight_out,
    up_full,
    up_piece,
    scale_in,
    scale_out,
    layout,
    shard_idx,
    group_bits,
):
    widened = inputs.astype(jnp.float32)
    inverse = lax.rsqrt(jnp.mean(widened * widened, axis=-1, keepdims=True) + EPSILON)
    gelu_val, slopes = gelu_parts(preact)
    activated = gelu_val.astype(jnp.bfloat16)
    d_out = (
        lax.dot_general(
            activated, up_full, (((0,), (0,)), ((), ())), preferred_element_type=jnp.float32
        )
        * scale_out
    )
    d_act = (
        lax.dot_general(
            up_full, weight_out, (((1,), (1,)), ((), ())), preferred_element_type=jnp.float32
        )
        * scale_out
    )
    d_pre = (d_act * slopes).astype(jnp.bfloat16)
    d_in = (
        lax.dot_general(normed, d_pre, (((0,), (0,)), ((), ())), preferred_element_type=jnp.float32)
        * scale_in
    )
    d_normed = (
        lax.dot_general(
            d_pre, weight_in, (((1,), (1,)), ((), ())), preferred_element_type=jnp.float32
        )
        * scale_in
    )
    normed_piece = share_sum(d_normed.reshape(layout), shard_idx, group_bits)
    wide_piece = own_part(widened, layout, shard_idx)
    inv_piece = own_part(inverse, layout[:-1] + (1,), shard_idx)
    grad_piece = (
        up_piece.astype(jnp.float32)
        + inv_piece * normed_piece
        - wide_piece
        * inv_piece
        * inv_piece
        * inv_piece
        * jnp.mean(normed_piece * wide_piece, axis=-1, keepdims=True)
    )
    return (grad_piece.astype(jnp.bfloat16), d_in, d_out)


def send_ahead(outbound, group_size, rep_count, replicas):
    moved = passed_along(outbound, "section", 1)
    spread = jnp.broadcast_to(moved[:, None], (replicas, group_size) + moved.shape[1:])
    spread = spread.reshape((rep_count,) + moved.shape[1:])
    received = lax.all_to_all(spread, "rep", split_axis=0, concat_axis=0, tiled=True)
    received = received.reshape((replicas, group_size) + moved.shape[1:])
    merged = jnp.sum(received.astype(jnp.float32), axis=0).astype(jnp.bfloat16)
    return merged.reshape(-1, moved.shape[-1])


def send_back(grad_piece, group_size, rep_count, replicas):
    moved = passed_along(grad_piece, "section", -1)
    spread = jnp.broadcast_to(moved[None], (rep_count,) + moved.shape)
    received = lax.all_to_all(spread, "rep", split_axis=0, concat_axis=0, tiled=True)
    return received.reshape((replicas, group_size) + moved.shape)


def stash(stack, item, slot_idx, usable):
    current = lax.dynamic_index_in_dim(stack, slot_idx, 0, keepdims=False)
    return lax.dynamic_update_index_in_dim(stack, jnp.where(usable, item, current), slot_idx, 0)


def on_device(block_inputs, routes, cotangent, gossip_peer, w_in, w_out):
    section_count = lax.axis_size("section")
    rep_count = lax.axis_size("rep")
    replicas = gossip_peer.shape[1]
    group_size = rep_count // replicas
    group_bits = group_size.bit_length() - 1
    my_section = lax.axis_index("section")
    rep_idx = lax.axis_index("rep")
    replica = rep_idx // group_size
    shard_idx = rep_idx % group_size
    micro_count, blocks, piece_rows, model_width = block_inputs.shape
    capacity = cotangent.shape[1]
    weight_in = w_in[0]
    weight_out = w_out[0]
    hidden = weight_in.shape[1]
    scale_in = model_width ** (-0.5)
    scale_out = (hidden * group_size) ** (-0.5)
    layout = (group_size, capacity, piece_rows, model_width)
    link_list, live_list = route_tables(routes, blocks)
    link_stack = jnp.stack(link_list + [jnp.zeros_like(link_list[0])])
    own_links = lax.dynamic_index_in_dim(link_stack, my_section, 0, keepdims=False)
    own_links = lax.dynamic_index_in_dim(own_links, replica, 1, keepdims=False)
    own_flat = own_links.reshape(micro_count, capacity, replicas * capacity).astype(jnp.bfloat16)
    last_live = lax.dynamic_index_in_dim(live_list[section_count - 1], replica, 1, keepdims=False)
    tick_count = micro_count + section_count - 1
    flat_count = group_size * capacity * piece_rows
    kept_inputs = jnp.zeros((micro_count, flat_count, model_width), jnp.bfloat16)
    arrived = jnp.zeros((flat_count, model_width), jnp.bfloat16)
    for moment in range(tick_count):
        offset = moment - my_section
        usable = jnp.logical_and(offset >= 0, offset < micro_count)
        slot_idx = jnp.clip(offset, 0, micro_count - 1)
        flat_rows = arrived
        if moment < micro_count:
            opening = jnp.concatenate(
                [
                    block_inputs[moment],
                    jnp.zeros((capacity - blocks, piece_rows, model_width), jnp.bfloat16),
                ],
                axis=0,
            )
            opened = gather_rows(opening, shard_idx, group_bits).reshape(flat_count, model_width)
            flat_rows = jnp.where(my_section == 0, opened, arrived)
        kept_inputs = stash(kept_inputs, flat_rows, slot_idx, usable)
        if moment < tick_count - 1:
            widened, inverse, normed, preact = layer_front(flat_rows, weight_in, scale_in)
            out_piece = layer_rest(
                widened, preact, weight_out, scale_out, layout, shard_idx, group_bits
            )
        if moment < tick_count - 1:
            routing = lax.dynamic_index_in_dim(own_flat, slot_idx, 0, keepdims=False)
            outbound = lax.dot_general(
                routing,
                out_piece.reshape(capacity, piece_rows * model_width),
                (((0,), (0,)), ((), ())),
                preferred_element_type=jnp.float32,
            )
            outbound = outbound.astype(jnp.bfloat16).reshape(
                replicas, capacity, piece_rows, model_width
            )
            arrived = send_ahead(outbound, group_size, rep_count, replicas)
    accum_in = jnp.zeros((model_width, hidden), jnp.float32)
    accum_out = jnp.zeros((hidden, model_width), jnp.float32)
    routed = jnp.zeros((replicas, group_size, capacity, piece_rows, model_width), jnp.bfloat16)
    for moment in range(tick_count):
        offset = moment - (section_count - 1 - my_section)
        usable = jnp.logical_and(offset >= 0, offset < micro_count)
        slot_idx = jnp.clip(offset, 0, micro_count - 1)
        routing = lax.dynamic_index_in_dim(own_flat, slot_idx, 0, keepdims=False)
        placed_full = jnp.einsum(
            "kqj,qgjpd->gkpd",
            routing.reshape(capacity, replicas, capacity),
            routed,
            preferred_element_type=jnp.float32,
        ).astype(jnp.bfloat16)
        placed = lax.dynamic_index_in_dim(placed_full, shard_idx, 0, keepdims=False)
        placed_flat = placed_full.reshape(flat_count, model_width)
        if moment < micro_count:
            opening = jnp.where(
                last_live[moment][:, None, None], cotangent[moment], jnp.zeros((), jnp.bfloat16)
            )
            opened = gather_rows(opening, shard_idx, group_bits).reshape(flat_count, model_width)
            at_end = my_section == section_count - 1
            up_piece = jnp.where(at_end, opening, placed)
            up_full = jnp.where(at_end, opened, placed_flat)
        else:
            up_piece = placed
            up_full = placed_flat
        inputs = lax.dynamic_index_in_dim(kept_inputs, slot_idx, 0, keepdims=False)
        widened, inverse, normed, preact = layer_front(inputs, weight_in, scale_in)
        grad_piece, d_in, d_out = layer_backward(
            inputs,
            normed,
            preact,
            weight_in,
            weight_out,
            up_full,
            up_piece,
            scale_in,
            scale_out,
            layout,
            shard_idx,
            group_bits,
        )
        accum_in = accum_in + jnp.where(usable, d_in, 0.0)
        accum_out = accum_out + jnp.where(usable, d_out, 0.0)
        if moment < tick_count - 1:
            routed = send_back(grad_piece, group_size, rep_count, replicas)
    stepped_in = (weight_in.astype(jnp.float32) - LEARNING * accum_in).astype(jnp.bfloat16)
    stepped_out = (weight_out.astype(jnp.float32) - LEARNING * accum_out).astype(jnp.bfloat16)
    partner = gossip_peer[my_section, replica]
    paired = partner != replica
    other_in = swapped(stepped_in, "rep", group_bits)
    other_out = swapped(stepped_out, "rep", group_bits)
    chosen_in = jnp.where(paired, other_in, stepped_in)
    chosen_out = jnp.where(paired, other_out, stepped_out)
    new_in = (0.5 * (stepped_in.astype(jnp.float32) + chosen_in.astype(jnp.float32))).astype(
        jnp.bfloat16
    )
    new_out = (0.5 * (stepped_out.astype(jnp.float32) + chosen_out.astype(jnp.float32))).astype(
        jnp.bfloat16
    )
    return (new_in[None], new_out[None])


def solution(mesh):
    return jax.shard_map(
        on_device,
        mesh=mesh,
        in_specs=(
            P(None, None, "rep", None),
            P(),
            P(None, None, "rep", None),
            P(),
            P("section", None, "rep"),
            P("section", "rep", None),
        ),
        out_specs=(P("section", None, "rep"), P("section", "rep", None)),
        check_vma=False,
    )
```

profile of v0, /device:TPU:16, one launch (start us, length us, event | category | flops | bytes accessed | tf_op | source)
XLA Modules:
  0.0 739.4 jit_solution(9616093420158281156)
XLA Ops:
  30.5 5.9 fusion.58
  68.5 7.6 %all-to-all-start = ((bf16[32,4,1,3072]{3,1,2,0:T(4,128)(2,1)}), bf16[32,4,1,3072]{3,1,2,0:T(4,128)(2,1)S(1)}, u32[]{:S(2)}, u32[]{:S(2)}) async-start(bf16[32,4,1,3072]{3,1,2,0:T(4,128)(2,1)} %bitcast.27), calls=%async_computation | async-start | bytes 1572864 | tf_op jit(solution)/shard_map/all_to_all | solution.py:163
  80.3 8.8 %all-to-all-done = bf16[32,4,1,3072]{3,1,2,0:T(4,128)(2,1)S(1)} async-done(((bf16[32,4,1,3072]{3,1,2,0:T(4,128)(2,1)}), bf16[32,4,1,3072]{3,1,2,0:T(4,128)(2,1)S(1)}, u32[]{:S(2)}, u32[]{:S(2)}) %all-to-all-start) | async-done | bytes 786464 | tf_op jit(solution)/shard_map/all_to_all | solution.py:163
  91.3 5.9 fusion.61
  98.9 6.5 collective-permute-done.13
  134.2 11.4 %all-to-all-done.1 = bf16[32,4,1,3072]{3,1,2,0:T(4,128)(2,1)S(1)} async-done(((bf16[32,4,1,3072]{3,1,2,0:T(4,128)(2,1)}), bf16[32,4,1,3072]{3,1,2,0:T(4,128)(2,1)S(1)}, u32[]{:S(2)}, u32[]{:S(2)}) %all-to-all-start.1) | async-done | bytes 786464 | tf_op jit(solution)/shard_map/all_to_all | solution.py:163
  147.0 5.9 fusion.64
  154.8 6.5 collective-permute-done.18
  192.9 8.5 %all-to-all-done.2 = bf16[32,4,1,3072]{3,1,2,0:T(4,128)(2,1)S(1)} async-done(((bf16[32,4,1,3072]{3,1,2,0:T(4,128)(2,1)}), bf16[32,4,1,3072]{3,1,2,0:T(4,128)(2,1)S(1)}, u32[]{:S(2)}, u32[]{:S(2)}) %all-to-all-start.2) | async-done | bytes 786464 | tf_op jit(solution)/shard_map/all_to_all | solution.py:163
  202.9 5.9 fusion.67
  211.1 7.0 collective-permute-done.23
  242.6 5.8 all-to-all-start.3
  248.7 11.2 %all-to-all-done.3 = bf16[32,4,1,3072]{3,1,2,0:T(4,128)(2,1)S(1)} async-done(((bf16[32,4,1,3072]{3,1,2,0:T(4,128)(2,1)}), bf16[32,4,1,3072]{3,1,2,0:T(4,128)(2,1)S(1)}, u32[]{:S(2)}, u32[]{:S(2)}) %all-to-all-start.3) | async-done | bytes 786464 | tf_op jit(solution)/shard_map/all_to_all | solution.py:163
  271.0 6.5 collective-permute-done.36
  308.9 9.9 %all-to-all-done.4 = bf16[32,4,1,3072]{3,1,2,0:T(4,128)(2,1)S(1)} async-done(((bf16[32,4,1,3072]{3,1,2,0:T(4,128)(2,1)}), bf16[32,4,1,3072]{3,1,2,0:T(4,128)(2,1)S(1)}, u32[]{:S(2)}, u32[]{:S(2)}) %all-to-all-start.4) | async-done | bytes 786464 | tf_op jit(solution)/shard_map/all_to_all | solution.py:172
  333.1 5.4 collective-permute-done.41
  372.7 5.7 all-to-all-done.5
  485.5 6.8 all-to-all-start.7
  507.0 22.3 %subtract_convert_fusion.1 = bf16[3072,768]{1,0:T(8,128)(2,1)} fusion(f32[3072,768]{1,0:T(8,128)} %fusion.165, f32[3072,768]{1,0:T(8,128)} %fusion.163, f32[3072,768]{1,0:T(8,128)} %fusion.161, f32[3072,768]{1,0:T(8,128)} %fusion.159, bf16[1,3072,768]{2,1,0:T(8,128)(2,1)} %param.10, pred[]{:T(512)S(6)} %and.55, pred[]{:T(512)S(6)} %and.54, pred[]{:T(512)S(6)} %and.53, ...), kind=kOutput, calls=%fused_computation.3 | convolution fusion | flops 648069120 | bytes 52888072 | tf_op jit(solution)/shard_map/dot_general | solution.py:135
  530.7 18.5 %subtract_convert_fusion = bf16[768,3072]{1,0:T(8,128)(2,1)} fusion(f32[768,3072]{1,0:T(8,128)} %fusion.267, f32[768,3072]{1,0:T(8,128)} %fusion.266, f32[768,3072]{1,0:T(8,128)} %fusion.265, f32[768,3072]{1,0:T(8,128)} %fusion.264, bf16[64,3072]{1,0:T(8,128)(2,1)S(1)} %reshape.4028, bf16[1,768,3072]{2,1,0:T(8,128)(2,1)} %param.11, pred[]{:T(512)S(6)} %and.55, ...), kind=kOutput, calls=%fused_computation.1 | convolution fusion | flops 344948736 | bytes 47775748 | tf_op jit(solution)/shard_map/dot_general | solution.py:122
  551.3 83.2 %collective-permute-done.56 = bf16[3072,768]{1,0:T(8,128)(2,1)} collective-permute-done((bf16[3072,768]{1,0:T(8,128)(2,1)}, bf16[3072,768]{1,0:T(8,128)(2,1)}, u32[]{:S(2)}, u32[]{:S(2)}) %collective-permute-start.56) | collective-permute-done | bytes 4718624 | tf_op jit(solution)/shard_map/ppermute | solution.py:14
  634.6 9.3 %fusion = bf16[1,3072,768]{2,1,0:T(8,128)(2,1)} fusion(bf16[3072,768]{1,0:T(8,128)(2,1)} %subtract_convert_fusion.1, bf16[3072,768]{1,0:T(8,128)(2,1)} %collective-permute-done.56, pred[]{:T(512)S(6)} %ne.17), kind=kLoop, calls=%fused_computation.4 | loop fusion | flops 14155776 | bytes 14155777 | tf_op jit(solution)/shard_map/broadcast_in_dim | solution.py:303
  643.9 88.8 %collective-permute-done.57 = bf16[768,3072]{1,0:T(8,128)(2,1)} collective-permute-done((bf16[768,3072]{1,0:T(8,128)(2,1)}, bf16[768,3072]{1,0:T(8,128)(2,1)}, u32[]{:S(2)}, u32[]{:S(2)}) %collective-permute-start.57) | collective-permute-done | bytes 4718624 | tf_op jit(solution)/shard_map/ppermute | solution.py:14
  732.6 6.6 fusion.1
  (462 shorter events, 376.6 us)
Async XLA Ops:
  1.4 9.8 %collective-permute-start = (bf16[1,4,1,3072]{3,1,2,0:T(4,128)(2,1)S(1)}, bf16[1,4,1,3072]{3,1,2,0:T(4,128)(2,1)S(1)}, u32[]{:S(2)}, u32[]{:S(2)}) collective-permute-start(bf16[1,4,1,3072]{3,1,2,0:T(4,128)(2,1)S(1)} %get-tuple-element.29), channel_id=1, source_target_pairs={{0,1},{1,0},{2,3},{3,2},{4,5},{5,4},{6,7},{7,6},{8,9},{9,8},{10,11... | collective-permute-start | bytes 73736 | tf_op jit(solution)/shard_map/ppermute | solution.py:14
  3.4 43.0 %collective-permute-start.4 = (bf16[1,4,1,3072]{3,1,2,0:T(4,128)(2,1)S(1)}, bf16[1,4,1,3072]{3,1,2,0:T(4,128)(2,1)S(1)}, u32[]{:S(2)}, u32[]{:S(2)}) collective-permute-start(bf16[1,4,1,3072]{3,1,2,0:T(4,128)(2,1)S(1)} %get-tuple-element.27), channel_id=1, source_target_pairs={{0,1},{1,0},{2,3},{3,2},{4,5},{5,4},{6,7},{7,6},{8,9},{9,8},{10,11... | collective-permute-start | bytes 73736 | tf_op jit(solution)/shard_map/ppermute | solution.py:14
  62.6 13.7 %collective-permute-start.6 = (bf16[4,4,1,3072]{3,1,0,2:T(4,128)(2,1)S(1)}, bf16[4,4,1,3072]{3,1,0,2:T(4,128)(2,1)S(1)}, u32[]{:S(2)}, u32[]{:S(2)}) collective-permute-start(bf16[4,4,1,3072]{3,1,0,2:T(4,128)(2,1)S(1)} %maximum_select_fusion.11), channel_id=1, source_target_pairs={{0,4},{1,5},{2,6},{3,7},{4,0},{5,1},{6,2},{7,3},{8,12},{9,13},{10,... | collective-permute-start | bytes 294920 | tf_op jit(solution)/shard_map/ppermute | solution.py:14
  68.5 20.6 %all-to-all-start = ((bf16[32,4,1,3072]{3,1,2,0:T(4,128)(2,1)}), bf16[32,4,1,3072]{3,1,2,0:T(4,128)(2,1)S(1)}, u32[]{:S(2)}, u32[]{:S(2)}) async-start(bf16[32,4,1,3072]{3,1,2,0:T(4,128)(2,1)} %bitcast.27), calls=%async_computation | async-start | bytes 1572864 | tf_op jit(solution)/shard_map/all_to_all | solution.py:163
  76.5 13.4 %collective-permute-start.7 = (bf16[8,4,1,3072]{3,1,0,2:T(4,128)(2,1)S(1)}, bf16[8,4,1,3072]{3,1,0,2:T(4,128)(2,1)S(1)}, u32[]{:S(2)}, u32[]{:S(2)}) collective-permute-start(bf16[8,4,1,3072]{3,1,0,2:T(4,128)(2,1)S(1)} %maximum_select_fusion.2), channel_id=1, source_target_pairs={{0,8},{1,9},{2,10},{3,11},{4,12},{5,13},{6,14},{7,15},{8,0},{9,1},... | collective-permute-start | bytes 589832 | tf_op jit(solution)/shard_map/ppermute | solution.py:14
  113.7 9.3 %collective-permute-start.32 = (bf16[1,4,1,3072]{3,1,0,2:T(4,128)(2,1)S(1)}, bf16[1,4,1,3072]{3,1,0,2:T(4,128)(2,1)S(1)}, u32[]{:S(2)}, u32[]{:S(2)}) collective-permute-start(bf16[1,4,1,3072]{3,1,0,2:T(4,128)(2,1)S(1)} %bitcast.669), channel_id=1, source_target_pairs={{0,1},{1,0},{2,3},{3,2},{4,5},{5,4},{6,7},{7,6},{8,9},{9,8},{10,11... | collective-permute-start | bytes 73736 | tf_op jit(solution)/shard_map/ppermute | solution.py:14
  114.1 20.0 %collective-permute-start.28 = (bf16[1,4,1,3072]{3,1,2,0:T(4,128)(2,1)S(1)}, bf16[1,4,1,3072]{3,1,2,0:T(4,128)(2,1)S(1)}, u32[]{:S(2)}, u32[]{:S(2)}) collective-permute-start(bf16[1,4,1,3072]{3,1,2,0:T(4,128)(2,1)S(1)} %get-tuple-element.23), channel_id=1, source_target_pairs={{0,1},{1,0},{2,3},{3,2},{4,5},{5,4},{6,7},{7,6},{8,9},{9,8},{10,11... | collective-permute-start | bytes 73736 | tf_op jit(solution)/shard_map/ppermute | solution.py:14
  129.1 16.5 %all-to-all-start.1 = ((bf16[32,4,1,3072]{3,1,2,0:T(4,128)(2,1)}), bf16[32,4,1,3072]{3,1,2,0:T(4,128)(2,1)S(1)}, u32[]{:S(2)}, u32[]{:S(2)}) async-start(bf16[32,4,1,3072]{3,1,2,0:T(4,128)(2,1)} %bitcast.37), calls=%async_computation.1 | async-start | bytes 1572864 | tf_op jit(solution)/shard_map/all_to_all | solution.py:163
  153.0 8.3 %collective-permute-start.18 = (bf16[8,4,1,3072]{3,1,0,2:T(4,128)(2,1)S(1)}, bf16[8,4,1,3072]{3,1,0,2:T(4,128)(2,1)S(1)}, u32[]{:S(2)}, u32[]{:S(2)}) collective-permute-start(bf16[8,4,1,3072]{3,1,0,2:T(4,128)(2,1)S(1)} %convert_element_type.990), channel_id=1, source_target_pairs={{0,8},{1,9},{2,10},{3,11},{4,12},{5,13},{6,14},{7,15},{8,0},{9,1},... | collective-permute-start | bytes 589832 | tf_op jit(solution)/shard_map/ppermute | solution.py:14
  161.6 10.7 %collective-permute-start.33 = (bf16[2,4,1,3072]{3,1,0,2:T(4,128)(2,1)S(1)}, bf16[2,4,1,3072]{3,1,0,2:T(4,128)(2,1)S(1)}, u32[]{:S(2)}, u32[]{:S(2)}) collective-permute-start(bf16[2,4,1,3072]{3,1,0,2:T(4,128)(2,1)S(1)} %bitcast_select_fusion.5), channel_id=1, source_target_pairs={{0,2},{1,3},{2,0},{3,1},{4,6},{5,7},{6,4},{7,5},{8,10},{9,11},{10,... | collective-permute-start | bytes 147464 | tf_op jit(solution)/shard_map/ppermute | solution.py:14
  167.3 11.0 %collective-permute-start.29 = (bf16[2,4,1,3072]{3,1,0,2:T(4,128)(2,1)S(1)}, bf16[2,4,1,3072]{3,1,0,2:T(4,128)(2,1)S(1)}, u32[]{:S(2)}, u32[]{:S(2)}) collective-permute-start(bf16[2,4,1,3072]{3,1,0,2:T(4,128)(2,1)S(1)} %fusion.321), channel_id=1, source_target_pairs={{0,2},{1,3},{2,0},{3,1},{4,6},{5,7},{6,4},{7,5},{8,10},{9,11},{10,... | collective-permute-start | bytes 147464 | tf_op jit(solution)/shard_map/ppermute | solution.py:14
  173.1 122.9 %collective-permute-start.34 = (bf16[4,4,1,3072]{3,1,0,2:T(4,128)(2,1)}, bf16[4,4,1,3072]{3,1,0,2:T(4,128)(2,1)}, u32[]{:S(2)}, u32[]{:S(2)}) collective-permute-start(bf16[4,4,1,3072]{3,1,0,2:T(4,128)(2,1)} %maximum_select_fusion.15), channel_id=1, source_target_pairs={{0,4},{1,5},{2,6},{3,7},{4,0},{5,1},{6,2},{7,3},{8,12},{9,13},{10,... | collective-permute-start | bytes 294920 | tf_op jit(solution)/shard_map/ppermute | solution.py:14
  178.4 10.1 %collective-permute-start.30 = (bf16[4,4,1,3072]{3,1,0,2:T(4,128)(2,1)S(1)}, bf16[4,4,1,3072]{3,1,0,2:T(4,128)(2,1)S(1)}, u32[]{:S(2)}, u32[]{:S(2)}) collective-permute-start(bf16[4,4,1,3072]{3,1,0,2:T(4,128)(2,1)S(1)} %maximum_select_fusion.13), channel_id=1, source_target_pairs={{0,4},{1,5},{2,6},{3,7},{4,0},{5,1},{6,2},{7,3},{8,12},{9,13},{10,... | collective-permute-start | bytes 294920 | tf_op jit(solution)/shard_map/ppermute | solution.py:14
  184.3 17.1 %all-to-all-start.2 = ((bf16[32,4,1,3072]{3,1,2,0:T(4,128)(2,1)}), bf16[32,4,1,3072]{3,1,2,0:T(4,128)(2,1)S(1)}, u32[]{:S(2)}, u32[]{:S(2)}) async-start(bf16[32,4,1,3072]{3,1,2,0:T(4,128)(2,1)} %bitcast.43), calls=%async_computation.2 | async-start | bytes 1572864 | tf_op jit(solution)/shard_map/all_to_all | solution.py:163
  188.7 41.8 %collective-permute-start.31 = (bf16[8,4,1,3072]{3,1,0,2:T(4,128)(2,1)S(1)}, bf16[8,4,1,3072]{3,1,0,2:T(4,128)(2,1)}, u32[]{:S(2)}, u32[]{:S(2)}) collective-permute-start(bf16[8,4,1,3072]{3,1,0,2:T(4,128)(2,1)S(1)} %maximum_select_fusion.5), channel_id=1, source_target_pairs={{0,8},{1,9},{2,10},{3,11},{4,12},{5,13},{6,14},{7,15},{8,0},{9,1},... | collective-permute-start | bytes 589832 | tf_op jit(solution)/shard_map/ppermute | solution.py:14
  209.5 8.5 %collective-permute-start.23 = (bf16[8,4,1,3072]{3,1,0,2:T(4,128)(2,1)}, bf16[8,4,1,3072]{3,1,0,2:T(4,128)(2,1)}, u32[]{:S(2)}, u32[]{:S(2)}) collective-permute-start(bf16[8,4,1,3072]{3,1,0,2:T(4,128)(2,1)} %convert_element_type.1006), channel_id=1, source_target_pairs={{0,8},{1,9},{2,10},{3,11},{4,12},{5,13},{6,14},{7,15},{8,0},{9,1},... | collective-permute-start | bytes 589832 | tf_op jit(solution)/shard_map/ppermute | solution.py:14
  242.6 17.3 %all-to-all-start.3 = ((bf16[32,4,1,3072]{3,1,2,0:T(4,128)(2,1)}), bf16[32,4,1,3072]{3,1,2,0:T(4,128)(2,1)S(1)}, u32[]{:S(2)}, u32[]{:S(2)}) async-start(bf16[32,4,1,3072]{3,1,2,0:T(4,128)(2,1)} %bitcast.49), calls=%async_computation.3 | async-start | bytes 1572864 | tf_op jit(solution)/shard_map/all_to_all | solution.py:163
  297.2 11.7 %collective-permute-start.35 = (bf16[8,4,1,3072]{3,1,0,2:T(4,128)(2,1)S(1)}, bf16[8,4,1,3072]{3,1,0,2:T(4,128)(2,1)}, u32[]{:S(2)}, u32[]{:S(2)}) collective-permute-start(bf16[8,4,1,3072]{3,1,0,2:T(4,128)(2,1)S(1)} %maximum_select_fusion.7), channel_id=1, source_target_pairs={{0,8},{1,9},{2,10},{3,11},{4,12},{5,13},{6,14},{7,15},{8,0},{9,1},... | collective-permute-start | bytes 589832 | tf_op jit(solution)/shard_map/ppermute | solution.py:14
  299.2 19.7 %all-to-all-start.4 = ((bf16[32,4,1,3072]{3,1,2,0:T(4,128)(2,1)}), bf16[32,4,1,3072]{3,1,2,0:T(4,128)(2,1)S(1)}, u32[]{:S(2)}, u32[]{:S(2)}) async-start(bf16[32,4,1,3072]{3,1,2,0:T(4,128)(2,1)} %broadcast_in_dim.226), calls=%async_computation.4 | async-start | bytes 1572864 | tf_op jit(solution)/shard_map/all_to_all | solution.py:172
  359.5 18.9 %all-to-all-start.5 = ((bf16[32,4,1,3072]{3,1,2,0:T(4,128)(2,1)}), bf16[32,4,1,3072]{3,1,2,0:T(4,128)(2,1)}, u32[]{:S(2)}, u32[]{:S(2)}) async-start(bf16[32,4,1,3072]{3,1,2,0:T(4,128)(2,1)} %broadcast_in_dim.229), calls=%async_computation.5 | async-start | bytes 1572864 | tf_op jit(solution)/shard_map/all_to_all | solution.py:172
  417.4 19.1 %all-to-all-start.6 = ((bf16[32,4,1,3072]{3,1,2,0:T(4,128)(2,1)}), bf16[32,4,1,3072]{3,1,2,0:T(4,128)(2,1)S(1)}, u32[]{:S(2)}, u32[]{:S(2)}) async-start(bf16[32,4,1,3072]{3,1,2,0:T(4,128)(2,1)} %broadcast_in_dim.231), calls=%async_computation.6 | async-start | bytes 1572864 | tf_op jit(solution)/shard_map/all_to_all | solution.py:172
  485.5 20.7 %all-to-all-start.7 = ((bf16[32,4,1,3072]{3,1,2,0:T(4,128)(2,1)}), bf16[32,4,1,3072]{3,1,2,0:T(4,128)(2,1)S(1)}, u32[]{:S(2)}, u32[]{:S(2)}) async-start(bf16[32,4,1,3072]{3,1,2,0:T(4,128)(2,1)} %broadcast_in_dim.233), calls=%async_computation.7 | async-start | bytes 1572864 | tf_op jit(solution)/shard_map/all_to_all | solution.py:172
  529.3 105.2 %collective-permute-start.56 = (bf16[3072,768]{1,0:T(8,128)(2,1)}, bf16[3072,768]{1,0:T(8,128)(2,1)}, u32[]{:S(2)}, u32[]{:S(2)}) collective-permute-start(bf16[3072,768]{1,0:T(8,128)(2,1)} %subtract_convert_fusion.1), channel_id=1, source_target_pairs={{0,16},{1,17},{2,18},{3,19},{4,20},{5,21},{6,22},{7,23},{8,24},{9,... | collective-permute-start | bytes 14155784 | tf_op jit(solution)/shard_map/ppermute | solution.py:14
  549.2 183.4 %collective-permute-start.57 = (bf16[768,3072]{1,0:T(8,128)(2,1)}, bf16[768,3072]{1,0:T(8,128)(2,1)}, u32[]{:S(2)}, u32[]{:S(2)}) collective-permute-start(bf16[768,3072]{1,0:T(8,128)(2,1)} %subtract_convert_fusion), channel_id=1, source_target_pairs={{0,16},{1,17},{2,18},{3,19},{4,20},{5,21},{6,22},{7,23},{8,24},{9,... | collective-permute-start | bytes 14155784 | tf_op jit(solution)/shard_map/ppermute | solution.py:14
  (70 other events, 939.0 us)
where the time goes:
time: 749 us; the launch traced here: 739 us
  waiting for transfers between devices  359 us (48%)
  matrix products  159 us (21%)
  starting transfers between devices  133 us (18%)
  other arithmetic  52.5 us (7%)
  local copies, waits for them, and re-layouts  31.8 us (4%)
    ppermute x50, waiting for transfers between devices, swapped(): return lax.ppermute(value, axis, pairs)  277 us
    ppermute x50, starting transfers between devices, swapped(): return lax.ppermute(value, axis, pairs)  73.9 us
    dot_general x5, matrix products, layer_backward(): lax.dot_general(normed, d_pre, (((0,), (0,)), ((), ())), preferred_elemen...  42.7 us
    all_to_all x4, waiting for transfers between devices, send_ahead(): lax.all_to_all(spread, 'rep', split_axis=0, concat_axis=0, tiled=True)  39.8 us
    dot_general x5, matrix products, layer_backward(): lax.dot_general(activated, up_full, (((0,), (0,)), ((), ())), preferred_e...  38.8 us
    all_to_all x4, waiting for transfers between devices, send_back(): lax.all_to_all(spread, 'rep', split_axis=0, concat_axis=0, tiled=True)  23.6 us
    dot_general x4, matrix products, layer_rest(): jnp.dot(activated, weight_out, preferred_element_type=jnp.float32)  23.4 us
    all_to_all x4, starting transfers between devices, send_ahead(): lax.all_to_all(spread, 'rep', split_axis=0, concat_axis=0, tiled=True)  22.4 us
  transfers between devices with their start and end apart: 66, of which 47 were waited for; matrix products, arithmetic and copies ran while one was open for 21% of the time, Pallas kernels for 0%

commit v1 on v0

--- a/solution.py
+++ b/solution.py
@@ -156,6 +156,26 @@
     return (grad_piece.astype(jnp.bfloat16), d_in, d_out)
 
 
+def peer_grads(rows, ups, weight_in, weight_out, scale_in, scale_out):
+    widened, inverse, normed, preact = layer_front(rows, weight_in, scale_in)
+    gelu_val, slopes = gelu_parts(preact)
+    activated = gelu_val.astype(jnp.bfloat16)
+    d_out = (
+        lax.dot_general(activated, ups, (((0,), (0,)), ((), ())), preferred_element_type=jnp.float32)
+        * scale_out
+    )
+    d_act = (
+        lax.dot_general(ups, weight_out, (((1,), (1,)), ((), ())), preferred_element_type=jnp.float32)
+        * scale_out
+    )
+    d_pre = (d_act * slopes).astype(jnp.bfloat16)
+    d_in = (
+        lax.dot_general(normed, d_pre, (((0,), (0,)), ((), ())), preferred_element_type=jnp.float32)
+        * scale_in
+    )
+    return (d_in, d_out)
+
+
 def send_ahead(outbound, group_size, rep_count, replicas):
     moved = passed_along(outbound, "section", 1)
     spread = jnp.broadcast_to(moved[:, None], (replicas, group_size) + moved.shape[1:])
@@ -196,6 +216,8 @@
     scale_in = model_width ** (-0.5)
     scale_out = (hidden * group_size) ** (-0.5)
     layout = (group_size, capacity, piece_rows, model_width)
+    peer_in = swapped(weight_in, "rep", group_bits)
+    peer_out = swapped(weight_out, "rep", group_bits)
     link_list, live_list = route_tables(routes, blocks)
     link_stack = jnp.stack(link_list + [jnp.zeros_like(link_list[0])])
     own_links = lax.dynamic_index_in_dim(link_stack, my_section, 0, keepdims=False)
@@ -242,6 +264,7 @@
     accum_in = jnp.zeros((model_width, hidden), jnp.float32)
     accum_out = jnp.zeros((hidden, model_width), jnp.float32)
     routed = jnp.zeros((replicas, group_size, capacity, piece_rows, model_width), jnp.bfloat16)
+    kept_ups = jnp.zeros((micro_count, flat_count, model_width), jnp.bfloat16)
     for moment in range(tick_count):
         offset = moment - (section_count - 1 - my_section)
         usable = jnp.logical_and(offset >= 0, offset < micro_count)
@@ -266,6 +289,7 @@
         else:
             up_piece = placed
             up_full = placed_flat
+        kept_ups = stash(kept_ups, up_full, slot_idx, usable)
         inputs = lax.dynamic_index_in_dim(kept_inputs, slot_idx, 0, keepdims=False)
         widened, inverse, normed, preact = layer_front(inputs, weight_in, scale_in)
         grad_piece, d_in, d_out = layer_backward(
@@ -290,8 +314,11 @@
     stepped_out = (weight_out.astype(jnp.float32) - LEARNING * accum_out).astype(jnp.bfloat16)
     partner = gossip_peer[my_section, replica]
     paired = partner != replica
-    other_in = swapped(stepped_in, "rep", group_bits)
-    other_out = swapped(stepped_out, "rep", group_bits)
+    peer_rows = swapped(kept_inputs, "rep", group_bits).reshape(-1, model_width)
+    peer_ups = swapped(kept_ups, "rep", group_bits).reshape(-1, model_width)
+    peer_d_in, peer_d_out = peer_grads(peer_rows, peer_ups, peer_in, peer_out, scale_in, scale_out)
+    other_in = (peer_in.astype(jnp.float32) - LEARNING * peer_d_in).astype(jnp.bfloat16)
+    other_out = (peer_out.astype(jnp.float32) - LEARNING * peer_d_out).astype(jnp.bfloat16)
     chosen_in = jnp.where(paired, other_in, stepped_in)
     chosen_out = jnp.where(paired, other_out, stepped_out)
     new_in = (0.5 * (stepped_in.astype(jnp.float32) + chosen_in.astype(jnp.float32))).astype(

time: 749 us -> 757 us (1.011)
  waiting for transfers between devices: 359 us -> 308 us
  matrix products: 159 us -> 190 us
  starting transfers between devices: 133 us -> 149 us
  local copies, waits for them, and re-layouts: 31.8 us -> 45.6 us
    ppermute x50 -> x52, waiting for transfers between devices: 277 us -> 99.6 us  [swapped(): return lax.ppermute(value, axis, pairs)]
    ppermute x8, waiting for transfers between devices: 19 us -> 159 us  [passed_along(): lax.ppermute(value, axis, [(source, source + steps) for source in range(l...]
    dot_general x0 -> x2, matrix products: none -> 21.9 us  [the longest x1 12.6 us: peer_grads(): lax.dot_general(normed, d_pre, (((0,), (0,)), ((), ())), preferred_elemen...]
    all_to_all x4, waiting for transfers between devices: 39.8 us -> 23.2 us  [send_ahead(): lax.all_to_all(spread, 'rep', split_axis=0, concat_axis=0, tiled=True)]
    broadcast_in_dim x2 -> x0, other arithmetic: 15.9 us -> none  [on_device(): return (new_in[None], new_out[None])]
    ppermute x50 -> x52, starting transfers between devices: 73.9 us -> 85.8 us  [swapped(): return lax.ppermute(value, axis, pairs)]
    dot_general x5 -> x6, matrix products: 17.9 us -> 22.4 us  [layer_front(): jnp.dot(normed, weight_in, preferred_element_type=jnp.float32) * scale_in]
  transfers between devices with their start and end apart: 66 -> 68, of which waited for: 47 -> 42; matrix products, arithmetic and copies ran while one was open for 21% -> 35% of each run, Pallas kernels for 0% -> 0%
where the time goes in v1:
time: 757 us; the launch traced here: 746 us
  waiting for transfers between devices  308 us (41%)
  matrix products  190 us (25%)
  starting transfers between devices  149 us (20%)
  other arithmetic  50.3 us (7%)
  local copies, waits for them, and re-layouts  45.6 us (6%)
    ppermute x8, waiting for transfers between devices, passed_along(): lax.ppermute(value, axis, [(source, source + steps) for source in range(l...  159 us
    ppermute x52, waiting for transfers between devices, swapped(): return lax.ppermute(value, axis, pairs)  99.6 us
    ppermute x52, starting transfers between devices, swapped(): return lax.ppermute(value, axis, pairs)  85.8 us
    dot_general x5, matrix products, layer_backward(): lax.dot_general(normed, d_pre, (((0,), (0,)), ((), ())), preferred_elemen...  42.8 us
    dot_general x5, matrix products, layer_backward(): lax.dot_general(activated, up_full, (((0,), (0,)), ((), ())), preferred_e...  39.8 us
    all_to_all x4, starting transfers between devices, send_ahead(): lax.all_to_all(spread, 'rep', split_axis=0, concat_axis=0, tiled=True)  26.5 us
    all_to_all x4, waiting for transfers between devices, send_back(): lax.all_to_all(spread, 'rep', split_axis=0, concat_axis=0, tiled=True)  26.3 us
    dot_general x4, matrix products, layer_rest(): jnp.dot(activated, weight_out, preferred_element_type=jnp.float32)  23.4 us
  transfers between devices with their start and end apart: 68, of which 42 were waited for; matrix products, arithmetic and copies ran while one was open for 35% of the time, Pallas kernels for 0%

profile of v1, /device:TPU:16, one launch (start us, length us, event | category | flops | bytes accessed | tf_op | source)
XLA Modules:
  0.0 746.3 jit_solution(782777950132981587)
XLA Ops:
  38.2 5.9 convolution_multiply_fusion.7
  74.3 144.1 %collective-permute-done.12 = bf16[2,4,1,3072]{3,1,0,2:T(4,128)(2,1)S(1)} collective-permute-done((bf16[2,4,1,3072]{3,1,0,2:T(4,128)(2,1)S(1)}, bf16[2,4,1,3072]{3,1,0,2:T(4,128)(2,1)S(1)}, u32[]{:S(2)}, u32[]{:S(2)}) %collective-permute-start.12) | collective-permute-done | bytes 49184 | tf_op jit(solution)/shard_map/ppermute | solution.py:20
  219.4 8.1 %all-to-all-start = ((bf16[32,4,1,3072]{3,1,2,0:T(4,128)(2,1)}), bf16[32,4,1,3072]{3,1,2,0:T(4,128)(2,1)S(1)}, u32[]{:S(2)}, u32[]{:S(2)}) async-start(bf16[32,4,1,3072]{3,1,2,0:T(4,128)(2,1)} %bitcast.32), calls=%async_computation | async-start | bytes 1572864 | tf_op jit(solution)/shard_map/all_to_all | solution.py:183
  231.7 9.4 %all-to-all-done = bf16[32,4,1,3072]{3,1,2,0:T(4,128)(2,1)S(1)} async-done(((bf16[32,4,1,3072]{3,1,2,0:T(4,128)(2,1)}), bf16[32,4,1,3072]{3,1,2,0:T(4,128)(2,1)S(1)}, u32[]{:S(2)}, u32[]{:S(2)}) %all-to-all-start) | async-done | bytes 786464 | tf_op jit(solution)/shard_map/all_to_all | solution.py:183
  243.3 5.9 convolution_multiply_fusion.6
  250.9 5.7 collective-permute-done.13
  280.7 6.3 all-to-all-start.1
  300.8 5.9 convolution_multiply_fusion.5
  332.3 6.1 collective-permute-done.22
  339.6 6.0 all-to-all-start.2
  358.5 5.9 convolution_multiply_fusion.4
  397.2 6.1 all-to-all-start.3
  406.4 8.4 %all-to-all-done.3 = bf16[32,4,1,3072]{3,1,2,0:T(4,128)(2,1)S(1)} async-done(((bf16[32,4,1,3072]{3,1,2,0:T(4,128)(2,1)}), bf16[32,4,1,3072]{3,1,2,0:T(4,128)(2,1)S(1)}, u32[]{:S(2)}, u32[]{:S(2)}) %all-to-all-start.3) | async-done | bytes 786464 | tf_op jit(solution)/shard_map/all_to_all | solution.py:183
  469.5 5.5 all-to-all-done.4
  490.1 5.6 collective-permute-done.41
  554.7 5.7 collective-permute-done.46
  583.0 6.1 fusion.181
  603.3 6.8 all-to-all-done.6
  659.2 6.0 all-to-all-start.7
  670.5 9.3 %all-to-all-done.7 = bf16[32,4,1,3072]{3,1,2,0:T(4,128)(2,1)} async-done(((bf16[32,4,1,3072]{3,1,2,0:T(4,128)(2,1)}), bf16[32,4,1,3072]{3,1,2,0:T(4,128)(2,1)}, u32[]{:S(2)}, u32[]{:S(2)}) %all-to-all-start.7) | async-done | bytes 786464 | tf_op jit(solution)/shard_map/all_to_all | solution.py:192
  683.3 22.3 %subtract_convert_fusion.3 = bf16[3072,768]{1,0:T(8,128)(2,1)} fusion(f32[3072,768]{1,0:T(8,128)} %fusion.69, f32[3072,768]{1,0:T(8,128)} %fusion.67, f32[3072,768]{1,0:T(8,128)} %fusion.65, f32[3072,768]{1,0:T(8,128)} %fusion.63, pred[]{:T(512)S(6)} %and.55, pred[]{:T(512)S(6)} %and.54, pred[]{:T(512)S(6)} %and.53, pred[]{:T(512)S(6)} %and.52, ...), kind=kOutput, calls=%fused_computation.5 | convolution fusion | flops 648069120 | bytes 52888072 | tf_op jit(solution)/shard_map/dot_general | solution.py:135
  705.6 18.5 %subtract_convert_fusion.1 = bf16[768,3072]{1,0:T(8,128)(2,1)} fusion(f32[768,3072]{1,0:T(8,128)} %fusion.183, f32[768,3072]{1,0:T(8,128)} %fusion.182, f32[768,3072]{1,0:T(8,128)} %fusion.181, f32[768,3072]{1,0:T(8,128)} %fusion.180, bf16[64,3072]{1,0:T(8,128)(2,1)S(1)} %reshape.4132, pred[]{:T(512)S(6)} %and.55, pred[]{:T(512)S(6)} %and.54, pred[]{:T(512)S(6)} %and.53, ...), kind=kOutput, calls=%fused_computation.2 | convolution fusion | flops 344948736 | bytes 47775748 | tf_op jit(solution)/shard_map/dot_general | solution.py:122
  724.2 12.6 %fusion = bf16[1,3072,768]{2,1,0:T(8,128)(2,1)} fusion(bf16[3072,768]{1,0:T(8,128)(2,1)} %subtract_convert_fusion.3, pred[]{:T(512)S(6)} %ne.17, bf16[128,3072]{1,0:T(8,128)(2,1)S(1)} %copy-done.1, bf16[3072,768]{1,0:T(8,128)(2,1)} %collective-permute-done.56, bf16[128,3072]{1,0:T(8,128)(2,1)} %bitcast.166, bf16[768,3072]{1,0:T(8,128)(2,1)} %collective-permute-done.59, ...), kind=kOutput, calls=%fused_computation.6 | convolution fusion | flops 1233616896 | bytes 20840448 | tf_op jit(solution)/shard_map/dot_general | solution.py:173
  736.8 9.3 %fusion.1 = bf16[1,768,3072]{2,1,0:T(8,128)(2,1)} fusion(bf16[768,3072]{1,0:T(8,128)(2,1)} %subtract_convert_fusion.1, pred[]{:T(512)S(6)} %ne.17, bf16[128,3072]{1,0:T(8,128)(2,1)} %bitcast.166, bf16[768,3072]{1,0:T(8,128)(2,1)} %collective-permute-done.59, f32[128,768]{1,0:T(8,128)S(1)} %copy-done.24), kind=kOutput, calls=%fused_computation.7 | convolution fusion | flops 628555776 | bytes 15335425 | tf_op jit(solution)/shard_map/dot_general | solution.py:164
  (499 shorter events, 411.6 us)
Async XLA Ops:
  1.4 16.5 %collective-permute-start = (bf16[1,4,1,3072]{3,1,0,2:T(4,128)(2,1)S(1)}, bf16[1,4,1,3072]{3,1,0,2:T(4,128)(2,1)S(1)}, u32[]{:S(2)}, u32[]{:S(2)}) collective-permute-start(bf16[1,4,1,3072]{3,1,0,2:T(4,128)(2,1)S(1)} %get-tuple-element.34), channel_id=1, source_target_pairs={{0,1},{1,0},{2,3},{3,2},{4,5},{5,4},{6,7},{7,6},{8,9},{9,8},{10,11... | collective-permute-start | bytes 73736 | tf_op jit(solution)/shard_map/ppermute | solution.py:14
  3.4 15.5 %collective-permute-start.4 = (bf16[1,4,1,3072]{3,1,0,2:T(4,128)(2,1)S(1)}, bf16[1,4,1,3072]{3,1,0,2:T(4,128)(2,1)S(1)}, u32[]{:S(2)}, u32[]{:S(2)}) collective-permute-start(bf16[1,4,1,3072]{3,1,0,2:T(4,128)(2,1)S(1)} %get-tuple-element.31), channel_id=1, source_target_pairs={{0,1},{1,0},{2,3},{3,2},{4,5},{5,4},{6,7},{7,6},{8,9},{9,8},{10,11... | collective-permute-start | bytes 73736 | tf_op jit(solution)/shard_map/ppermute | solution.py:14
  10.2 56.5 %collective-permute-start.32 = (bf16[1,4,1,3072]{3,1,0,2:T(4,128)(2,1)S(1)}, bf16[1,4,1,3072]{3,1,0,2:T(4,128)(2,1)S(1)}, u32[]{:S(2)}, u32[]{:S(2)}) collective-permute-start(bf16[1,4,1,3072]{3,1,0,2:T(4,128)(2,1)S(1)} %bitcast.659), channel_id=1, source_target_pairs={{0,1},{1,0},{2,3},{3,2},{4,5},{5,4},{6,7},{7,6},{8,9},{9,8},{10,11... | collective-permute-start | bytes 73736 | tf_op jit(solution)/shard_map/ppermute | solution.py:14
  12.2 251.3 %collective-permute-start.28 = (bf16[1,4,1,3072]{3,1,0,2:T(4,128)(2,1)S(1)}, bf16[1,4,1,3072]{3,1,0,2:T(4,128)(2,1)S(1)}, u32[]{:S(2)}, u32[]{:S(2)}) collective-permute-start(bf16[1,4,1,3072]{3,1,0,2:T(4,128)(2,1)S(1)} %get-tuple-element.24), channel_id=1, source_target_pairs={{0,1},{1,0},{2,3},{3,2},{4,5},{5,4},{6,7},{7,6},{8,9},{9,8},{10,11... | collective-permute-start | bytes 73736 | tf_op jit(solution)/shard_map/ppermute | solution.py:14
  12.3 561.1 %collective-permute-start.56 = (bf16[3072,768]{1,0:T(8,128)(2,1)}, bf16[3072,768]{1,0:T(8,128)(2,1)}, u32[]{:S(2)}, u32[]{:S(2)}) collective-permute-start(bf16[3072,768]{1,0:T(8,128)(2,1)} %bitcast.609), channel_id=1, source_target_pairs={{0,16},{1,17},{2,18},{3,19},{4,20},{5,21},{6,22},{7,23},{8,24},{9,... | collective-permute-start | bytes 14155784 | tf_op jit(solution)/shard_map/ppermute | solution.py:14
  17.9 706.2 %collective-permute-start.59 = (bf16[768,3072]{1,0:T(8,128)(2,1)}, bf16[768,3072]{1,0:T(8,128)(2,1)}, u32[]{:S(2)}, u32[]{:S(2)}) collective-permute-start(bf16[768,3072]{1,0:T(8,128)(2,1)} %bitcast.612), channel_id=1, source_target_pairs={{0,16},{1,17},{2,18},{3,19},{4,20},{5,21},{6,22},{7,23},{8,24},{9,... | collective-permute-start | bytes 14155784 | tf_op jit(solution)/shard_map/ppermute | solution.py:14
  70.9 147.5 %collective-permute-start.12 = (bf16[2,4,1,3072]{3,1,0,2:T(4,128)(2,1)S(1)}, bf16[2,4,1,3072]{3,1,0,2:T(4,128)(2,1)S(1)}, u32[]{:S(2)}, u32[]{:S(2)}) collective-permute-start(bf16[2,4,1,3072]{3,1,0,2:T(4,128)(2,1)S(1)} %reshape.4107), channel_id=1, source_target_pairs={{0,32},{32,64},{64,96},{1,33},{33,65},{65,97},{2,34},{34,66},{66,9... | collective-permute-start | bytes 147464 | tf_op jit(solution)/shard_map/ppermute | solution.py:20
  72.9 154.8 %collective-permute-start.6 = (bf16[4,4,1,3072]{3,1,0,2:T(4,128)(2,1)S(1)}, bf16[4,4,1,3072]{3,1,0,2:T(4,128)(2,1)S(1)}, u32[]{:S(2)}, u32[]{:S(2)}) collective-permute-start(bf16[4,4,1,3072]{3,1,0,2:T(4,128)(2,1)S(1)} %maximum_select_fusion.11), channel_id=1, source_target_pairs={{0,4},{1,5},{2,6},{3,7},{4,0},{5,1},{6,2},{7,3},{8,12},{9,13},{10,... | collective-permute-start | bytes 294920 | tf_op jit(solution)/shard_map/ppermute | solution.py:14
  219.4 21.7 %all-to-all-start = ((bf16[32,4,1,3072]{3,1,2,0:T(4,128)(2,1)}), bf16[32,4,1,3072]{3,1,2,0:T(4,128)(2,1)S(1)}, u32[]{:S(2)}, u32[]{:S(2)}) async-start(bf16[32,4,1,3072]{3,1,2,0:T(4,128)(2,1)} %bitcast.32), calls=%async_computation | async-start | bytes 1572864 | tf_op jit(solution)/shard_map/all_to_all | solution.py:183
  227.9 14.0 %collective-permute-start.7 = (bf16[8,4,1,3072]{3,1,0,2:T(4,128)(2,1)S(1)}, bf16[8,4,1,3072]{3,1,0,2:T(4,128)(2,1)S(1)}, u32[]{:S(2)}, u32[]{:S(2)}) collective-permute-start(bf16[8,4,1,3072]{3,1,0,2:T(4,128)(2,1)S(1)} %maximum_select_fusion.2), channel_id=1, source_target_pairs={{0,8},{1,9},{2,10},{3,11},{4,12},{5,13},{6,14},{7,15},{8,0},{9,1},... | collective-permute-start | bytes 589832 | tf_op jit(solution)/shard_map/ppermute | solution.py:14
  273.4 17.1 %collective-permute-start.33 = (bf16[2,4,1,3072]{3,1,0,2:T(4,128)(2,1)S(1)}, bf16[2,4,1,3072]{3,1,0,2:T(4,128)(2,1)S(1)}, u32[]{:S(2)}, u32[]{:S(2)}) collective-permute-start(bf16[2,4,1,3072]{3,1,0,2:T(4,128)(2,1)S(1)} %fusion.242), channel_id=1, source_target_pairs={{0,2},{1,3},{2,0},{3,1},{4,6},{5,7},{6,4},{7,5},{8,10},{9,11},{10,... | collective-permute-start | bytes 147464 | tf_op jit(solution)/shard_map/ppermute | solution.py:14
  280.7 18.6 %all-to-all-start.1 = ((bf16[32,4,1,3072]{3,1,2,0:T(4,128)(2,1)}), bf16[32,4,1,3072]{3,1,2,0:T(4,128)(2,1)S(1)}, u32[]{:S(2)}, u32[]{:S(2)}) async-start(bf16[32,4,1,3072]{3,1,2,0:T(4,128)(2,1)} %bitcast.42), calls=%async_computation.1 | async-start | bytes 1572864 | tf_op jit(solution)/shard_map/all_to_all | solution.py:183
  291.2 34.2 %collective-permute-start.34 = (bf16[4,4,1,3072]{3,1,0,2:T(4,128)(2,1)}, bf16[4,4,1,3072]{3,1,0,2:T(4,128)(2,1)S(1)}, u32[]{:S(2)}, u32[]{:S(2)}) collective-permute-start(bf16[4,4,1,3072]{3,1,0,2:T(4,128)(2,1)} %maximum_select_fusion.15), channel_id=1, source_target_pairs={{0,4},{1,5},{2,6},{3,7},{4,0},{5,1},{6,2},{7,3},{8,12},{9,13},{10,... | collective-permute-start | bytes 294920 | tf_op jit(solution)/shard_map/ppermute | solution.py:14
  294.6 51.0 %collective-permute-start.30 = (bf16[4,4,1,3072]{3,1,0,2:T(4,128)(2,1)}, bf16[4,4,1,3072]{3,1,0,2:T(4,128)(2,1)}, u32[]{:S(2)}, u32[]{:S(2)}) collective-permute-start(bf16[4,4,1,3072]{3,1,0,2:T(4,128)(2,1)} %maximum_select_fusion.13), channel_id=1, source_target_pairs={{0,4},{1,5},{2,6},{3,7},{4,0},{5,1},{6,2},{7,3},{8,12},{9,13},{10,... | collective-permute-start | bytes 294920 | tf_op jit(solution)/shard_map/ppermute | solution.py:14
  326.4 143.2 %collective-permute-start.35 = (bf16[8,4,1,3072]{3,1,0,2:T(4,128)(2,1)}, bf16[8,4,1,3072]{3,1,0,2:T(4,128)(2,1)}, u32[]{:S(2)}, u32[]{:S(2)}) collective-permute-start(bf16[8,4,1,3072]{3,1,0,2:T(4,128)(2,1)} %maximum_select_fusion.7), channel_id=1, source_target_pairs={{0,8},{1,9},{2,10},{3,11},{4,12},{5,13},{6,14},{7,15},{8,0},{9,1},... | collective-permute-start | bytes 589832 | tf_op jit(solution)/shard_map/ppermute | solution.py:14
  339.6 17.5 %all-to-all-start.2 = ((bf16[32,4,1,3072]{3,1,2,0:T(4,128)(2,1)}), bf16[32,4,1,3072]{3,1,2,0:T(4,128)(2,1)S(1)}, u32[]{:S(2)}, u32[]{:S(2)}) async-start(bf16[32,4,1,3072]{3,1,2,0:T(4,128)(2,1)} %bitcast.48), calls=%async_computation.2 | async-start | bytes 1572864 | tf_op jit(solution)/shard_map/all_to_all | solution.py:183
  347.4 30.7 %collective-permute-start.31 = (bf16[8,4,1,3072]{3,1,0,2:T(4,128)(2,1)}, bf16[8,4,1,3072]{3,1,0,2:T(4,128)(2,1)}, u32[]{:S(2)}, u32[]{:S(2)}) collective-permute-start(bf16[8,4,1,3072]{3,1,0,2:T(4,128)(2,1)} %maximum_select_fusion.5), channel_id=1, source_target_pairs={{0,8},{1,9},{2,10},{3,11},{4,12},{5,13},{6,14},{7,15},{8,0},{9,1},... | collective-permute-start | bytes 589832 | tf_op jit(solution)/shard_map/ppermute | solution.py:14
  397.2 17.6 %all-to-all-start.3 = ((bf16[32,4,1,3072]{3,1,2,0:T(4,128)(2,1)}), bf16[32,4,1,3072]{3,1,2,0:T(4,128)(2,1)S(1)}, u32[]{:S(2)}, u32[]{:S(2)}) async-start(bf16[32,4,1,3072]{3,1,2,0:T(4,128)(2,1)} %bitcast.620), calls=%async_computation.3 | async-start | bytes 1572864 | tf_op jit(solution)/shard_map/all_to_all | solution.py:183
  429.1 104.8 %collective-permute-start.57 = (bf16[2,64,3072]{2,1,0:T(8,128)(2,1)S(1)}, bf16[2,64,3072]{2,1,0:T(8,128)(2,1)}, u32[]{:S(2)}, u32[]{:S(2)}) collective-permute-start(bf16[2,64,3072]{2,1,0:T(8,128)(2,1)S(1)} %select_dynamic-update-slice_fusion.4), channel_id=1, source_target_pairs={{0,16},{1,17},{2,18},{3,19},{4,20},{5,21},{6,22},{7,23},{8,24},{9,... | collective-permute-start | bytes 2359304 | tf_op jit(solution)/shard_map/ppermute | solution.py:14
  456.2 18.9 %all-to-all-start.4 = ((bf16[32,4,1,3072]{3,1,2,0:T(4,128)(2,1)}), bf16[32,4,1,3072]{3,1,2,0:T(4,128)(2,1)S(1)}, u32[]{:S(2)}, u32[]{:S(2)}) async-start(bf16[32,4,1,3072]{3,1,2,0:T(4,128)(2,1)} %broadcast_in_dim.228), calls=%async_computation.4 | async-start | bytes 1572864 | tf_op jit(solution)/shard_map/all_to_all | solution.py:192
  519.9 20.1 %all-to-all-start.5 = ((bf16[32,4,1,3072]{3,1,2,0:T(4,128)(2,1)}), bf16[32,4,1,3072]{3,1,2,0:T(4,128)(2,1)}, u32[]{:S(2)}, u32[]{:S(2)}) async-start(bf16[32,4,1,3072]{3,1,2,0:T(4,128)(2,1)} %broadcast_in_dim.231), calls=%async_computation.5 | async-start | bytes 1572864 | tf_op jit(solution)/shard_map/all_to_all | solution.py:192
  590.1 20.0 %all-to-all-start.6 = ((bf16[32,4,1,3072]{3,1,2,0:T(4,128)(2,1)}), bf16[32,4,1,3072]{3,1,2,0:T(4,128)(2,1)}, u32[]{:S(2)}, u32[]{:S(2)}) async-start(bf16[32,4,1,3072]{3,1,2,0:T(4,128)(2,1)} %broadcast_in_dim.233), calls=%async_computation.6 | async-start | bytes 1572864 | tf_op jit(solution)/shard_map/all_to_all | solution.py:192
  659.2 20.6 %all-to-all-start.7 = ((bf16[32,4,1,3072]{3,1,2,0:T(4,128)(2,1)}), bf16[32,4,1,3072]{3,1,2,0:T(4,128)(2,1)}, u32[]{:S(2)}, u32[]{:S(2)}) async-start(bf16[32,4,1,3072]{3,1,2,0:T(4,128)(2,1)} %broadcast_in_dim.235), calls=%async_computation.7 | async-start | bytes 1572864 | tf_op jit(solution)/shard_map/all_to_all | solution.py:192
  681.9 42.3 %collective-permute-start.58 = (bf16[2,64,3072]{2,1,0:T(8,128)(2,1)S(1)}, bf16[2,64,3072]{2,1,0:T(8,128)(2,1)}, u32[]{:S(2)}, u32[]{:S(2)}) collective-permute-start(bf16[2,64,3072]{2,1,0:T(8,128)(2,1)S(1)} %select_dynamic-update-slice_fusion), channel_id=1, source_target_pairs={{0,16},{1,17},{2,18},{3,19},{4,20},{5,21},{6,22},{7,23},{8,24},{9,... | collective-permute-start | bytes 2359304 | tf_op jit(solution)/shard_map/ppermute | solution.py:14
  (81 other events, 692.5 us)

commit v2 on v1

v2 whole, which is shorter than its diff:
```python
import numpy as np
import jax
import jax.numpy as jnp
from jax import lax
from jax.sharding import Mesh, PartitionSpec as P

EPSILON = 1e-06
GELU_SCALE = 0.7978845608028654
LEARNING = 8.0
PAIR = ("section", "half")


def gelu_parts(preact):
    inner = GELU_SCALE * (preact + 0.044715 * preact * preact * preact)
    tanh_val = jnp.tanh(inner)
    gelu_val = 0.5 * preact * (1.0 + tanh_val)
    slopes = 0.5 * (1.0 + tanh_val) + 0.5 * preact * (1.0 - tanh_val * tanh_val) * GELU_SCALE * (
        1.0 + 3.0 * 0.044715 * preact * preact
    )
    return (gelu_val, slopes)


def route_tables(routes, blocks):
    micro_count, bound_count, replicas, capacity = routes.shape
    slot_ids = jnp.arange(capacity, dtype=jnp.int32)
    replica_ids = jnp.arange(replicas, dtype=jnp.int32)
    live_now = jnp.broadcast_to(slot_ids[None, None, :] < blocks, (micro_count, replicas, capacity))
    link_list = []
    live_list = [live_now]
    for bound_idx in range(bound_count):
        target = jnp.where(live_now, routes[:, bound_idx], -1).reshape(
            micro_count, replicas * capacity
        )
        matches = (target[:, :, None] == replica_ids[None, None, :]).astype(jnp.int32)
        before = jnp.cumsum(matches, axis=1) - matches
        position = jnp.sum(matches * before, axis=2)
        link_table = matches[:, :, :, None] * (
            position[:, :, None, None] == slot_ids[None, None, None, :]
        ).astype(jnp.int32)
        link_table = link_table.reshape(micro_count, replicas, capacity, replicas, capacity)
        link_list.append(link_table.astype(jnp.float32))
        live_now = jnp.sum(link_table, axis=(1, 2)) > 0
        live_list.append(live_now)
    return (link_list, live_list)


def layer_front(flat_rows, weight_in, scale_in):
    widened = flat_rows.astype(jnp.float32)
    inverse = lax.rsqrt(jnp.mean(widened * widened, axis=-1, keepdims=True) + EPSILON)
    normed = (widened * inverse).astype(jnp.bfloat16)
    preact = jnp.dot(normed, weight_in, preferred_element_type=jnp.float32) * scale_in
    return (widened, inverse, normed, preact)


def gather_rows(piece):
    return lax.all_gather(piece, "plane", axis=0, tiled=True)


def own_rows(full, shard_idx):
    return lax.dynamic_slice_in_dim(full, shard_idx, 1, axis=0)


def forward_piece(x_full, weight_in, weight_out, scale_in, scale_out, shard_idx):
    shape = x_full.shape
    widened, inverse, normed, preact = layer_front(x_full.reshape(-1, shape[-1]), weight_in, scale_in)
    gelu_val, slopes = gelu_parts(preact)
    activated = gelu_val.astype(jnp.bfloat16)
    partial_value = jnp.dot(activated, weight_out, preferred_element_type=jnp.float32) * scale_out
    summed = lax.psum_scatter(partial_value.reshape(shape), "plane", scatter_dimension=0, tiled=True)
    return (own_rows(x_full, shard_idx).astype(jnp.float32) + summed).astype(jnp.bfloat16)


def backward_piece(x_full, up_full, up_piece, weight_in, weight_out, scale_in, scale_out, shard_idx):
    shape = x_full.shape
    widened, inverse, normed, preact = layer_front(x_full.reshape(-1, shape[-1]), weight_in, scale_in)
    gelu_val, slopes = gelu_parts(preact)
    d_act = (
        lax.dot_general(
            up_full.reshape(-1, shape[-1]), weight_out, (((1,), (1,)), ((), ())),
            preferred_element_type=jnp.float32,
        )
        * scale_out
    )
    d_pre = (d_act * slopes).astype(jnp.bfloat16)
    d_normed = (
        lax.dot_general(d_pre, weight_in, (((1,), (1,)), ((), ())), preferred_element_type=jnp.float32)
        * scale_in
    )
    normed_piece = lax.psum_scatter(d_normed.reshape(shape), "plane", scatter_dimension=0, tiled=True)
    wide_piece = own_rows(x_full, shard_idx).astype(jnp.float32)
    inv_piece = own_rows(inverse.reshape(shape[:-1] + (1,)), shard_idx)
    grad_piece = (
        up_piece.astype(jnp.float32)
        + inv_piece * normed_piece
        - wide_piece
        * inv_piece
        * inv_piece
        * inv_piece
        * jnp.mean(normed_piece * wide_piece, axis=-1, keepdims=True)
    )
    return grad_piece.astype(jnp.bfloat16)


def weight_grads(x_full, up_full, weight_in, weight_out, scale_in, scale_out):
    width = x_full.shape[-1]
    widened, inverse, normed, preact = layer_front(x_full.reshape(-1, width), weight_in, scale_in)
    gelu_val, slopes = gelu_parts(preact)
    activated = gelu_val.astype(jnp.bfloat16)
    ups = up_full.reshape(-1, width)
    d_out = (
        lax.dot_general(activated, ups, (((0,), (0,)), ((), ())), preferred_element_type=jnp.float32)
        * scale_out
    )
    d_act = (
        lax.dot_general(ups, weight_out, (((1,), (1,)), ((), ())), preferred_element_type=jnp.float32)
        * scale_out
    )
    d_pre = (d_act * slopes).astype(jnp.bfloat16)
    d_in = (
        lax.dot_general(normed, d_pre, (((0,), (0,)), ((), ())), preferred_element_type=jnp.float32)
        * scale_in
    )
    return (d_in, d_out)


def cross_boundary(piece, source, target, replicas):
    straight = [(source * replicas + h, target * replicas + h) for h in range(replicas)]
    crossed = [(source * replicas + h, target * replicas + (replicas - 1 - h)) for h in range(replicas)]
    return (lax.ppermute(piece, PAIR, straight), lax.ppermute(piece, PAIR, crossed))


def on_device(block_inputs, routes, cotangent, gossip_peer, w_in, w_out):
    section_count = lax.axis_size("section")
    replicas = lax.axis_size("half")
    group_size = lax.axis_size("plane")
    my_section = lax.axis_index("section")
    replica = lax.axis_index("half")
    shard_idx = lax.axis_index("plane")
    micro_count, blocks, piece_rows, model_width = block_inputs.shape
    capacity = cotangent.shape[1]
    weight_in = w_in[0]
    weight_out = w_out[0]
    hidden = weight_in.shape[1]
    scale_in = model_width ** (-0.5)
    scale_out = (hidden * group_size) ** (-0.5)
    link_list, live_list = route_tables(routes, blocks)

    opening = jnp.concatenate(
        [
            block_inputs,
            jnp.zeros((micro_count, capacity - blocks, piece_rows, model_width), jnp.bfloat16),
        ],
        axis=1,
    ).transpose(2, 0, 1, 3)
    x_cur = gather_rows(opening)
    x_keep = x_cur
    for bound in range(section_count - 1):
        piece = forward_piece(x_cur, weight_in, weight_out, scale_in, scale_out, shard_idx)
        straight, crossed = cross_boundary(piece, bound, bound + 1, replicas)
        sources = jnp.stack(
            [jnp.where(replica == h, straight, crossed) for h in range(replicas)]
        )[:, 0]
        mine = lax.dynamic_index_in_dim(link_list[bound], replica, 3, keepdims=False)
        routed = jnp.einsum(
            "mqjk,qmjd->mkd", mine.astype(jnp.bfloat16), sources,
            preferred_element_type=jnp.float32,
        ).astype(jnp.bfloat16)[None]
        x_cur = gather_rows(routed)
        x_keep = jnp.where(my_section == bound + 1, x_cur, x_keep)

    last_live = lax.dynamic_index_in_dim(live_list[section_count - 1], replica, 1, keepdims=False)
    up_piece = jnp.where(
        last_live[None, :, :, None], cotangent.transpose(2, 0, 1, 3), jnp.zeros((), jnp.bfloat16)
    )
    up_full = gather_rows(up_piece)
    up_keep = up_full
    for depth in reversed(range(1, section_count)):
        grad_piece = backward_piece(
            x_keep, up_full, up_piece, weight_in, weight_out, scale_in, scale_out, shard_idx
        )
        straight, crossed = cross_boundary(grad_piece, depth, depth - 1, replicas)
        sources = jnp.stack(
            [jnp.where(replica == h, straight, crossed) for h in range(replicas)]
        )[:, 0]
        mine = lax.dynamic_index_in_dim(link_list[depth - 1], replica, 1, keepdims=False)
        up_piece = jnp.einsum(
            "mjdk,dmkD->mjD", mine.astype(jnp.bfloat16), sources,
            preferred_element_type=jnp.float32,
        ).astype(jnp.bfloat16)[None]
        up_full = gather_rows(up_piece)
        up_keep = jnp.where(my_section == depth - 1, up_full, up_keep)

    accum_in, accum_out = weight_grads(x_keep, up_keep, weight_in, weight_out, scale_in, scale_out)
    stepped_in = (weight_in.astype(jnp.float32) - LEARNING * accum_in).astype(jnp.bfloat16)
    stepped_out = (weight_out.astype(jnp.float32) - LEARNING * accum_out).astype(jnp.bfloat16)
    partner = gossip_peer[my_section, replica]
    paired = partner != replica
    swap = [(h, replicas - 1 - h) for h in range(replicas)]
    other_in = lax.ppermute(stepped_in, "half", swap)
    other_out = lax.ppermute(stepped_out, "half", swap)
    chosen_in = jnp.where(paired, other_in, stepped_in)
    chosen_out = jnp.where(paired, other_out, stepped_out)
    new_in = (0.5 * (stepped_in.astype(jnp.float32) + chosen_in.astype(jnp.float32))).astype(
        jnp.bfloat16
    )
    new_out = (0.5 * (stepped_out.astype(jnp.float32) + chosen_out.astype(jnp.float32))).astype(
        jnp.bfloat16
    )
    return (new_in[None], new_out[None])


def solution(mesh):
    sections = mesh.shape["section"]
    reps = mesh.shape["rep"]
    inner = Mesh(np.asarray(mesh.devices).reshape(sections, 2, reps // 2), ("section", "half", "plane"))
    rows = ("half", "plane")
    return jax.shard_map(
        on_device,
        mesh=inner,
        in_specs=(
            P(None, None, rows, None),
            P(),
            P(None, None, rows, None),
            P(),
            P("section", None, rows),
            P("section", rows, None),
        ),
        out_specs=(P("section", None, rows), P("section", rows, None)),
        check_vma=False,
    )
```

time: 757 us -> 1050 us (1.39)
  waiting for transfers between devices: 308 us -> 683 us
  blocking collectives: 0 us -> 192 us
  starting transfers between devices: 149 us -> 16.7 us
  matrix products: 190 us -> 64.8 us
  local copies, waits for them, and re-layouts: 45.6 us -> 25.3 us
  other arithmetic: 50.3 us -> 37.1 us
  between operations: 3.22 us -> 15.7 us
    unnamed x0 -> x12, waiting for transfers between devices: none -> 498 us
    all_gather x0 -> x8, blocking collectives: none -> 192 us  [gather_rows(): return lax.all_gather(piece, 'plane', axis=0, tiled=True)]
    dot_general x33 -> x14, matrix products: 167 us -> 61.6 us  [the longest x3 24.8 us: backward_piece(): lax.dot_general(d_pre, weight_in, (((1,), (1,)), ((), ())), preferred_ele...]
    ppermute x60 -> x14, starting transfers between devices: 101 us -> 16.4 us  [the longest x6 7.1 us: cross_boundary(): lax.ppermute(piece, PAIR, straight)]
    ppermute x60 -> x14, waiting for transfers between devices: 259 us -> 185 us  [the longest x1 91.4 us: on_device(): other_out = lax.ppermute(stepped_out, 'half', swap)]
    all_to_all x8 -> x0, waiting for transfers between devices: 49.5 us -> none  [the longest x4 26.3 us: send_back(): lax.all_to_all(spread, 'rep', split_axis=0, concat_axis=0, tiled=True)]
    all_to_all x8 -> x0, starting transfers between devices: 47.8 us -> none  [the longest x4 26.5 us: send_ahead(): lax.all_to_all(spread, 'rep', split_axis=0, concat_axis=0, tiled=True)]
    dot_general x6 -> x1, matrix products: 22.4 us -> 3.12 us  [layer_front(): jnp.dot(normed, weight_in, preferred_element_type=jnp.float32) * scale_in]
  transfers between devices with their start and end apart: 68 -> 20, of which waited for: 42 -> 13; matrix products, arithmetic and copies ran while one was open for 35% -> 2% of each run, Pallas kernels for 0% -> 0%
where the time goes in v2:
time: 1050 us; the launch traced here: 1030 us
  waiting for transfers between devices  683 us (65%)
  blocking collectives  192 us (18%)
  matrix products  64.8 us (6%)
  other arithmetic  37.1 us (4%)
  local copies, waits for them, and re-layouts  25.3 us (2%)
  starting transfers between devices  16.7 us (2%)
  between operations  15.7 us (1%)
    unnamed x12, waiting for transfers between devices  498 us
    all_gather x8, blocking collectives, gather_rows(): return lax.all_gather(piece, 'plane', axis=0, tiled=True)  192 us
    ppermute x1, waiting for transfers between devices, on_device(): other_out = lax.ppermute(stepped_out, 'half', swap)  91.4 us
    ppermute x1, waiting for transfers between devices, on_device(): other_in = lax.ppermute(stepped_in, 'half', swap)  83.4 us
    dot_general x3, matrix products, backward_piece(): lax.dot_general(d_pre, weight_in, (((1,), (1,)), ((), ())), preferred_ele...  24.8 us
  transfers between devices with their start and end apart: 20, of which 13 were waited for; matrix products, arithmetic and copies ran while one was open for 2% of the time, Pallas kernels for 0%

profile of v2, /device:TPU:16, one launch (start us, length us, event | category | flops | bytes accessed | tf_op | source)
XLA Modules:
  0.0 1034.5 jit_solution(6647910657615466202)
XLA Ops:
  8.0 25.7 %all-gather = bf16[32,4,1,3072]{3,1,2,0:T(4,128)(2,1)S(1)} all-gather(bf16[2,4,1,3072]{3,1,2,0:T(4,128)(2,1)S(1)} %concatenate.3), channel_id=2, replica_groups=mesh['section'=4,'half'=2,'plane'=16] {'plane'}, dimensions={0}, use_global_device_ids=true | all-gather | bytes 835584 | tf_op jit(solution)/shard_map/all_gather | solution.py:56
  44.0 86.4 %all-reduce.14.cloned.1.call-done = f32[16,2,4,3072]{3,2,1,0:T(4,128)} async-done(((f32[16,2,4,3072]{3,2,1,0:T(4,128)}), f32[16,2,4,3072]{3,2,1,0:T(4,128)}) %all-reduce.14.cloned.1.call-update) | async-done | bytes 1572880
  133.5 23.8 %all-gather.1 = bf16[32,4,3072]{2,1,0:T(4,128)(2,1)S(1)} all-gather(bf16[2,4,3072]{2,1,0:T(4,128)(2,1)S(1)} %fusion.48), channel_id=3, replica_groups=mesh['section'=4,'half'=2,'plane'=16] {'plane'}, dimensions={0}, use_global_device_ids=true | all-gather | bytes 835584 | tf_op jit(solution)/shard_map/all_gather | solution.py:56
  158.4 6.8 fusion.42
  169.3 86.4 %all-reduce.16.cloned.1.call-done = f32[16,2,4,3072]{3,2,1,0:T(4,128)} async-done(((f32[16,2,4,3072]{3,2,1,0:T(4,128)}), f32[16,2,4,3072]{3,2,1,0:T(4,128)}) %all-reduce.16.cloned.1.call-update) | async-done | bytes 1572880
  265.8 24.1 %all-gather.2 = bf16[32,4,3072]{2,1,0:T(4,128)(2,1)S(1)} all-gather(bf16[2,4,3072]{2,1,0:T(4,128)(2,1)S(1)} %fusion.49), channel_id=4, replica_groups=mesh['section'=4,'half'=2,'plane'=16] {'plane'}, dimensions={0}, use_global_device_ids=true | all-gather | bytes 835584 | tf_op jit(solution)/shard_map/all_gather | solution.py:56
  293.3 6.8 fusion.45
  303.9 23.2 %all_gather.28 = bf16[16,2,4,3072]{3,2,1,0:T(4,128)(2,1)S(1)} all-gather(bf16[1,2,4,3072]{3,2,1,0:T(4,128)(2,1)S(1)} %bitcast_select_fusion), channel_id=1, replica_groups=mesh['section'=4,'half'=2,'plane'=16] {'plane'}, dimensions={0}, use_global_device_ids=true | all-gather | bytes 835584 | tf_op jit(solution)/shard_map/all_gather | solution.py:56
  327.1 63.6 %all-reduce.18.cloned.1.call-done = f32[16,2,4,3072]{3,2,1,0:T(4,128)} async-done(((f32[16,2,4,3072]{3,2,1,0:T(4,128)}), f32[16,2,4,3072]{3,2,1,0:T(4,128)}) %all-reduce.18.cloned.1.call-update) | async-done | bytes 1572880
  396.2 23.7 %all-gather.3 = bf16[32,4,3072]{2,1,0:T(4,128)(2,1)S(1)} all-gather(bf16[2,4,3072]{2,1,0:T(4,128)(2,1)S(1)} %fusion.50), channel_id=5, replica_groups=mesh['section'=4,'half'=2,'plane'=16] {'plane'}, dimensions={0}, use_global_device_ids=true | all-gather | bytes 835584 | tf_op jit(solution)/shard_map/all_gather | solution.py:56
  424.9 7.5 fusion.30
  434.2 87.2 %all-reduce.20.cloned.1.call-done = f32[16,2,4,3072]{3,2,1,0:T(4,128)} async-done(((f32[16,2,4,3072]{3,2,1,0:T(4,128)}), f32[16,2,4,3072]{3,2,1,0:T(4,128)}) %all-reduce.20.cloned.1.call-update) | async-done | bytes 1572880
  530.3 23.8 %all-gather.4 = bf16[32,4,3072]{2,1,0:T(4,128)(2,1)S(1)} all-gather(bf16[2,4,3072]{2,1,0:T(4,128)(2,1)S(1)} %fusion.51), channel_id=6, replica_groups=mesh['section'=4,'half'=2,'plane'=16] {'plane'}, dimensions={0}, use_global_device_ids=true | all-gather | bytes 835584 | tf_op jit(solution)/shard_map/all_gather | solution.py:56
  554.3 8.6 fusion.33
  565.7 87.2 %all-reduce.22.cloned.1.call-done = f32[16,2,4,3072]{3,2,1,0:T(4,128)} async-done(((f32[16,2,4,3072]{3,2,1,0:T(4,128)}), f32[16,2,4,3072]{3,2,1,0:T(4,128)}) %all-reduce.22.cloned.1.call-update) | async-done | bytes 1572880
  661.4 23.7 %all-gather.5 = bf16[32,4,3072]{2,1,0:T(4,128)(2,1)S(1)} all-gather(bf16[2,4,3072]{2,1,0:T(4,128)(2,1)S(1)} %fusion.52), channel_id=7, replica_groups=mesh['section'=4,'half'=2,'plane'=16] {'plane'}, dimensions={0}, use_global_device_ids=true | all-gather | bytes 835584 | tf_op jit(solution)/shard_map/all_gather | solution.py:56
  685.3 8.6 fusion.36
  696.8 87.2 %all-reduce.24.cloned.1.call-done = f32[16,2,4,3072]{3,2,1,0:T(4,128)} async-done(((f32[16,2,4,3072]{3,2,1,0:T(4,128)}), f32[16,2,4,3072]{3,2,1,0:T(4,128)}) %all-reduce.24.cloned.1.call-update) | async-done | bytes 1572880
  793.4 23.8 %all-gather.6 = bf16[32,4,3072]{2,1,0:T(4,128)(2,1)S(1)} all-gather(bf16[2,4,3072]{2,1,0:T(4,128)(2,1)S(1)} %fusion.53), channel_id=8, replica_groups=mesh['section'=4,'half'=2,'plane'=16] {'plane'}, dimensions={0}, use_global_device_ids=true | all-gather | bytes 835584 | tf_op jit(solution)/shard_map/all_gather | solution.py:56
  819.8 6.0 subtract_convert_fusion
  827.8 9.5 subtract_convert_fusion.1
  839.5 91.4 %collective-permute-done.13 = bf16[768,3072]{1,0:T(8,128)(2,1)} collective-permute-done((bf16[768,3072]{1,0:T(8,128)(2,1)}, bf16[768,3072]{1,0:T(8,128)(2,1)}, u32[]{:S(2)}, u32[]{:S(2)}) %collective-permute-start.13) | collective-permute-done | bytes 4718624 | tf_op jit(solution)/shard_map/ppermute | solution.py:200
  931.0 9.1 fusion.1
  940.1 83.4 %collective-permute-done.12 = bf16[3072,768]{1,0:T(8,128)(2,1)} collective-permute-done((bf16[3072,768]{1,0:T(8,128)(2,1)}, bf16[3072,768]{1,0:T(8,128)(2,1)}, u32[]{:S(2)}, u32[]{:S(2)}) %collective-permute-start.12) | collective-permute-done | bytes 4718624 | tf_op jit(solution)/shard_map/ppermute | solution.py:199
  (189 shorter events, 90.9 us)
Async XLA Ops:
  7.2 123.2 %all-reduce.14.cloned.1.call-start = ((), (), s32[]{:S(2)}) async-start(), calls=%async_computation | async-start | bytes 3145728
  42.2 213.6 %all-reduce.16.cloned.1.call-start = ((), (), s32[]{:S(2)}) async-start(), calls=%async_computation.1 | async-start | bytes 3145728
  131.8 1.4 collective-permute-start.1
  132.5 0.7 collective-permute-start
  168.0 222.8 %all-reduce.18.cloned.1.call-start = ((), (), s32[]{:S(2)}) async-start(), calls=%async_computation.2 | async-start | bytes 3145728
  257.3 5.4 collective-permute-start.3
  258.6 6.9 collective-permute-start.2
  302.8 218.6 %all-reduce.20.cloned.1.call-start = ((), (), s32[]{:S(2)}) async-start(), calls=%async_computation.3 | async-start | bytes 3145728
  392.2 3.7 collective-permute-start.5
  393.5 2.4 collective-permute-start.4
  434.1 218.9 %all-reduce.22.cloned.1.call-start = ((), (), s32[]{:S(2)}) async-start(), calls=%async_computation.4 | async-start | bytes 3145728
  434.2 220.4 %copy-start.12 = (f32[2,4]{1,0:T(2,128)}, f32[2,4]{1,0:T(2,128)S(1)}, u32[]{:S(2)}) copy-start(f32[2,4]{1,0:T(2,128)S(1)} %fusion.199) | copy-start | bytes 100
  524.6 5.4 collective-permute-start.7
  525.9 4.1 collective-permute-start.6
  565.7 218.3 %all-reduce.24.cloned.1.call-start = ((), (), s32[]{:S(2)}) async-start(), calls=%async_computation.5 | async-start | bytes 3145728
  656.1 3.0 collective-permute-start.9
  657.4 3.0 collective-permute-start.8
  693.9 123.2 %copy-start.1 = (bf16[16,2,4,3072]{3,2,1,0:T(4,128)(2,1)S(1)}, bf16[16,2,4,3072]{3,2,1,0:T(4,128)(2,1)}, u32[]{:S(2)}) copy-start(bf16[16,2,4,3072]{3,2,1,0:T(4,128)(2,1)} %copy-done) | copy-start | bytes 2359300
  787.8 3.8 collective-permute-start.11
  789.1 2.5 collective-permute-start.10
  825.7 105.2 %collective-permute-start.13 = (bf16[768,3072]{1,0:T(8,128)(2,1)}, bf16[768,3072]{1,0:T(8,128)(2,1)}, u32[]{:S(2)}, u32[]{:S(2)}) collective-permute-start(bf16[768,3072]{1,0:T(8,128)(2,1)} %subtract_convert_fusion), channel_id=1, source_target_pairs={{0,16},{16,0},{1,17},{17,1},{2,18},{18,2},{3,19},{19,3},{4,20},{20... | collective-permute-start | bytes 14155784 | tf_op jit(solution)/shard_map/ppermute | solution.py:200
  837.4 186.1 %collective-permute-start.12 = (bf16[3072,768]{1,0:T(8,128)(2,1)}, bf16[3072,768]{1,0:T(8,128)(2,1)}, u32[]{:S(2)}, u32[]{:S(2)}) collective-permute-start(bf16[3072,768]{1,0:T(8,128)(2,1)} %subtract_convert_fusion.1), channel_id=1, source_target_pairs={{0,16},{16,0},{1,17},{17,1},{2,18},{18,2},{3,19},{19,3},{4,20},{20... | collective-permute-start | bytes 14155784 | tf_op jit(solution)/shard_map/ppermute | solution.py:199
  838.8 184.7 %slice-start = ((s8[4718592]{0:T(1024)(128)(4,1)}), s8[524288]{0:T(1024)(128)(4,1)S(1)}, s32[]{:S(2)}) async-start(s8[4718592]{0:T(1024)(128)(4,1)} %bitcast.240), calls=%async_computation.6 | async-start | bytes 1048576
  839.5 184.0 %slice-start.1 = ((s8[4718592]{0:T(1024)(128)(4,1)}), s8[4194304]{0:T(1024)(128)(4,1)S(1)}, s32[]{:S(2)}) async-start(s8[4718592]{0:T(1024)(128)(4,1)} %bitcast.240), calls=%async_computation.7 | async-start | bytes 8388608
  (15 other events, 841.8 us)
Sparse Core Ops, SparseCore 0:
  42.3 88.0 all-reduce.13
  168.1 87.6 all-reduce.15
  303.0 87.7 all-reduce.17
  434.2 87.1 all-reduce.19
  565.8 87.1 all-reduce.21
  696.9 87.0 all-reduce.23

commit v3 on v2

--- a/solution.py
+++ b/solution.py
@@ -2,6 +2,8 @@
 import jax
 import jax.numpy as jnp
 from jax import lax
+from jax.experimental import pallas as pl
+from jax.experimental.pallas import tpu as pltpu
 from jax.sharding import Mesh, PartitionSpec as P
 
 EPSILON = 1e-06
@@ -52,8 +54,60 @@
     return (widened, inverse, normed, preact)
 
 
+def plane_kernel(count, spread, x_ref, out_ref, held, send_sem, recv_sem):
+    section = lax.axis_index("section")
+    half = lax.axis_index("half")
+    me = lax.axis_index("plane")
+    barrier = pltpu.get_barrier_semaphore()
+    for step in range(1, count):
+        peer = lax.rem(me + step, count)
+        pl.semaphore_signal(
+            barrier, inc=1, device_id=(section, half, peer), device_id_type=pl.DeviceIdType.MESH
+        )
+    pl.semaphore_wait(barrier, count - 1)
+    copies = []
+    for step in range(1, count):
+        peer = lax.rem(me + step, count)
+        copy = pltpu.make_async_remote_copy(
+            src_ref=x_ref.at[0] if spread else x_ref.at[peer],
+            dst_ref=held.at[me],
+            send_sem=send_sem.at[step],
+            recv_sem=recv_sem.at[step],
+            device_id=(section, half, peer),
+            device_id_type=pl.DeviceIdType.MESH,
+        )
+        copy.start()
+        copies.append(copy)
+    own = x_ref[0] if spread else x_ref[me]
+    for copy in copies:
+        copy.wait()
+    out_ref[...] = held[...]
+    out_ref[me] = own
+
+
+def plane_call(value, count, spread, ident):
+    shape = (count,) + value.shape[1:]
+    return pl.pallas_call(
+        lambda *refs: plane_kernel(count, spread, *refs),
+        out_shape=jax.ShapeDtypeStruct(shape, value.dtype),
+        in_specs=[pl.BlockSpec(memory_space=pltpu.VMEM)],
+        out_specs=pl.BlockSpec(memory_space=pltpu.VMEM),
+        scratch_shapes=[
+            pltpu.VMEM(shape, value.dtype),
+            pltpu.SemaphoreType.DMA((count,)),
+            pltpu.SemaphoreType.DMA((count,)),
+        ],
+        compiler_params=pltpu.CompilerParams(collective_id=ident, has_side_effects=True),
+    )(value)
+
+
 def gather_rows(piece):
-    return lax.all_gather(piece, "plane", axis=0, tiled=True)
+    return plane_call(piece, lax.axis_size("plane"), True, 1)
+
+
+def sum_rows(partial_value):
+    parts = plane_call(partial_value.astype(jnp.bfloat16), lax.axis_size("plane"), False, 0)
+    return jnp.sum(parts.astype(jnp.float32), axis=0, keepdims=True)
 
 
 def own_rows(full, shard_idx):
@@ -66,7 +120,7 @@
     gelu_val, slopes = gelu_parts(preact)
     activated = gelu_val.astype(jnp.bfloat16)
     partial_value = jnp.dot(activated, weight_out, preferred_element_type=jnp.float32) * scale_out
-    summed = lax.psum_scatter(partial_value.reshape(shape), "plane", scatter_dimension=0, tiled=True)
+    summed = sum_rows(partial_value.reshape(shape))
     return (own_rows(x_full, shard_idx).astype(jnp.float32) + summed).astype(jnp.bfloat16)
 
 
@@ -86,7 +140,7 @@
         lax.dot_general(d_pre, weight_in, (((1,), (1,)), ((), ())), preferred_element_type=jnp.float32)
         * scale_in
     )
-    normed_piece = lax.psum_scatter(d_normed.reshape(shape), "plane", scatter_dimension=0, tiled=True)
+    normed_piece = sum_rows(d_normed.reshape(shape))
     wide_piece = own_rows(x_full, shard_idx).astype(jnp.float32)
     inv_piece = own_rows(inverse.reshape(shape[:-1] + (1,)), shard_idx)
     grad_piece = (

time: 1050 us -> 583 us (0.56)
  the two profiles are of different devices: /device:TPU:16 before, /device:TPU:10 now
where the time goes in v3:
time: 583 us; the launch traced here: 574 us
  Pallas kernels  236 us (40%)
  waiting for transfers between devices  188 us (32%)
  matrix products  65.8 us (11%)
  other arithmetic  45.2 us (8%)
  local copies, waits for them, and re-layouts  22.1 us (4%)
  starting transfers between devices  13.9 us (2%)
    pallas_call x14, Pallas kernels, plane_call(): pl.pallas_call(lambda *refs: plane_kernel(count, spread, *refs), out_shap...  236 us
    ppermute x1, waiting for transfers between devices, on_device(): other_out = lax.ppermute(stepped_out, 'half', swap)  91.4 us
    ppermute x1, waiting for transfers between devices, on_device(): other_in = lax.ppermute(stepped_in, 'half', swap)  88.3 us
    dot_general x3, matrix products, backward_piece(): lax.dot_general(d_pre, weight_in, (((1,), (1,)), ((), ())), preferred_ele...  23.4 us
    dot_general x3, matrix products, forward_piece(): jnp.dot(activated, weight_out, preferred_element_type=jnp.float32)  18.1 us
    broadcast_in_dim x2, other arithmetic, on_device(): return (new_in[None], new_out[None])  16.7 us
  transfers between devices with their start and end apart: 14, of which 4 were waited for; matrix products, arithmetic and copies ran while one was open for 5% of the time, Pallas kernels for 3%

profile of v3, /device:TPU:10, one launch (start us, length us, event | category | flops | bytes accessed | tf_op | source)
XLA Modules:
  0.0 574.2 jit_solution(4969790661269755226)
XLA Ops:
  2.0 19.2 %shard_map.77 = bf16[16,2,4,3072]{3,2,1,0:T(4,128)(2,1)} custom-call(bf16[1,2,4,3072]{3,2,1,0:T(4,128)(2,1)} %pad_bitcast_fusion.refs_0_), custom_call_target="tpu_custom_call" | custom-call | tf_op jit(solution)/shard_map/pallas_call | solution.py:90
  31.5 16.0 %shard_map.78 = bf16[16,2,4,3072]{3,2,1,0:T(4,128)(2,1)} custom-call(bf16[16,2,4,3072]{3,2,1,0:T(4,128)(2,1)} %convert_element_type.349.refs_0_), custom_call_target="tpu_custom_call" | custom-call | tf_op jit(solution)/shard_map/pallas_call | solution.py:90
  56.1 15.7 %shard_map.79 = bf16[16,2,4,3072]{3,2,1,0:T(4,128)(2,1)} custom-call(bf16[1,2,4,3072]{3,2,1,0:T(4,128)(2,1)} %fusion.75.refs_0_), custom_call_target="tpu_custom_call" | custom-call | tf_op jit(solution)/shard_map/pallas_call | solution.py:90
  82.2 18.0 %shard_map.80 = bf16[16,2,4,3072]{3,2,1,0:T(4,128)(2,1)} custom-call(bf16[16,2,4,3072]{3,2,1,0:T(4,128)(2,1)} %convert_element_type.359.refs_0_), custom_call_target="tpu_custom_call" | custom-call | tf_op jit(solution)/shard_map/pallas_call | solution.py:90
  105.1 17.1 %shard_map.81 = bf16[16,2,4,3072]{3,2,1,0:T(4,128)(2,1)} custom-call(bf16[1,2,4,3072]{3,2,1,0:T(4,128)(2,1)} %fusion.74.refs_0_), custom_call_target="tpu_custom_call" | custom-call | tf_op jit(solution)/shard_map/pallas_call | solution.py:90
  125.7 6.6 %fusion.48 = bf16[128,3072]{1,0:T(8,128)(2,1)} fusion(bf16[1,768,3072]{2,1,0:T(8,128)(2,1)} %param.11, bf16[128,3072]{1,0:T(8,128)(2,1)S(1)} %convert_element_type.366, bf16[1,3072,768]{2,1,0:T(8,128)(2,1)} %param.10), kind=kOutput, calls=%fused_computation.40 | convolution fusion | flops 1209729024 | bytes 11010048 | tf_op jit(solution)/shard_map/dot_general | solution.py:122
  134.7 20.5 %shard_map.82 = bf16[16,2,4,3072]{3,2,1,0:T(4,128)(2,1)} custom-call(bf16[16,2,4,3072]{3,2,1,0:T(4,128)(2,1)} %convert_element_type.369.refs_0_), custom_call_target="tpu_custom_call" | custom-call | tf_op jit(solution)/shard_map/pallas_call | solution.py:90
  158.1 16.9 %shard_map.84 = bf16[16,2,4,3072]{3,2,1,0:T(4,128)(2,1)} custom-call(bf16[1,2,4,3072]{3,2,1,0:T(4,128)(2,1)} %bitcast_select_fusion.refs_0_), custom_call_target="tpu_custom_call" | custom-call | tf_op jit(solution)/shard_map/pallas_call | solution.py:90
  178.1 17.1 %shard_map.83 = bf16[16,2,4,3072]{3,2,1,0:T(4,128)(2,1)} custom-call(bf16[1,2,4,3072]{3,2,1,0:T(4,128)(2,1)} %fusion.73.refs_0_), custom_call_target="tpu_custom_call" | custom-call | tf_op jit(solution)/shard_map/pallas_call | solution.py:90
  201.1 7.5 %fusion.63 = bf16[128,3072]{1,0:T(8,128)(2,1)S(1)} fusion(bf16[1,3072,768]{2,1,0:T(8,128)(2,1)} %param.10, bf16[128,3072]{1,0:T(8,128)(2,1)S(1)} %copy-done.6, bf16[1,768,3072]{2,1,0:T(8,128)(2,1)} %param.11, f32[128,768]{1,0:T(8,128)S(1)} %fusion.22), kind=kOutput, calls=%fused_computation.45 | convolution fusion | flops 1210810368 | bytes 11403264 | tf_op jit(solution)/shard_map/dot_general | solution.py:140
  209.7 15.8 %shard_map.85 = bf16[16,2,4,3072]{3,2,1,0:T(4,128)(2,1)} custom-call(bf16[16,2,4,3072]{3,2,1,0:T(4,128)(2,1)} %convert_element_type.388.refs_0_), custom_call_target="tpu_custom_call" | custom-call | tf_op jit(solution)/shard_map/pallas_call | solution.py:90
  229.8 17.6 %shard_map.86 = bf16[16,2,4,3072]{3,2,1,0:T(4,128)(2,1)} custom-call(bf16[1,2,4,3072]{3,2,1,0:T(4,128)(2,1)} %bitcast.295), custom_call_target="tpu_custom_call" | custom-call | tf_op jit(solution)/shard_map/pallas_call | solution.py:90
  249.1 7.5 %fusion.60 = bf16[128,3072]{1,0:T(8,128)(2,1)S(1)} fusion(bf16[1,3072,768]{2,1,0:T(8,128)(2,1)} %param.10, bf16[128,3072]{1,0:T(8,128)(2,1)S(1)} %reshape.324, bf16[1,768,3072]{2,1,0:T(8,128)(2,1)} %param.11, f32[128,768]{1,0:T(8,128)S(1)} %fusion.22), kind=kOutput, calls=%fused_computation.44 | convolution fusion | flops 1210810368 | bytes 11403264 | tf_op jit(solution)/shard_map/dot_general | solution.py:140
  257.7 15.9 %shard_map.87 = bf16[16,2,4,3072]{3,2,1,0:T(4,128)(2,1)} custom-call(bf16[16,2,4,3072]{3,2,1,0:T(4,128)(2,1)} %convert_element_type.396.refs_0_), custom_call_target="tpu_custom_call" | custom-call | tf_op jit(solution)/shard_map/pallas_call | solution.py:90
  278.2 16.5 %shard_map.88 = bf16[16,2,4,3072]{3,2,1,0:T(4,128)(2,1)} custom-call(bf16[1,2,4,3072]{3,2,1,0:T(4,128)(2,1)} %bitcast.294), custom_call_target="tpu_custom_call" | custom-call | tf_op jit(solution)/shard_map/pallas_call | solution.py:90
  296.3 8.4 %fusion.57 = bf16[128,3072]{1,0:T(8,128)(2,1)} fusion(bf16[1,3072,768]{2,1,0:T(8,128)(2,1)} %param.10, bf16[128,3072]{1,0:T(8,128)(2,1)S(1)} %reshape.325, bf16[1,768,3072]{2,1,0:T(8,128)(2,1)} %param.11, f32[128,768]{1,0:T(8,128)S(1)} %fusion.22), kind=kOutput, calls=%fused_computation.43 | convolution fusion | flops 1210810368 | bytes 11403264 | tf_op jit(solution)/shard_map/dot_general | solution.py:140
  307.2 12.4 %shard_map.89 = bf16[16,2,4,3072]{3,2,1,0:T(4,128)(2,1)} custom-call(bf16[16,2,4,3072]{3,2,1,0:T(4,128)(2,1)} %convert_element_type.403.refs_0_), custom_call_target="tpu_custom_call" | custom-call | tf_op jit(solution)/shard_map/pallas_call | solution.py:90
  325.6 7.4 %collective-permute-done.11 = bf16[1,2,4,3072]{3,2,1,0:T(4,128)(2,1)} collective-permute-done((bf16[1,2,4,3072]{3,2,1,0:T(4,128)(2,1)}, bf16[1,2,4,3072]{3,2,1,0:T(4,128)(2,1)}, u32[]{:S(2)}, u32[]{:S(2)}) %collective-permute-start.11) | collective-permute-done | bytes 49184 | tf_op jit(solution)/shard_map/ppermute | solution.py:183
  336.6 17.6 %shard_map.90 = bf16[16,2,4,3072]{3,2,1,0:T(4,128)(2,1)} custom-call(bf16[1,2,4,3072]{3,2,1,0:T(4,128)(2,1)} %fusion.72.refs_0_), custom_call_target="tpu_custom_call" | custom-call | tf_op jit(solution)/shard_map/pallas_call | solution.py:90
  364.6 9.5 %subtract_convert_fusion.1 = bf16[3072,768]{1,0:T(8,128)(2,1)} fusion(bf16[1,3072,768]{2,1,0:T(8,128)(2,1)} %param.10, f32[128,3072]{1,0:T(8,128)S(1)} %reshape.327, f32[128]{0:T(128)} %rsqrt.51, bf16[128,3072]{1,0:T(8,128)(2,1)S(1)} %reshape.326, bf16[1,768,3072]{2,1,0:T(8,128)(2,1)} %param.11, f32[128,768]{1,0:T(8,128)S(1)} %fusion.22), kind=kOutput, calls=%fused_computation.3 | convolution fusion | flops 1220247552 | bytes 16908800 | tf_op jit(solution)/shard_map/dot_general | solution.py:174
  377.6 91.4 %collective-permute-done.13 = bf16[768,3072]{1,0:T(8,128)(2,1)} collective-permute-done((bf16[768,3072]{1,0:T(8,128)(2,1)}, bf16[768,3072]{1,0:T(8,128)(2,1)}, u32[]{:S(2)}, u32[]{:S(2)}) %collective-permute-start.13) | collective-permute-done | bytes 4718624 | tf_op jit(solution)/shard_map/ppermute | solution.py:254
  469.0 10.4 %fusion.1 = bf16[1,768,3072]{2,1,0:T(8,128)(2,1)} fusion(bf16[768,3072]{1,0:T(8,128)(2,1)} %subtract_convert_fusion, bf16[768,3072]{1,0:T(8,128)(2,1)} %collective-permute-done.13, pred[]{:T(512)S(6)} %ne.3), kind=kLoop, calls=%fused_computation.5 | loop fusion | flops 14155776 | bytes 14155777 | tf_op jit(solution)/shard_map/broadcast_in_dim | solution.py:263
  479.4 88.3 %collective-permute-done.12 = bf16[3072,768]{1,0:T(8,128)(2,1)} collective-permute-done((bf16[3072,768]{1,0:T(8,128)(2,1)}, bf16[3072,768]{1,0:T(8,128)(2,1)}, u32[]{:S(2)}, u32[]{:S(2)}) %collective-permute-start.12) | collective-permute-done | bytes 4718624 | tf_op jit(solution)/shard_map/ppermute | solution.py:253
  567.8 6.2 %fusion = bf16[1,3072,768]{2,1,0:T(8,128)(2,1)} fusion(bf16[3072,768]{1,0:T(8,128)(2,1)S(1)} %bitcast.288, bf16[3072,768]{1,0:T(8,128)(2,1)} %collective-permute-done.12, pred[]{:T(512)S(6)} %ne.3), kind=kLoop, calls=%fused_computation.4 | loop fusion | flops 14155776 | bytes 14155777 | tf_op jit(solution)/shard_map/broadcast_in_dim | solution.py:263
  (189 shorter events, 92.1 us)
Async XLA Ops:
  49.0 6.2 %collective-permute-start.1 = (bf16[1,2,4,3072]{3,2,1,0:T(4,128)(2,1)S(1)}, bf16[1,2,4,3072]{3,2,1,0:T(4,128)(2,1)S(1)}, u32[]{:S(2)}, u32[]{:S(2)}) collective-permute-start(bf16[1,2,4,3072]{3,2,1,0:T(4,128)(2,1)S(1)} %fusion.193), channel_id=1, source_target_pairs={{0,48},{16,32},{1,49},{17,33},{2,50},{18,34},{3,51},{19,35},{4,52}... | collective-permute-start | bytes 147464 | tf_op jit(solution)/shard_map/ppermute | solution.py:183
  50.9 4.3 collective-permute-start
  55.1 103.0 %copy-start.10 = (bf16[2,2,4,2,4]{4,3,2,0,1:T(2,128)(2,1)}, bf16[2,2,4,2,4]{4,3,2,0,1:T(2,128)(2,1)S(1)}, u32[]{:S(2)}) copy-start(bf16[2,2,4,2,4]{4,3,2,0,1:T(2,128)(2,1)S(1)} %get-tuple-element.21) | copy-start | bytes 772
  55.1 48.4 %copy-start.19 = (pred[2,1,4]{2,0,1:T(4,128)(4,1)}, pred[2,1,4]{2,0,1:T(4,128)(4,1)S(1)}, u32[]{:S(2)}) copy-start(pred[2,1,4]{2,0,1:T(4,128)(4,1)S(1)} %copy.121) | copy-start | bytes 28
  75.2 28.3 %copy-start.8 = (bf16[2,4,1,3072]{3,1,2,0:T(4,128)(2,1)S(1)}, bf16[2,4,1,3072]{3,1,2,0:T(4,128)(2,1)}, u32[]{:S(2)}) copy-start(bf16[2,4,1,3072]{3,1,2,0:T(4,128)(2,1)} %param.8) | copy-start | bytes 147460
  101.7 2.5 collective-permute-start.3
  102.4 1.9 collective-permute-start.2
  125.7 31.0 %copy-start.2 = (bf16[16,2,4,3072]{3,2,1,0:T(4,128)(2,1)S(1)}, bf16[16,2,4,3072]{3,2,1,0:T(4,128)(2,1)}, u32[]{:S(2)}) copy-start(bf16[16,2,4,3072]{3,2,1,0:T(4,128)(2,1)} %shard_map.81) | copy-start | bytes 2359300
  156.7 20.6 %collective-permute-start.5 = (bf16[1,2,4,3072]{3,2,1,0:T(4,128)(2,1)S(1)}, bf16[1,2,4,3072]{3,2,1,0:T(4,128)(2,1)S(1)}, u32[]{:S(2)}, u32[]{:S(2)}) collective-permute-start(bf16[1,2,4,3072]{3,2,1,0:T(4,128)(2,1)S(1)} %fusion.191), channel_id=1, source_target_pairs={{64,112},{80,96},{65,113},{81,97},{66,114},{82,98},{67,115},{83,99... | collective-permute-start | bytes 147464 | tf_op jit(solution)/shard_map/ppermute | solution.py:183
  157.4 19.9 %collective-permute-start.4 = (bf16[1,2,4,3072]{3,2,1,0:T(4,128)(2,1)S(1)}, bf16[1,2,4,3072]{3,2,1,0:T(4,128)(2,1)S(1)}, u32[]{:S(2)}, u32[]{:S(2)}) collective-permute-start(bf16[1,2,4,3072]{3,2,1,0:T(4,128)(2,1)S(1)} %fusion.191), channel_id=1, source_target_pairs={{64,96},{80,112},{65,97},{81,113},{66,98},{82,114},{67,99},{83,115... | collective-permute-start | bytes 147464 | tf_op jit(solution)/shard_map/ppermute | solution.py:183
  201.0 27.8 %copy-start.11 = (bf16[2,2,4,2,4]{4,3,2,0,1:T(2,128)(2,1)S(1)}, bf16[2,2,4,2,4]{4,3,2,0,1:T(2,128)(2,1)}, u32[]{:S(2)}) copy-start(bf16[2,2,4,2,4]{4,3,2,0,1:T(2,128)(2,1)} %copy-done.10) | copy-start | bytes 772
  227.3 1.5 collective-permute-start.7
  228.0 0.9 collective-permute-start.6
  275.4 2.0 collective-permute-start.9
  276.0 1.3 collective-permute-start.8
  304.7 49.5 %copy-start.3 = (bf16[16,2,4,3072]{3,2,1,0:T(4,128)(2,1)S(1)}, bf16[16,2,4,3072]{3,2,1,0:T(4,128)(2,1)}, u32[]{:S(2)}) copy-start(bf16[16,2,4,3072]{3,2,1,0:T(4,128)(2,1)} %shard_map.84) | copy-start | bytes 2359300
  304.7 49.5 %copy-start.4 = (bf16[16,2,4,3072]{3,2,1,0:T(4,128)(2,1)S(1)}, bf16[16,2,4,3072]{3,2,1,0:T(4,128)(2,1)}, u32[]{:S(2)}) copy-start(bf16[16,2,4,3072]{3,2,1,0:T(4,128)(2,1)} %shard_map.86) | copy-start | bytes 2359300
  304.7 49.5 %copy-start.5 = (bf16[16,2,4,3072]{3,2,1,0:T(4,128)(2,1)S(1)}, bf16[16,2,4,3072]{3,2,1,0:T(4,128)(2,1)}, u32[]{:S(2)}) copy-start(bf16[16,2,4,3072]{3,2,1,0:T(4,128)(2,1)} %shard_map.88) | copy-start | bytes 2359300
  322.8 10.2 %collective-permute-start.11 = (bf16[1,2,4,3072]{3,2,1,0:T(4,128)(2,1)}, bf16[1,2,4,3072]{3,2,1,0:T(4,128)(2,1)}, u32[]{:S(2)}, u32[]{:S(2)}) collective-permute-start(bf16[1,2,4,3072]{3,2,1,0:T(4,128)(2,1)} %fusion.186), channel_id=1, source_target_pairs={{32,16},{48,0},{33,17},{49,1},{34,18},{50,2},{35,19},{51,3},{36,20... | collective-permute-start | bytes 147464 | tf_op jit(solution)/shard_map/ppermute | solution.py:183
  324.1 10.1 %collective-permute-start.10 = (bf16[1,2,4,3072]{3,2,1,0:T(4,128)(2,1)}, bf16[1,2,4,3072]{3,2,1,0:T(4,128)(2,1)}, u32[]{:S(2)}, u32[]{:S(2)}) collective-permute-start(bf16[1,2,4,3072]{3,2,1,0:T(4,128)(2,1)} %fusion.186), channel_id=1, source_target_pairs={{32,0},{48,16},{33,1},{49,17},{34,2},{50,18},{35,3},{51,19},{36,4}... | collective-permute-start | bytes 147464 | tf_op jit(solution)/shard_map/ppermute | solution.py:183
  363.9 105.1 %collective-permute-start.13 = (bf16[768,3072]{1,0:T(8,128)(2,1)}, bf16[768,3072]{1,0:T(8,128)(2,1)}, u32[]{:S(2)}, u32[]{:S(2)}) collective-permute-start(bf16[768,3072]{1,0:T(8,128)(2,1)} %subtract_convert_fusion), channel_id=1, source_target_pairs={{0,16},{16,0},{1,17},{17,1},{2,18},{18,2},{3,19},{19,3},{4,20},{20... | collective-permute-start | bytes 14155784 | tf_op jit(solution)/shard_map/ppermute | solution.py:254
  374.2 193.6 %collective-permute-start.12 = (bf16[3072,768]{1,0:T(8,128)(2,1)}, bf16[3072,768]{1,0:T(8,128)(2,1)}, u32[]{:S(2)}, u32[]{:S(2)}) collective-permute-start(bf16[3072,768]{1,0:T(8,128)(2,1)} %subtract_convert_fusion.1), channel_id=1, source_target_pairs={{0,16},{16,0},{1,17},{17,1},{2,18},{18,2},{3,19},{19,3},{4,20},{20... | collective-permute-start | bytes 14155784 | tf_op jit(solution)/shard_map/ppermute | solution.py:253
  376.8 190.9 %slice-start = ((s8[4718592]{0:T(1024)(128)(4,1)}), s8[524288]{0:T(1024)(128)(4,1)S(1)}, s32[]{:S(2)}) async-start(s8[4718592]{0:T(1024)(128)(4,1)} %bitcast.287), calls=%async_computation | async-start | bytes 1048576
  377.5 190.2 %slice-start.1 = ((s8[4718592]{0:T(1024)(128)(4,1)}), s8[4194304]{0:T(1024)(128)(4,1)S(1)}, s32[]{:S(2)}) async-start(s8[4718592]{0:T(1024)(128)(4,1)} %bitcast.287), calls=%async_computation.1 | async-start | bytes 8388608
  (14 other events, 319.9 us)

commit v4 on v3

--- a/solution.py
+++ b/solution.py
@@ -86,6 +86,12 @@
 
 
 def plane_call(value, count, spread, ident):
+    lanes = value[0].size // 16
+    dense = plane_dense(value.reshape(value.shape[0], 16, lanes), count, spread, ident)
+    return dense.reshape((count,) + value.shape[1:])
+
+
+def plane_dense(value, count, spread, ident):
     shape = (count,) + value.shape[1:]
     return pl.pallas_call(
         lambda *refs: plane_kernel(count, spread, *refs),

time: 583 us -> 614 us (1.053)
  the two profiles are of different devices: /device:TPU:10 before, /device:TPU:96 now
where the time goes in v4:
time: 614 us; the launch traced here: 605 us
  Pallas kernels  239 us (39%)
  waiting for transfers between devices  190 us (31%)
  matrix products  61.1 us (10%)
  other arithmetic  47.3 us (8%)
  local copies, waits for them, and re-layouts  41.9 us (7%)
  starting transfers between devices  22.5 us (4%)
    pallas_call x14, Pallas kernels, plane_dense(): pl.pallas_call(lambda *refs: plane_kernel(count, spread, *refs), out_shap...  239 us
    ppermute x1, waiting for transfers between devices, on_device(): other_in = lax.ppermute(stepped_in, 'half', swap)  94.4 us
    ppermute x1, waiting for transfers between devices, on_device(): other_out = lax.ppermute(stepped_out, 'half', swap)  89.6 us
    dot_general x3, matrix products, backward_piece(): lax.dot_general(d_pre, weight_in, (((1,), (1,)), ((), ())), preferred_ele...  23.6 us
    broadcast_in_dim x2, other arithmetic, on_device(): return (new_in[None], new_out[None])  19.8 us
    dot_general x3, matrix products, forward_piece(): jnp.dot(activated, weight_out, preferred_element_type=jnp.float32)  17 us
    ppermute x6, starting transfers between devices, cross_boundary(): lax.ppermute(piece, PAIR, straight)  15.2 us
  transfers between devices with their start and end apart: 14, of which 3 were waited for; matrix products, arithmetic and copies ran while one was open for 4% of the time, Pallas kernels for 3%

profile of v4, /device:TPU:96, one launch (start us, length us, event | category | flops | bytes accessed | tf_op | source)
XLA Modules:
  0.0 604.6 jit_solution(13722026527814192577)
XLA Ops:
  2.0 18.9 %shard_map.77 = bf16[16,16,1536]{2,1,0:T(8,128)(2,1)} custom-call(bf16[1,16,1536]{2,1,0:T(8,128)(2,1)} %reshape_transpose.3.refs_0_), custom_call_target="tpu_custom_call" | custom-call | tf_op jit(solution)/shard_map/pallas_call | solution.py:96
  33.2 17.3 %shard_map.78 = bf16[16,16,1536]{2,1,0:T(8,128)(2,1)} custom-call(bf16[16,16,1536]{2,1,0:T(8,128)(2,1)} %convert_element_type.367.refs_0_), custom_call_target="tpu_custom_call" | custom-call | tf_op jit(solution)/shard_map/pallas_call | solution.py:96
  58.9 17.0 %shard_map.79 = bf16[16,16,1536]{2,1,0:T(8,128)(2,1)} custom-call(bf16[1,16,1536]{2,1,0:T(8,128)(2,1)} %reshape_broadcast_in_dim.18.refs_0_), custom_call_target="tpu_custom_call" | custom-call | tf_op jit(solution)/shard_map/pallas_call | solution.py:96
  88.2 15.5 %shard_map.80 = bf16[16,16,1536]{2,1,0:T(8,128)(2,1)} custom-call(bf16[16,16,1536]{2,1,0:T(8,128)(2,1)} %convert_element_type.377.refs_0_), custom_call_target="tpu_custom_call" | custom-call | tf_op jit(solution)/shard_map/pallas_call | solution.py:96
  105.7 10.2 %collective-permute-start.2 = (bf16[1,2,4,3072]{3,2,1,0:T(4,128)(2,1)S(1)}, bf16[1,2,4,3072]{3,2,1,0:T(4,128)(2,1)S(1)}, u32[]{:S(2)}, u32[]{:S(2)}) collective-permute-start(bf16[1,2,4,3072]{3,2,1,0:T(4,128)(2,1)S(1)} %add_convert_fusion.1), channel_id=1, source_target_pairs={{32,64},{48,80},{33,65},{49,81},{34,66},{50,82},{35,67},{51,83},{3... | collective-permute-start | bytes 147464 | tf_op jit(solution)/shard_map/ppermute | solution.py:189
  117.4 14.8 %shard_map.81 = bf16[16,16,1536]{2,1,0:T(8,128)(2,1)} custom-call(bf16[1,16,1536]{2,1,0:T(8,128)(2,1)} %reshape_broadcast_in_dim.19.refs_0_), custom_call_target="tpu_custom_call" | custom-call | tf_op jit(solution)/shard_map/pallas_call | solution.py:96
  145.2 22.6 %shard_map.82 = bf16[16,16,1536]{2,1,0:T(8,128)(2,1)} custom-call(bf16[16,16,1536]{2,1,0:T(8,128)(2,1)} %convert_element_type.387.refs_0_), custom_call_target="tpu_custom_call" | custom-call | tf_op jit(solution)/shard_map/pallas_call | solution.py:96
  171.9 17.5 %shard_map.84 = bf16[16,16,1536]{2,1,0:T(8,128)(2,1)} custom-call(bf16[1,16,1536]{2,1,0:T(8,128)(2,1)} %broadcast_select_fusion.refs_0_), custom_call_target="tpu_custom_call" | custom-call | tf_op jit(solution)/shard_map/pallas_call | solution.py:96
  192.5 17.3 %shard_map.83 = bf16[16,16,1536]{2,1,0:T(8,128)(2,1)} custom-call(bf16[1,16,1536]{2,1,0:T(8,128)(2,1)} %reshape_broadcast_in_dim.20.refs_0_), custom_call_target="tpu_custom_call" | custom-call | tf_op jit(solution)/shard_map/pallas_call | solution.py:96
  218.1 7.5 %fusion.63 = bf16[128,3072]{1,0:T(8,128)(2,1)S(1)} fusion(bf16[1,3072,768]{2,1,0:T(8,128)(2,1)} %param.10, bf16[128,3072]{1,0:T(8,128)(2,1)S(1)} %copy-done.7, bf16[1,768,3072]{2,1,0:T(8,128)(2,1)} %param.11, f32[128,768]{1,0:T(8,128)S(1)} %fusion.22), kind=kOutput, calls=%fused_computation.45 | convolution fusion | flops 1210810368 | bytes 11403264 | tf_op jit(solution)/shard_map/dot_general | solution.py:146
  226.8 17.1 %shard_map.85 = bf16[16,16,1536]{2,1,0:T(8,128)(2,1)} custom-call(bf16[16,16,1536]{2,1,0:T(8,128)(2,1)} %convert_element_type.406.refs_0_), custom_call_target="tpu_custom_call" | custom-call | tf_op jit(solution)/shard_map/pallas_call | solution.py:96
  248.9 15.2 %shard_map.86 = bf16[16,16,1536]{2,1,0:T(8,128)(2,1)} custom-call(bf16[1,16,1536]{2,1,0:T(8,128)(2,1)} %reshape_broadcast_in_dim.21.refs_0_), custom_call_target="tpu_custom_call" | custom-call | tf_op jit(solution)/shard_map/pallas_call | solution.py:96
  265.5 7.8 %fusion.60 = bf16[128,3072]{1,0:T(8,128)(2,1)S(1)} fusion(bf16[1,3072,768]{2,1,0:T(8,128)(2,1)} %param.10, bf16[128,3072]{1,0:T(8,128)(2,1)S(1)} %reshape_reshape.13, bf16[1,768,3072]{2,1,0:T(8,128)(2,1)} %param.11, f32[128,768]{1,0:T(8,128)S(1)} %fusion.22), kind=kOutput, calls=%fused_computation.44 | convolution fusion | flops 1210810368 | bytes 11403264 | tf_op jit(solution)/shard_map/dot_general | solution.py:146
  274.4 16.6 %shard_map.87 = bf16[16,16,1536]{2,1,0:T(8,128)(2,1)} custom-call(bf16[16,16,1536]{2,1,0:T(8,128)(2,1)} %convert_element_type.414.refs_0_), custom_call_target="tpu_custom_call" | custom-call | tf_op jit(solution)/shard_map/pallas_call | solution.py:96
  295.5 14.3 %shard_map.88 = bf16[16,16,1536]{2,1,0:T(8,128)(2,1)} custom-call(bf16[1,16,1536]{2,1,0:T(8,128)(2,1)} %reshape_broadcast_in_dim.22.refs_0_), custom_call_target="tpu_custom_call" | custom-call | tf_op jit(solution)/shard_map/pallas_call | solution.py:96
  312.1 8.4 %fusion.57 = bf16[128,3072]{1,0:T(8,128)(2,1)} fusion(bf16[1,3072,768]{2,1,0:T(8,128)(2,1)} %param.10, bf16[128,3072]{1,0:T(8,128)(2,1)S(1)} %reshape_reshape.14, bf16[1,768,3072]{2,1,0:T(8,128)(2,1)} %param.11, f32[128,768]{1,0:T(8,128)S(1)} %fusion.22), kind=kOutput, calls=%fused_computation.43 | convolution fusion | flops 1210810368 | bytes 11403264 | tf_op jit(solution)/shard_map/dot_general | solution.py:146
  322.8 15.1 %shard_map.89 = bf16[16,16,1536]{2,1,0:T(8,128)(2,1)} custom-call(bf16[16,16,1536]{2,1,0:T(8,128)(2,1)} %convert_element_type.421.refs_0_), custom_call_target="tpu_custom_call" | custom-call | tf_op jit(solution)/shard_map/pallas_call | solution.py:96
  357.3 20.2 %shard_map.90 = bf16[16,16,1536]{2,1,0:T(8,128)(2,1)} custom-call(bf16[1,16,1536]{2,1,0:T(8,128)(2,1)} %reshape_broadcast_in_dim.23.refs_0_), custom_call_target="tpu_custom_call" | custom-call | tf_op jit(solution)/shard_map/pallas_call | solution.py:96
  379.9 9.7 %subtract_convert_fusion.1 = bf16[3072,768]{1,0:T(8,128)(2,1)} fusion(bf16[1,3072,768]{2,1,0:T(8,128)(2,1)} %param.10, f32[128,3072]{1,0:T(8,128)} %reshape.400, f32[128]{0:T(128)S(1)} %copy-done.25, bf16[128,3072]{1,0:T(8,128)(2,1)} %select_n.268, bf16[1,768,3072]{2,1,0:T(8,128)(2,1)} %param.11, f32[128,768]{1,0:T(8,128)S(1)} %fusion.22), kind=kOutput, calls=%fused_computation.3 | convolution fusion | flops 1220247552 | bytes 16908800 | tf_op jit(solution)/shard_map/dot_general | solution.py:180
  391.2 6.2 %subtract_convert_fusion = bf16[768,3072]{1,0:T(8,128)(2,1)} fusion(bf16[1,768,3072]{2,1,0:T(8,128)(2,1)} %param.11, bf16[128,3072]{1,0:T(8,128)(2,1)} %reshape.399, bf16[128,3072]{1,0:T(8,128)(2,1)S(1)} %copy-done.12, bf16[128,3072]{1,0:T(8,128)(2,1)S(1)} %copy-done.10, bf16[128,3072]{1,0:T(8,128)(2,1)S(1)} %copy-done.8, pred[]{:T(512)S(6)} %eq.192, ...), kind=kOutput, calls=%fused_computation.1 | convolution fusion | flops 615579648 | bytes 12976131 | tf_op jit(solution)/shard_map/dot_general | solution.py:171
  400.3 94.4 %collective-permute-done.12 = bf16[3072,768]{1,0:T(8,128)(2,1)} collective-permute-done((bf16[3072,768]{1,0:T(8,128)(2,1)}, bf16[3072,768]{1,0:T(8,128)(2,1)}, u32[]{:S(2)}, u32[]{:S(2)}) %collective-permute-start.12) | collective-permute-done | bytes 4718624 | tf_op jit(solution)/shard_map/ppermute | solution.py:259
  494.7 9.4 %fusion = bf16[1,3072,768]{2,1,0:T(8,128)(2,1)} fusion(bf16[3072,768]{1,0:T(8,128)(2,1)} %subtract_convert_fusion.1, bf16[3072,768]{1,0:T(8,128)(2,1)} %collective-permute-done.12, pred[]{:T(512)S(6)} %ne.3), kind=kLoop, calls=%fused_computation.4 | loop fusion | flops 14155776 | bytes 14155777 | tf_op jit(solution)/shard_map/broadcast_in_dim | solution.py:269
  504.1 89.6 %collective-permute-done.13 = bf16[768,3072]{1,0:T(8,128)(2,1)} collective-permute-done((bf16[768,3072]{1,0:T(8,128)(2,1)}, bf16[768,3072]{1,0:T(8,128)(2,1)}, u32[]{:S(2)}, u32[]{:S(2)}) %collective-permute-start.13) | collective-permute-done | bytes 4718624 | tf_op jit(solution)/shard_map/ppermute | solution.py:260
  593.7 10.4 %fusion.1 = bf16[1,768,3072]{2,1,0:T(8,128)(2,1)} fusion(bf16[768,3072]{1,0:T(8,128)(2,1)} %subtract_convert_fusion, bf16[768,3072]{1,0:T(8,128)(2,1)} %collective-permute-done.13, pred[]{:T(512)S(6)} %ne.3), kind=kLoop, calls=%fused_computation.5 | loop fusion | flops 14155776 | bytes 14155777 | tf_op jit(solution)/shard_map/broadcast_in_dim | solution.py:269
  (247 shorter events, 108.9 us)
Async XLA Ops:
  51.9 6.1 %collective-permute-start.1 = (bf16[1,2,4,3072]{3,2,1,0:T(4,128)(2,1)S(1)}, bf16[1,2,4,3072]{3,2,1,0:T(4,128)(2,1)S(1)}, u32[]{:S(2)}, u32[]{:S(2)}) collective-permute-start(bf16[1,2,4,3072]{3,2,1,0:T(4,128)(2,1)S(1)} %add_convert_fusion.2), channel_id=1, source_target_pairs={{0,48},{16,32},{1,49},{17,33},{2,50},{18,34},{3,51},{19,35},{4,52}... | collective-permute-start | bytes 147464 | tf_op jit(solution)/shard_map/ppermute | solution.py:189
  53.2 4.8 collective-permute-start
  81.3 34.8 %copy-start.16 = (bf16[2,4,1,3072]{3,1,2,0:T(4,128)(2,1)S(1)}, bf16[2,4,1,3072]{3,1,2,0:T(4,128)(2,1)}, u32[]{:S(2)}) copy-start(bf16[2,4,1,3072]{3,1,2,0:T(4,128)(2,1)} %param.8) | copy-start | bytes 147460
  105.0 11.1 %collective-permute-start.3 = (bf16[1,2,4,3072]{3,2,1,0:T(4,128)(2,1)S(1)}, bf16[1,2,4,3072]{3,2,1,0:T(4,128)(2,1)S(1)}, u32[]{:S(2)}, u32[]{:S(2)}) collective-permute-start(bf16[1,2,4,3072]{3,2,1,0:T(4,128)(2,1)S(1)} %add_convert_fusion.1), channel_id=1, source_target_pairs={{32,80},{48,64},{33,81},{49,65},{34,82},{50,66},{35,83},{51,67},{3... | collective-permute-start | bytes 147464 | tf_op jit(solution)/shard_map/ppermute | solution.py:189
  105.7 10.8 %collective-permute-start.2 = (bf16[1,2,4,3072]{3,2,1,0:T(4,128)(2,1)S(1)}, bf16[1,2,4,3072]{3,2,1,0:T(4,128)(2,1)S(1)}, u32[]{:S(2)}, u32[]{:S(2)}) collective-permute-start(bf16[1,2,4,3072]{3,2,1,0:T(4,128)(2,1)S(1)} %add_convert_fusion.1), channel_id=1, source_target_pairs={{32,64},{48,80},{33,65},{49,81},{34,66},{50,82},{35,67},{51,83},{3... | collective-permute-start | bytes 147464 | tf_op jit(solution)/shard_map/ppermute | solution.py:189
  144.0 68.4 %copy-start = (bf16[16,16,1536]{2,1,0:T(8,128)(2,1)S(1)}, bf16[16,16,1536]{2,1,0:T(8,128)(2,1)}, u32[]{:S(2)}) copy-start(bf16[16,16,1536]{2,1,0:T(8,128)(2,1)} %shard_map.77) | copy-start | bytes 2359300
  144.0 68.4 %copy-start.1 = (bf16[16,16,1536]{2,1,0:T(8,128)(2,1)S(1)}, bf16[16,16,1536]{2,1,0:T(8,128)(2,1)}, u32[]{:S(2)}) copy-start(bf16[16,16,1536]{2,1,0:T(8,128)(2,1)} %shard_map.79) | copy-start | bytes 2359300
  144.0 68.4 %copy-start.2 = (bf16[16,16,1536]{2,1,0:T(8,128)(2,1)S(1)}, bf16[16,16,1536]{2,1,0:T(8,128)(2,1)}, u32[]{:S(2)}) copy-start(bf16[16,16,1536]{2,1,0:T(8,128)(2,1)} %shard_map.81) | copy-start | bytes 2359300
  170.0 21.6 %collective-permute-start.5 = (bf16[1,2,4,3072]{3,2,1,0:T(4,128)(2,1)S(1)}, bf16[1,2,4,3072]{3,2,1,0:T(4,128)(2,1)S(1)}, u32[]{:S(2)}, u32[]{:S(2)}) collective-permute-start(bf16[1,2,4,3072]{3,2,1,0:T(4,128)(2,1)S(1)} %add_convert_fusion), channel_id=1, source_target_pairs={{64,112},{80,96},{65,113},{81,97},{66,114},{82,98},{67,115},{83,99... | collective-permute-start | bytes 147464 | tf_op jit(solution)/shard_map/ppermute | solution.py:189
  170.7 20.9 %collective-permute-start.4 = (bf16[1,2,4,3072]{3,2,1,0:T(4,128)(2,1)S(1)}, bf16[1,2,4,3072]{3,2,1,0:T(4,128)(2,1)S(1)}, u32[]{:S(2)}, u32[]{:S(2)}) collective-permute-start(bf16[1,2,4,3072]{3,2,1,0:T(4,128)(2,1)S(1)} %add_convert_fusion), channel_id=1, source_target_pairs={{64,96},{80,112},{65,97},{81,113},{66,98},{82,114},{67,99},{83,115... | collective-permute-start | bytes 147464 | tf_op jit(solution)/shard_map/ppermute | solution.py:189
  246.2 46.3 %copy-start.13 = (bf16[1,2,4,3072]{3,2,1,0:T(4,128)(2,1)}, bf16[1,2,4,3072]{3,2,1,0:T(4,128)(2,1)S(1)}, u32[]{:S(2)}) copy-start(bf16[1,2,4,3072]{3,2,1,0:T(4,128)(2,1)S(1)} %get-tuple-element.3) | copy-start | bytes 147460
  246.4 1.6 collective-permute-start.7
  247.0 0.9 collective-permute-start.6
  292.6 2.0 collective-permute-start.9
  293.3 1.3 collective-permute-start.8
  312.1 31.8 %copy-start.22 = (f32[2,4]{1,0:T(2,128)S(1)}, f32[2,4]{1,0:T(2,128)}, u32[]{:S(2)}) copy-start(f32[2,4]{1,0:T(2,128)} %fusion.218) | copy-start | bytes 100
  320.5 35.9 %copy-start.26 = (bf16[2,4,2,4]{3,2,1,0:T(2,128)(2,1)S(1)}, bf16[2,4,2,4]{3,2,1,0:T(2,128)(2,1)}, u32[]{:S(2)}) copy-start(bf16[2,4,2,4]{3,2,1,0:T(2,128)(2,1)} %get-tuple-element.33) | copy-start | bytes 388
  320.5 57.0 %copy-start.3 = (bf16[16,16,1536]{2,1,0:T(8,128)(2,1)S(1)}, bf16[16,16,1536]{2,1,0:T(8,128)(2,1)}, u32[]{:S(2)}) copy-start(bf16[16,16,1536]{2,1,0:T(8,128)(2,1)} %shard_map.84) | copy-start | bytes 2359300
  320.5 57.0 %copy-start.4 = (bf16[16,16,1536]{2,1,0:T(8,128)(2,1)S(1)}, bf16[16,16,1536]{2,1,0:T(8,128)(2,1)}, u32[]{:S(2)}) copy-start(bf16[16,16,1536]{2,1,0:T(8,128)(2,1)} %shard_map.86) | copy-start | bytes 2359300
  320.5 57.0 %copy-start.5 = (bf16[16,16,1536]{2,1,0:T(8,128)(2,1)S(1)}, bf16[16,16,1536]{2,1,0:T(8,128)(2,1)}, u32[]{:S(2)}) copy-start(bf16[16,16,1536]{2,1,0:T(8,128)(2,1)} %shard_map.88) | copy-start | bytes 2359300
  345.6 9.9 %collective-permute-start.11 = (bf16[1,2,4,3072]{3,2,1,0:T(4,128)(2,1)}, bf16[1,2,4,3072]{3,2,1,0:T(4,128)(2,1)}, u32[]{:S(2)}, u32[]{:S(2)}) collective-permute-start(bf16[1,2,4,3072]{3,2,1,0:T(4,128)(2,1)} %fusion.190), channel_id=1, source_target_pairs={{32,16},{48,0},{33,17},{49,1},{34,18},{50,2},{35,19},{51,3},{36,20... | collective-permute-start | bytes 147464 | tf_op jit(solution)/shard_map/ppermute | solution.py:189
  346.9 8.7 %collective-permute-start.10 = (bf16[1,2,4,3072]{3,2,1,0:T(4,128)(2,1)}, bf16[1,2,4,3072]{3,2,1,0:T(4,128)(2,1)}, u32[]{:S(2)}, u32[]{:S(2)}) collective-permute-start(bf16[1,2,4,3072]{3,2,1,0:T(4,128)(2,1)} %fusion.190), channel_id=1, source_target_pairs={{32,0},{48,16},{33,1},{49,17},{34,2},{50,18},{35,3},{51,19},{36,4}... | collective-permute-start | bytes 147464 | tf_op jit(solution)/shard_map/ppermute | solution.py:189
  389.6 105.1 %collective-permute-start.12 = (bf16[3072,768]{1,0:T(8,128)(2,1)}, bf16[3072,768]{1,0:T(8,128)(2,1)}, u32[]{:S(2)}, u32[]{:S(2)}) collective-permute-start(bf16[3072,768]{1,0:T(8,128)(2,1)} %subtract_convert_fusion.1), channel_id=1, source_target_pairs={{0,16},{16,0},{1,17},{17,1},{2,18},{18,2},{3,19},{19,3},{4,20},{20... | collective-permute-start | bytes 14155784 | tf_op jit(solution)/shard_map/ppermute | solution.py:259
  397.4 196.3 %collective-permute-start.13 = (bf16[768,3072]{1,0:T(8,128)(2,1)}, bf16[768,3072]{1,0:T(8,128)(2,1)}, u32[]{:S(2)}, u32[]{:S(2)}) collective-permute-start(bf16[768,3072]{1,0:T(8,128)(2,1)} %subtract_convert_fusion), channel_id=1, source_target_pairs={{0,16},{16,0},{1,17},{17,1},{2,18},{18,2},{3,19},{19,3},{4,20},{20... | collective-permute-start | bytes 14155784 | tf_op jit(solution)/shard_map/ppermute | solution.py:260
  (20 other events, 287.2 us)

commit v5 on v4

--- a/solution.py
+++ b/solution.py
@@ -187,6 +187,18 @@
     straight = [(source * replicas + h, target * replicas + h) for h in range(replicas)]
     crossed = [(source * replicas + h, target * replicas + (replicas - 1 - h)) for h in range(replicas)]
     return (lax.ppermute(piece, PAIR, straight), lax.ppermute(piece, PAIR, crossed))
+
+
+def swap_sections(stepped_in, stepped_out, chosen, section_count, replicas):
+    pairs = [
+        (section * replicas + h, section * replicas + replicas - 1 - h)
+        for section in range(section_count)
+        if (chosen >> section) & 1
+        for h in range(replicas)
+    ]
+    if not pairs:
+        return (jnp.zeros_like(stepped_in), jnp.zeros_like(stepped_out))
+    return (lax.ppermute(stepped_in, PAIR, pairs), lax.ppermute(stepped_out, PAIR, pairs))
 
 
 def on_device(block_inputs, routes, cotangent, gossip_peer, w_in, w_out):
@@ -255,9 +267,18 @@
     stepped_out = (weight_out.astype(jnp.float32) - LEARNING * accum_out).astype(jnp.bfloat16)
     partner = gossip_peer[my_section, replica]
     paired = partner != replica
-    swap = [(h, replicas - 1 - h) for h in range(replicas)]
-    other_in = lax.ppermute(stepped_in, "half", swap)
-    other_out = lax.ppermute(stepped_out, "half", swap)
+    pattern = jnp.sum(
+        (gossip_peer[:, 0] != 0).astype(jnp.int32) << jnp.arange(section_count, dtype=jnp.int32)
+    )
+    other_in, other_out = lax.switch(
+        pattern,
+        [
+            lambda a, b, chosen=chosen: swap_sections(a, b, chosen, section_count, replicas)
+            for chosen in range(2**section_count)
+        ],
+        stepped_in,
+        stepped_out,
+    )
     chosen_in = jnp.where(paired, other_in, stepped_in)
     chosen_out = jnp.where(paired, other_out, stepped_out)
     new_in = (0.5 * (stepped_in.astype(jnp.float32) + chosen_in.astype(jnp.float32))).astype(

time: 614 us -> 633 us (1.031)
  the two profiles are of different devices: /device:TPU:96 before, /device:TPU:1 now
where the time goes in v5:
time: 633 us; the launch traced here: 623 us
  Pallas kernels  230 us (36%)
  waiting for transfers between devices  200 us (32%)
  matrix products  61 us (10%)
  other arithmetic  44 us (7%)
  starting transfers between devices  42.7 us (7%)
  local copies, waits for them, and re-layouts  41.9 us (7%)
    pallas_call x14, Pallas kernels, plane_dense(): pl.pallas_call(lambda *refs: plane_kernel(count, spread, *refs), out_shap...  230 us
    ppermute x1, waiting for transfers between devices, swap_sections(): lax.ppermute(stepped_out, PAIR, pairs)  101 us
    ppermute x1, waiting for transfers between devices, swap_sections(): lax.ppermute(stepped_in, PAIR, pairs)  91.9 us
    dot_general x3, matrix products, backward_piece(): lax.dot_general(d_pre, weight_in, (((1,), (1,)), ((), ())), preferred_ele...  23 us
    dot_general x3, matrix products, forward_piece(): jnp.dot(activated, weight_out, preferred_element_type=jnp.float32)  17 us
    broadcast_in_dim x2, other arithmetic, on_device(): return (new_in[None], new_out[None])  16.1 us
    ppermute x6, starting transfers between devices, cross_boundary(): lax.ppermute(piece, PAIR, crossed)  13.9 us
  transfers between devices with their start and end apart: 14, of which 6 were waited for; matrix products, arithmetic and copies ran while one was open for 1% of the time, Pallas kernels for 3%

profile of v5, /device:TPU:1, one launch (start us, length us, event | category | flops | bytes accessed | tf_op | source)
XLA Modules:
  0.0 623.4 jit_solution(1070797298833924869)
XLA Ops:
  2.0 17.9 %shard_map.77 = bf16[16,16,1536]{2,1,0:T(8,128)(2,1)} custom-call(bf16[1,16,1536]{2,1,0:T(8,128)(2,1)} %reshape_transpose.3.refs_0_), custom_call_target="tpu_custom_call" | custom-call | tf_op jit(solution)/shard_map/pallas_call | solution.py:96
  32.2 17.1 %shard_map.78 = bf16[16,16,1536]{2,1,0:T(8,128)(2,1)} custom-call(bf16[16,16,1536]{2,1,0:T(8,128)(2,1)} %convert_element_type.373.refs_0_), custom_call_target="tpu_custom_call" | custom-call | tf_op jit(solution)/shard_map/pallas_call | solution.py:96
  59.5 14.1 %shard_map.79 = bf16[16,16,1536]{2,1,0:T(8,128)(2,1)} custom-call(bf16[1,16,1536]{2,1,0:T(8,128)(2,1)} %reshape_broadcast_in_dim.18.refs_0_), custom_call_target="tpu_custom_call" | custom-call | tf_op jit(solution)/shard_map/pallas_call | solution.py:96
  85.9 16.1 %shard_map.80 = bf16[16,16,1536]{2,1,0:T(8,128)(2,1)} custom-call(bf16[16,16,1536]{2,1,0:T(8,128)(2,1)} %convert_element_type.383.refs_0_), custom_call_target="tpu_custom_call" | custom-call | tf_op jit(solution)/shard_map/pallas_call | solution.py:96
  113.8 14.1 %shard_map.81 = bf16[16,16,1536]{2,1,0:T(8,128)(2,1)} custom-call(bf16[1,16,1536]{2,1,0:T(8,128)(2,1)} %reshape_broadcast_in_dim.19.refs_0_), custom_call_target="tpu_custom_call" | custom-call | tf_op jit(solution)/shard_map/pallas_call | solution.py:96
  140.8 16.3 %shard_map.82 = bf16[16,16,1536]{2,1,0:T(8,128)(2,1)} custom-call(bf16[16,16,1536]{2,1,0:T(8,128)(2,1)} %convert_element_type.393.refs_0_), custom_call_target="tpu_custom_call" | custom-call | tf_op jit(solution)/shard_map/pallas_call | solution.py:96
  161.2 18.7 %shard_map.84 = bf16[16,16,1536]{2,1,0:T(8,128)(2,1)} custom-call(bf16[1,16,1536]{2,1,0:T(8,128)(2,1)} %broadcast_select_fusion.refs_0_), custom_call_target="tpu_custom_call" | custom-call | tf_op jit(solution)/shard_map/pallas_call | solution.py:96
  183.0 17.7 %shard_map.83 = bf16[16,16,1536]{2,1,0:T(8,128)(2,1)} custom-call(bf16[1,16,1536]{2,1,0:T(8,128)(2,1)} %reshape_broadcast_in_dim.20.refs_0_), custom_call_target="tpu_custom_call" | custom-call | tf_op jit(solution)/shard_map/pallas_call | solution.py:96
  209.1 7.5 %fusion.63 = bf16[128,3072]{1,0:T(8,128)(2,1)S(1)} fusion(bf16[1,3072,768]{2,1,0:T(8,128)(2,1)} %param.26, bf16[128,3072]{1,0:T(8,128)(2,1)S(1)} %copy-done.8, bf16[1,768,3072]{2,1,0:T(8,128)(2,1)} %param.27, f32[128,768]{1,0:T(8,128)S(1)} %fusion.22), kind=kOutput, calls=%fused_computation.45 | convolution fusion | flops 1210810368 | bytes 11403264 | tf_op jit(solution)/shard_map/dot_general | solution.py:146
  217.8 16.2 %shard_map.85 = bf16[16,16,1536]{2,1,0:T(8,128)(2,1)} custom-call(bf16[16,16,1536]{2,1,0:T(8,128)(2,1)} %convert_element_type.412.refs_0_), custom_call_target="tpu_custom_call" | custom-call | tf_op jit(solution)/shard_map/pallas_call | solution.py:96
  239.0 16.7 %shard_map.86 = bf16[16,16,1536]{2,1,0:T(8,128)(2,1)} custom-call(bf16[1,16,1536]{2,1,0:T(8,128)(2,1)} %reshape_broadcast_in_dim.21.refs_0_), custom_call_target="tpu_custom_call" | custom-call | tf_op jit(solution)/shard_map/pallas_call | solution.py:96
  257.1 7.8 %fusion.60 = bf16[128,3072]{1,0:T(8,128)(2,1)S(1)} fusion(bf16[1,3072,768]{2,1,0:T(8,128)(2,1)} %param.26, bf16[128,3072]{1,0:T(8,128)(2,1)S(1)} %reshape_reshape.13, bf16[1,768,3072]{2,1,0:T(8,128)(2,1)} %param.27, f32[128,768]{1,0:T(8,128)S(1)} %fusion.22), kind=kOutput, calls=%fused_computation.44 | convolution fusion | flops 1210810368 | bytes 11403264 | tf_op jit(solution)/shard_map/dot_general | solution.py:146
  266.0 16.5 %shard_map.87 = bf16[16,16,1536]{2,1,0:T(8,128)(2,1)} custom-call(bf16[16,16,1536]{2,1,0:T(8,128)(2,1)} %convert_element_type.420.refs_0_), custom_call_target="tpu_custom_call" | custom-call | tf_op jit(solution)/shard_map/pallas_call | solution.py:96
  293.3 14.6 %shard_map.88 = bf16[16,16,1536]{2,1,0:T(8,128)(2,1)} custom-call(bf16[1,16,1536]{2,1,0:T(8,128)(2,1)} %reshape_broadcast_in_dim.22.refs_0_), custom_call_target="tpu_custom_call" | custom-call | tf_op jit(solution)/shard_map/pallas_call | solution.py:96
  309.3 7.8 %fusion.57 = bf16[128,3072]{1,0:T(8,128)(2,1)S(1)} fusion(bf16[1,3072,768]{2,1,0:T(8,128)(2,1)} %param.26, bf16[128,3072]{1,0:T(8,128)(2,1)S(1)} %reshape_reshape.14, bf16[1,768,3072]{2,1,0:T(8,128)(2,1)} %param.27, f32[128,768]{1,0:T(8,128)S(1)} %fusion.22), kind=kOutput, calls=%fused_computation.43 | convolution fusion | flops 1210810368 | bytes 11403264 | tf_op jit(solution)/shard_map/dot_general | solution.py:146
  318.2 16.5 %shard_map.89 = bf16[16,16,1536]{2,1,0:T(8,128)(2,1)} custom-call(bf16[16,16,1536]{2,1,0:T(8,128)(2,1)} %convert_element_type.427.refs_0_), custom_call_target="tpu_custom_call" | custom-call | tf_op jit(solution)/shard_map/pallas_call | solution.py:96
  355.0 17.7 %shard_map.90 = bf16[16,16,1536]{2,1,0:T(8,128)(2,1)} custom-call(bf16[1,16,1536]{2,1,0:T(8,128)(2,1)} %reshape_broadcast_in_dim.23.refs_0_), custom_call_target="tpu_custom_call" | custom-call | tf_op jit(solution)/shard_map/pallas_call | solution.py:96
  383.7 9.5 %subtract_convert_fusion.1 = bf16[3072,768]{1,0:T(8,128)(2,1)} fusion(bf16[1,3072,768]{2,1,0:T(8,128)(2,1)} %param.26, f32[128,3072]{1,0:T(8,128)S(1)} %copy-done.7, f32[128]{0:T(128)S(1)} %copy-done.24, bf16[128,3072]{1,0:T(8,128)(2,1)S(1)} %select_n.268, bf16[1,768,3072]{2,1,0:T(8,128)(2,1)} %param.27, f32[128,768]{1,0:T(8,128)S(1)} %fusion.22), kind=kOutput, calls=%fused_computation.3 | convolution fusion | flops 1220247552 | bytes 16908800 | tf_op jit(solution)/shard_map/dot_general | solution.py:180
  393.2 213.9 %conditional.1 = (bf16[3072,768]{1,0:T(8,128)(2,1)}, bf16[768,3072]{1,0:T(8,128)(2,1)}) conditional(s32[]{:T(128)} %clamp.3, () %tuple.72, (bf16[3072,768]{1,0:T(8,128)(2,1)}, bf16[768,3072]{1,0:T(8,128)(2,1)}) %tuple.73, (bf16[3072,768]{1,0:T(8,128)(2,1)}, bf16[768,3072]{1,0:T(8,128)(2,1)}) %tuple.73, ...), branch_computations={%region_27.28_spmd, %region_28.29_spmd, %region_29.30_spmd, %regio... | conditional | bytes 37748832 | solution.py:273
  393.2 9.0 %collective-permute-start.20 = (bf16[3072,768]{1,0:T(8,128)(2,1)}, bf16[3072,768]{1,0:T(8,128)(2,1)}, u32[]{:S(2)}, u32[]{:S(2)}) collective-permute-start(bf16[3072,768]{1,0:T(8,128)(2,1)} %get-tuple-element.80), channel_id=1, source_target_pairs={{0,16},{16,0},{32,48},{48,32},{96,112},{112,96},{1,17},{17,1},{33,... | collective-permute-start | bytes 14155784 | tf_op jit(solution)/shard_map/cond/branch_11_fun/ppermute | solution.py:201
  402.3 11.7 %collective-permute-start.21 = (bf16[768,3072]{1,0:T(8,128)(2,1)}, bf16[768,3072]{1,0:T(8,128)(2,1)}, u32[]{:S(2)}, u32[]{:S(2)}) collective-permute-start(bf16[768,3072]{1,0:T(8,128)(2,1)} %get-tuple-element.81), channel_id=1, source_target_pairs={{0,16},{16,0},{32,48},{48,32},{96,112},{112,96},{1,17},{17,1},{33,... | collective-permute-start | bytes 14155784 | tf_op jit(solution)/shard_map/cond/branch_11_fun/ppermute | solution.py:201
  414.0 91.9 %collective-permute-done.20 = bf16[3072,768]{1,0:T(8,128)(2,1)} collective-permute-done((bf16[3072,768]{1,0:T(8,128)(2,1)}, bf16[3072,768]{1,0:T(8,128)(2,1)}, u32[]{:S(2)}, u32[]{:S(2)}) %collective-permute-start.20) | collective-permute-done | bytes 4718624 | tf_op jit(solution)/shard_map/cond/branch_11_fun/ppermute | solution.py:201
  505.8 101.1 %collective-permute-done.21 = bf16[768,3072]{1,0:T(8,128)(2,1)} collective-permute-done((bf16[768,3072]{1,0:T(8,128)(2,1)}, bf16[768,3072]{1,0:T(8,128)(2,1)}, u32[]{:S(2)}, u32[]{:S(2)}) %collective-permute-start.21) | collective-permute-done | bytes 4718624 | tf_op jit(solution)/shard_map/cond/branch_11_fun/ppermute | solution.py:201
  607.1 9.5 %fusion = bf16[1,3072,768]{2,1,0:T(8,128)(2,1)} fusion(bf16[3072,768]{1,0:T(8,128)(2,1)} %subtract_convert_fusion.1, bf16[3072,768]{1,0:T(8,128)(2,1)} %get-tuple-element.94, pred[]{:T(512)S(6)} %ne.7), kind=kLoop, calls=%fused_computation.4 | loop fusion | flops 14155776 | bytes 14155777 | tf_op jit(solution)/shard_map/broadcast_in_dim | solution.py:290
  (247 shorter events, 134.1 us)
Async XLA Ops:
  50.7 7.9 %collective-permute-start.31 = (bf16[1,2,4,3072]{3,2,1,0:T(4,128)(2,1)S(1)}, bf16[1,2,4,3072]{3,2,1,0:T(4,128)(2,1)S(1)}, u32[]{:S(2)}, u32[]{:S(2)}) collective-permute-start(bf16[1,2,4,3072]{3,2,1,0:T(4,128)(2,1)S(1)} %add_convert_fusion.2), channel_id=1, source_target_pairs={{0,48},{16,32},{1,49},{17,33},{2,50},{18,34},{3,51},{19,35},{4,52}... | collective-permute-start | bytes 147464 | tf_op jit(solution)/shard_map/ppermute | solution.py:189
  52.0 6.6 %collective-permute-start.30 = (bf16[1,2,4,3072]{3,2,1,0:T(4,128)(2,1)S(1)}, bf16[1,2,4,3072]{3,2,1,0:T(4,128)(2,1)S(1)}, u32[]{:S(2)}, u32[]{:S(2)}) collective-permute-start(bf16[1,2,4,3072]{3,2,1,0:T(4,128)(2,1)S(1)} %add_convert_fusion.2), channel_id=1, source_target_pairs={{0,32},{16,48},{1,33},{17,49},{2,34},{18,50},{3,35},{19,51},{4,36}... | collective-permute-start | bytes 147464 | tf_op jit(solution)/shard_map/ppermute | solution.py:189
  79.1 33.0 %copy-start.15 = (bf16[2,4,1,3072]{3,1,2,0:T(4,128)(2,1)S(1)}, bf16[2,4,1,3072]{3,1,2,0:T(4,128)(2,1)}, u32[]{:S(2)}) copy-start(bf16[2,4,1,3072]{3,1,2,0:T(4,128)(2,1)} %param.24) | copy-start | bytes 147460
  103.4 8.7 %collective-permute-start.33 = (bf16[1,2,4,3072]{3,2,1,0:T(4,128)(2,1)S(1)}, bf16[1,2,4,3072]{3,2,1,0:T(4,128)(2,1)S(1)}, u32[]{:S(2)}, u32[]{:S(2)}) collective-permute-start(bf16[1,2,4,3072]{3,2,1,0:T(4,128)(2,1)S(1)} %add_convert_fusion.1), channel_id=1, source_target_pairs={{32,80},{48,64},{33,81},{49,65},{34,82},{50,66},{35,83},{51,67},{3... | collective-permute-start | bytes 147464 | tf_op jit(solution)/shard_map/ppermute | solution.py:189
  110.3 2.6 collective-permute-start.32
  139.7 63.8 %copy-start.1 = (bf16[16,16,1536]{2,1,0:T(8,128)(2,1)S(1)}, bf16[16,16,1536]{2,1,0:T(8,128)(2,1)}, u32[]{:S(2)}) copy-start(bf16[16,16,1536]{2,1,0:T(8,128)(2,1)} %shard_map.77) | copy-start | bytes 2359300
  139.7 63.8 %copy-start.2 = (bf16[16,16,1536]{2,1,0:T(8,128)(2,1)S(1)}, bf16[16,16,1536]{2,1,0:T(8,128)(2,1)}, u32[]{:S(2)}) copy-start(bf16[16,16,1536]{2,1,0:T(8,128)(2,1)} %shard_map.79) | copy-start | bytes 2359300
  139.7 63.8 %copy-start.3 = (bf16[16,16,1536]{2,1,0:T(8,128)(2,1)S(1)}, bf16[16,16,1536]{2,1,0:T(8,128)(2,1)}, u32[]{:S(2)}) copy-start(bf16[16,16,1536]{2,1,0:T(8,128)(2,1)} %shard_map.81) | copy-start | bytes 2359300
  159.2 22.8 %collective-permute-start.35 = (bf16[1,2,4,3072]{3,2,1,0:T(4,128)(2,1)S(1)}, bf16[1,2,4,3072]{3,2,1,0:T(4,128)(2,1)S(1)}, u32[]{:S(2)}, u32[]{:S(2)}) collective-permute-start(bf16[1,2,4,3072]{3,2,1,0:T(4,128)(2,1)S(1)} %add_convert_fusion), channel_id=1, source_target_pairs={{64,112},{80,96},{65,113},{81,97},{66,114},{82,98},{67,115},{83,99... | collective-permute-start | bytes 147464 | tf_op jit(solution)/shard_map/ppermute | solution.py:189
  159.9 22.1 %collective-permute-start.34 = (bf16[1,2,4,3072]{3,2,1,0:T(4,128)(2,1)S(1)}, bf16[1,2,4,3072]{3,2,1,0:T(4,128)(2,1)S(1)}, u32[]{:S(2)}, u32[]{:S(2)}) collective-permute-start(bf16[1,2,4,3072]{3,2,1,0:T(4,128)(2,1)S(1)} %add_convert_fusion), channel_id=1, source_target_pairs={{64,96},{80,112},{65,97},{81,113},{66,98},{82,114},{67,99},{83,115... | collective-permute-start | bytes 147464 | tf_op jit(solution)/shard_map/ppermute | solution.py:189
  236.3 47.7 %copy-start.12 = (bf16[1,2,4,3072]{3,2,1,0:T(4,128)(2,1)}, bf16[1,2,4,3072]{3,2,1,0:T(4,128)(2,1)S(1)}, u32[]{:S(2)}) copy-start(bf16[1,2,4,3072]{3,2,1,0:T(4,128)(2,1)S(1)} %get-tuple-element.97) | copy-start | bytes 147460
  236.5 1.6 collective-permute-start.37
  237.1 0.9 collective-permute-start.36
  284.1 6.6 %collective-permute-start.39 = (bf16[1,2,4,3072]{3,2,1,0:T(4,128)(2,1)S(1)}, bf16[1,2,4,3072]{3,2,1,0:T(4,128)(2,1)S(1)}, u32[]{:S(2)}, u32[]{:S(2)}) collective-permute-start(bf16[1,2,4,3072]{3,2,1,0:T(4,128)(2,1)S(1)} %fusion.191), channel_id=1, source_target_pairs={{64,48},{80,32},{65,49},{81,33},{66,50},{82,34},{67,51},{83,35},{6... | collective-permute-start | bytes 147464 | tf_op jit(solution)/shard_map/ppermute | solution.py:189
  285.4 6.9 %collective-permute-start.38 = (bf16[1,2,4,3072]{3,2,1,0:T(4,128)(2,1)S(1)}, bf16[1,2,4,3072]{3,2,1,0:T(4,128)(2,1)S(1)}, u32[]{:S(2)}, u32[]{:S(2)}) collective-permute-start(bf16[1,2,4,3072]{3,2,1,0:T(4,128)(2,1)S(1)} %fusion.191), channel_id=1, source_target_pairs={{64,32},{80,48},{65,33},{81,49},{66,34},{82,50},{67,35},{83,51},{6... | collective-permute-start | bytes 147464 | tf_op jit(solution)/shard_map/ppermute | solution.py:189
  309.3 31.5 %copy-start.21 = (f32[2,4]{1,0:T(2,128)S(1)}, f32[2,4]{1,0:T(2,128)}, u32[]{:S(2)}) copy-start(f32[2,4]{1,0:T(2,128)} %fusion.218) | copy-start | bytes 100
  317.1 35.7 %copy-start.25 = (bf16[2,4,2,4]{3,2,1,0:T(2,128)(2,1)S(1)}, bf16[2,4,2,4]{3,2,1,0:T(2,128)(2,1)}, u32[]{:S(2)}) copy-start(bf16[2,4,2,4]{3,2,1,0:T(2,128)(2,1)} %get-tuple-element.127) | copy-start | bytes 388
  318.2 56.7 %copy-start.4 = (bf16[16,16,1536]{2,1,0:T(8,128)(2,1)S(1)}, bf16[16,16,1536]{2,1,0:T(8,128)(2,1)}, u32[]{:S(2)}) copy-start(bf16[16,16,1536]{2,1,0:T(8,128)(2,1)} %shard_map.84) | copy-start | bytes 2359300
  318.2 56.7 %copy-start.5 = (bf16[16,16,1536]{2,1,0:T(8,128)(2,1)S(1)}, bf16[16,16,1536]{2,1,0:T(8,128)(2,1)}, u32[]{:S(2)}) copy-start(bf16[16,16,1536]{2,1,0:T(8,128)(2,1)} %shard_map.86) | copy-start | bytes 2359300
  318.2 56.7 %copy-start.6 = (bf16[16,16,1536]{2,1,0:T(8,128)(2,1)S(1)}, bf16[16,16,1536]{2,1,0:T(8,128)(2,1)}, u32[]{:S(2)}) copy-start(bf16[16,16,1536]{2,1,0:T(8,128)(2,1)} %shard_map.88) | copy-start | bytes 2359300
  342.5 9.3 %collective-permute-start.41 = (bf16[1,2,4,3072]{3,2,1,0:T(4,128)(2,1)}, bf16[1,2,4,3072]{3,2,1,0:T(4,128)(2,1)}, u32[]{:S(2)}, u32[]{:S(2)}) collective-permute-start(bf16[1,2,4,3072]{3,2,1,0:T(4,128)(2,1)} %fusion.190), channel_id=1, source_target_pairs={{32,16},{48,0},{33,17},{49,1},{34,18},{50,2},{35,19},{51,3},{36,20... | collective-permute-start | bytes 147464 | tf_op jit(solution)/shard_map/ppermute | solution.py:189
  345.6 6.2 collective-permute-start.40
  393.2 112.6 %collective-permute-start.20 = (bf16[3072,768]{1,0:T(8,128)(2,1)}, bf16[3072,768]{1,0:T(8,128)(2,1)}, u32[]{:S(2)}, u32[]{:S(2)}) collective-permute-start(bf16[3072,768]{1,0:T(8,128)(2,1)} %get-tuple-element.80), channel_id=1, source_target_pairs={{0,16},{16,0},{32,48},{48,32},{96,112},{112,96},{1,17},{17,1},{33,... | collective-permute-start | bytes 14155784 | tf_op jit(solution)/shard_map/cond/branch_11_fun/ppermute | solution.py:201
  402.3 204.7 %collective-permute-start.21 = (bf16[768,3072]{1,0:T(8,128)(2,1)}, bf16[768,3072]{1,0:T(8,128)(2,1)}, u32[]{:S(2)}, u32[]{:S(2)}) collective-permute-start(bf16[768,3072]{1,0:T(8,128)(2,1)} %get-tuple-element.81), channel_id=1, source_target_pairs={{0,16},{16,0},{32,48},{48,32},{96,112},{112,96},{1,17},{17,1},{33,... | collective-permute-start | bytes 14155784 | tf_op jit(solution)/shard_map/cond/branch_11_fun/ppermute | solution.py:201
  (19 other events, 286.2 us)

commit v6 on v5

--- a/solution.py
+++ b/solution.py
@@ -54,8 +54,19 @@
     return (widened, inverse, normed, preact)
 
 
-def plane_kernel(count, spread, x_ref, out_ref, held, send_sem, recv_sem):
+def plane_kernel(count, spread, active, x_ref, out_ref, held, send_sem, recv_sem):
     section = lax.axis_index("section")
+
+    @pl.when(section == active)
+    def _():
+        plane_exchange(count, spread, section, x_ref, out_ref, held, send_sem, recv_sem)
+
+    @pl.when(section != active)
+    def _():
+        out_ref[...] = jnp.zeros_like(out_ref)
+
+
+def plane_exchange(count, spread, section, x_ref, out_ref, held, send_sem, recv_sem):
     half = lax.axis_index("half")
     me = lax.axis_index("plane")
     barrier = pltpu.get_barrier_semaphore()
@@ -85,16 +96,16 @@
     out_ref[me] = own
 
 
-def plane_call(value, count, spread, ident):
+def plane_call(value, count, spread, ident, active):
     lanes = value[0].size // 16
-    dense = plane_dense(value.reshape(value.shape[0], 16, lanes), count, spread, ident)
+    dense = plane_dense(value.reshape(value.shape[0], 16, lanes), count, spread, ident, active)
     return dense.reshape((count,) + value.shape[1:])
 
 
-def plane_dense(value, count, spread, ident):
+def plane_dense(value, count, spread, ident, active):
     shape = (count,) + value.shape[1:]
     return pl.pallas_call(
-        lambda *refs: plane_kernel(count, spread, *refs),
+        lambda *refs: plane_kernel(count, spread, active, *refs),
         out_shape=jax.ShapeDtypeStruct(shape, value.dtype),
         in_specs=[pl.BlockSpec(memory_space=pltpu.VMEM)],
         out_specs=pl.BlockSpec(memory_space=pltpu.VMEM),
@@ -107,12 +118,12 @@
     )(value)
 
 
-def gather_rows(piece):
-    return plane_call(piece, lax.axis_size("plane"), True, 1)
-
-
-def sum_rows(partial_value):
-    parts = plane_call(partial_value.astype(jnp.bfloat16), lax.axis_size("plane"), False, 0)
+def gather_rows(piece, active):
+    return plane_call(piece, lax.axis_size("plane"), True, 4 + active, active)
+
+
+def sum_rows(partial_value, active):
+    parts = plane_call(partial_value.astype(jnp.bfloat16), lax.axis_size("plane"), False, active, active)
     return jnp.sum(parts.astype(jnp.float32), axis=0, keepdims=True)
 
 
@@ -120,17 +131,19 @@
     return lax.dynamic_slice_in_dim(full, shard_idx, 1, axis=0)
 
 
-def forward_piece(x_full, weight_in, weight_out, scale_in, scale_out, shard_idx):
+def forward_piece(x_full, weight_in, weight_out, scale_in, scale_out, shard_idx, active):
     shape = x_full.shape
     widened, inverse, normed, preact = layer_front(x_full.reshape(-1, shape[-1]), weight_in, scale_in)
     gelu_val, slopes = gelu_parts(preact)
     activated = gelu_val.astype(jnp.bfloat16)
     partial_value = jnp.dot(activated, weight_out, preferred_element_type=jnp.float32) * scale_out
-    summed = sum_rows(partial_value.reshape(shape))
+    summed = sum_rows(partial_value.reshape(shape), active)
     return (own_rows(x_full, shard_idx).astype(jnp.float32) + summed).astype(jnp.bfloat16)
 
 
-def backward_piece(x_full, up_full, up_piece, weight_in, weight_out, scale_in, scale_out, shard_idx):
+def backward_piece(
+    x_full, up_full, up_piece, weight_in, weight_out, scale_in, scale_out, shard_idx, active
+):
     shape = x_full.shape
     widened, inverse, normed, preact = layer_front(x_full.reshape(-1, shape[-1]), weight_in, scale_in)
     gelu_val, slopes = gelu_parts(preact)
@@ -146,7 +159,7 @@
         lax.dot_general(d_pre, weight_in, (((1,), (1,)), ((), ())), preferred_element_type=jnp.float32)
         * scale_in
     )
-    normed_piece = sum_rows(d_normed.reshape(shape))
+    normed_piece = sum_rows(d_normed.reshape(shape), active)
     wide_piece = own_rows(x_full, shard_idx).astype(jnp.float32)
     inv_piece = own_rows(inverse.reshape(shape[:-1] + (1,)), shard_idx)
     grad_piece = (
@@ -224,10 +237,10 @@
         ],
         axis=1,
     ).transpose(2, 0, 1, 3)
-    x_cur = gather_rows(opening)
+    x_cur = gather_rows(opening, 0)
     x_keep = x_cur
     for bound in range(section_count - 1):
-        piece = forward_piece(x_cur, weight_in, weight_out, scale_in, scale_out, shard_idx)
+        piece = forward_piece(x_cur, weight_in, weight_out, scale_in, scale_out, shard_idx, bound)
         straight, crossed = cross_boundary(piece, bound, bound + 1, replicas)
         sources = jnp.stack(
             [jnp.where(replica == h, straight, crossed) for h in range(replicas)]
@@ -237,18 +250,18 @@
             "mqjk,qmjd->mkd", mine.astype(jnp.bfloat16), sources,
             preferred_element_type=jnp.float32,
         ).astype(jnp.bfloat16)[None]
-        x_cur = gather_rows(routed)
+        x_cur = gather_rows(routed, bound + 1)
         x_keep = jnp.where(my_section == bound + 1, x_cur, x_keep)
 
     last_live = lax.dynamic_index_in_dim(live_list[section_count - 1], replica, 1, keepdims=False)
     up_piece = jnp.where(
         last_live[None, :, :, None], cotangent.transpose(2, 0, 1, 3), jnp.zeros((), jnp.bfloat16)
     )
-    up_full = gather_rows(up_piece)
+    up_full = gather_rows(up_piece, section_count - 1)
     up_keep = up_full
     for depth in reversed(range(1, section_count)):
         grad_piece = backward_piece(
-            x_keep, up_full, up_piece, weight_in, weight_out, scale_in, scale_out, shard_idx
+            x_keep, up_full, up_piece, weight_in, weight_out, scale_in, scale_out, shard_idx, depth
         )
         straight, crossed = cross_boundary(grad_piece, depth, depth - 1, replicas)
         sources = jnp.stack(
@@ -259,7 +272,7 @@
             "mjdk,dmkD->mjD", mine.astype(jnp.bfloat16), sources,
             preferred_element_type=jnp.float32,
         ).astype(jnp.bfloat16)[None]
-        up_full = gather_rows(up_piece)
+        up_full = gather_rows(up_piece, depth - 1)
         up_keep = jnp.where(my_section == depth - 1, up_full, up_keep)
 
     accum_in, accum_out = weight_grads(x_keep, up_keep, weight_in, weight_out, scale_in, scale_out)

time: 633 us -> 589 us (0.930)
  the two profiles are of different devices: /device:TPU:1 before, /device:TPU:16 now
where the time goes in v6:
time: 589 us; the launch traced here: 578 us
  waiting for transfers between devices  246 us (42%)
  Pallas kernels  116 us (20%)
  starting transfers between devices  64.9 us (11%)
  matrix products  61 us (10%)
  other arithmetic  44 us (7%)
  local copies, waits for them, and re-layouts  41.5 us (7%)
    pallas_call x14, Pallas kernels, plane_dense(): pl.pallas_call(lambda *refs: plane_kernel(count, spread, active, *refs),...  116 us
    ppermute x1, waiting for transfers between devices, swap_sections(): lax.ppermute(stepped_out, PAIR, pairs)  101 us
    ppermute x1, waiting for transfers between devices, swap_sections(): lax.ppermute(stepped_in, PAIR, pairs)  95.2 us
    ppermute x6, waiting for transfers between devices, cross_boundary(): lax.ppermute(piece, PAIR, crossed)  47.1 us
    ppermute x1, starting transfers between devices, swap_sections(): lax.ppermute(stepped_in, PAIR, pairs)  41.8 us
    dot_general x3, matrix products, backward_piece(): lax.dot_general(d_pre, weight_in, (((1,), (1,)), ((), ())), preferred_ele...  23 us
    dot_general x3, matrix products, forward_piece(): jnp.dot(activated, weight_out, preferred_element_type=jnp.float32)  17 us
    broadcast_in_dim x2, other arithmetic, on_device(): return (new_in[None], new_out[None])  16.1 us
  transfers between devices with their start and end apart: 14, of which 6 were waited for; matrix products, arithmetic and copies ran while one was open for 2% of the time, Pallas kernels for 0%

profile of v6, /device:TPU:16, one launch (start us, length us, event | category | flops | bytes accessed | tf_op | source)
XLA Modules:
  0.0 577.5 jit_solution(375606762217257934)
XLA Ops:
  9.5 5.7 fusion.54
  16.3 22.3 %shard_map.78 = bf16[16,16,1536]{2,1,0:T(8,128)(2,1)} custom-call(bf16[16,16,1536]{2,1,0:T(8,128)(2,1)} %convert_element_type.373.refs_0_), custom_call_target="tpu_custom_call" | custom-call | tf_op jit(solution)/shard_map/pallas_call | solution.py:107
  53.3 5.7 fusion.51
  66.6 34.0 %collective-permute-done.33 = bf16[1,2,4,3072]{3,2,1,0:T(4,128)(2,1)S(1)} collective-permute-done((bf16[1,2,4,3072]{3,2,1,0:T(4,128)(2,1)S(1)}, bf16[1,2,4,3072]{3,2,1,0:T(4,128)(2,1)S(1)}, u32[]{:S(2)}, u32[]{:S(2)}) %collective-permute-start.33) | collective-permute-done | bytes 49184 | tf_op jit(solution)/shard_map/ppermute | solution.py:202
  103.7 14.2 %shard_map.81 = bf16[16,16,1536]{2,1,0:T(8,128)(2,1)} custom-call(bf16[1,16,1536]{2,1,0:T(8,128)(2,1)} %reshape_broadcast_in_dim.19.refs_0_), custom_call_target="tpu_custom_call" | custom-call | tf_op jit(solution)/shard_map/pallas_call | solution.py:107
  124.0 5.7 fusion.48
  130.9 14.6 %shard_map.82 = bf16[16,16,1536]{2,1,0:T(8,128)(2,1)} custom-call(bf16[16,16,1536]{2,1,0:T(8,128)(2,1)} %convert_element_type.393.refs_0_), custom_call_target="tpu_custom_call" | custom-call | tf_op jit(solution)/shard_map/pallas_call | solution.py:107
  163.2 3.1 fusion.22
  166.4 7.5 %fusion.63 = bf16[128,3072]{1,0:T(8,128)(2,1)S(1)} fusion(bf16[1,3072,768]{2,1,0:T(8,128)(2,1)} %param.26, bf16[128,3072]{1,0:T(8,128)(2,1)S(1)} %copy-done.8, bf16[1,768,3072]{2,1,0:T(8,128)(2,1)} %param.27, f32[128,768]{1,0:T(8,128)S(1)} %fusion.22), kind=kOutput, calls=%fused_computation.45 | convolution fusion | flops 1210810368 | bytes 11403264 | tf_op jit(solution)/shard_map/dot_general | solution.py:159
  175.0 19.3 %shard_map.85 = bf16[16,16,1536]{2,1,0:T(8,128)(2,1)} custom-call(bf16[16,16,1536]{2,1,0:T(8,128)(2,1)} %convert_element_type.412.refs_0_), custom_call_target="tpu_custom_call" | custom-call | tf_op jit(solution)/shard_map/pallas_call | solution.py:107
  199.5 13.1 %collective-permute-done.37 = bf16[1,2,4,3072]{3,2,1,0:T(4,128)(2,1)S(1)} collective-permute-done((bf16[1,2,4,3072]{3,2,1,0:T(4,128)(2,1)S(1)}, bf16[1,2,4,3072]{3,2,1,0:T(4,128)(2,1)S(1)}, u32[]{:S(2)}, u32[]{:S(2)}) %collective-permute-start.37) | collective-permute-done | bytes 49184 | tf_op jit(solution)/shard_map/ppermute | solution.py:202
  213.5 14.0 %shard_map.86 = bf16[16,16,1536]{2,1,0:T(8,128)(2,1)} custom-call(bf16[1,16,1536]{2,1,0:T(8,128)(2,1)} %reshape_broadcast_in_dim.21.refs_0_), custom_call_target="tpu_custom_call" | custom-call | tf_op jit(solution)/shard_map/pallas_call | solution.py:107
  228.9 7.8 %fusion.60 = bf16[128,3072]{1,0:T(8,128)(2,1)S(1)} fusion(bf16[1,3072,768]{2,1,0:T(8,128)(2,1)} %param.26, bf16[128,3072]{1,0:T(8,128)(2,1)S(1)} %reshape_reshape.13, bf16[1,768,3072]{2,1,0:T(8,128)(2,1)} %param.27, f32[128,768]{1,0:T(8,128)S(1)} %fusion.22), kind=kOutput, calls=%fused_computation.44 | convolution fusion | flops 1210810368 | bytes 11403264 | tf_op jit(solution)/shard_map/dot_general | solution.py:159
  237.8 14.5 %shard_map.87 = bf16[16,16,1536]{2,1,0:T(8,128)(2,1)} custom-call(bf16[16,16,1536]{2,1,0:T(8,128)(2,1)} %convert_element_type.420.refs_0_), custom_call_target="tpu_custom_call" | custom-call | tf_op jit(solution)/shard_map/pallas_call | solution.py:107
  262.6 7.8 %fusion.57 = bf16[128,3072]{1,0:T(8,128)(2,1)S(1)} fusion(bf16[1,3072,768]{2,1,0:T(8,128)(2,1)} %param.26, bf16[128,3072]{1,0:T(8,128)(2,1)S(1)} %reshape_reshape.14, bf16[1,768,3072]{2,1,0:T(8,128)(2,1)} %param.27, f32[128,768]{1,0:T(8,128)S(1)} %fusion.22), kind=kOutput, calls=%fused_computation.43 | convolution fusion | flops 1210810368 | bytes 11403264 | tf_op jit(solution)/shard_map/dot_general | solution.py:159
  298.3 6.3 %subtract_convert_fusion = bf16[768,3072]{1,0:T(8,128)(2,1)} fusion(bf16[1,768,3072]{2,1,0:T(8,128)(2,1)} %param.27, bf16[128,3072]{1,0:T(8,128)(2,1)} %reshape.403, bf16[128,3072]{1,0:T(8,128)(2,1)} %copy-done.11, bf16[128,3072]{1,0:T(8,128)(2,1)} %copy-done.10, bf16[128,3072]{1,0:T(8,128)(2,1)S(1)} %copy-done.9, pred[]{:T(512)S(6)} %eq.192, pred[]{:T(512)S(6)} %eq.193, ...), kind=kOutput, calls=%fused_computation.2 | convolution fusion | flops 615579648 | bytes 12976131 | tf_op jit(solution)/shard_map/dot_general | solution.py:184
  304.7 9.5 %subtract_convert_fusion.1 = bf16[3072,768]{1,0:T(8,128)(2,1)} fusion(bf16[1,3072,768]{2,1,0:T(8,128)(2,1)} %param.26, f32[128,3072]{1,0:T(8,128)S(1)} %copy-done.7, f32[128]{0:T(128)S(1)} %copy-done.24, bf16[128,3072]{1,0:T(8,128)(2,1)S(1)} %select_n.268, bf16[1,768,3072]{2,1,0:T(8,128)(2,1)} %param.27, f32[128,768]{1,0:T(8,128)S(1)} %fusion.22), kind=kOutput, calls=%fused_computation.3 | convolution fusion | flops 1220247552 | bytes 16908800 | tf_op jit(solution)/shard_map/dot_general | solution.py:193
  314.2 247.1 %conditional.1 = (bf16[3072,768]{1,0:T(8,128)(2,1)}, bf16[768,3072]{1,0:T(8,128)(2,1)}) conditional(s32[]{:T(128)} %clamp.3, () %tuple.72, (bf16[3072,768]{1,0:T(8,128)(2,1)}, bf16[768,3072]{1,0:T(8,128)(2,1)}) %tuple.73, (bf16[3072,768]{1,0:T(8,128)(2,1)}, bf16[768,3072]{1,0:T(8,128)(2,1)}) %tuple.73, ...), branch_computations={%region_27.28_spmd, %region_28.29_spmd, %region_29.30_spmd, %regio... | conditional | bytes 37748832 | solution.py:286
  314.2 41.8 %collective-permute-start.28 = (bf16[3072,768]{1,0:T(8,128)(2,1)}, bf16[3072,768]{1,0:T(8,128)(2,1)}, u32[]{:S(2)}, u32[]{:S(2)}) collective-permute-start(bf16[3072,768]{1,0:T(8,128)(2,1)} %get-tuple-element.88), channel_id=1, source_target_pairs={{0,16},{16,0},{32,48},{48,32},{64,80},{80,64},{96,112},{112,96},{1... | collective-permute-start | bytes 14155784 | tf_op jit(solution)/shard_map/cond/branch_15_fun/ppermute | solution.py:214
  356.1 8.9 %collective-permute-start.29 = (bf16[768,3072]{1,0:T(8,128)(2,1)}, bf16[768,3072]{1,0:T(8,128)(2,1)}, u32[]{:S(2)}, u32[]{:S(2)}) collective-permute-start(bf16[768,3072]{1,0:T(8,128)(2,1)} %get-tuple-element.89), channel_id=1, source_target_pairs={{0,16},{16,0},{32,48},{48,32},{64,80},{80,64},{96,112},{112,96},{1... | collective-permute-start | bytes 14155784 | tf_op jit(solution)/shard_map/cond/branch_15_fun/ppermute | solution.py:214
  364.9 95.2 %collective-permute-done.28 = bf16[3072,768]{1,0:T(8,128)(2,1)} collective-permute-done((bf16[3072,768]{1,0:T(8,128)(2,1)}, bf16[3072,768]{1,0:T(8,128)(2,1)}, u32[]{:S(2)}, u32[]{:S(2)}) %collective-permute-start.28) | collective-permute-done | bytes 4718624 | tf_op jit(solution)/shard_map/cond/branch_15_fun/ppermute | solution.py:214
  460.2 100.6 %collective-permute-done.29 = bf16[768,3072]{1,0:T(8,128)(2,1)} collective-permute-done((bf16[768,3072]{1,0:T(8,128)(2,1)}, bf16[768,3072]{1,0:T(8,128)(2,1)}, u32[]{:S(2)}, u32[]{:S(2)}) %collective-permute-start.29) | collective-permute-done | bytes 4718624 | tf_op jit(solution)/shard_map/cond/branch_15_fun/ppermute | solution.py:214
  561.3 9.5 %fusion = bf16[1,3072,768]{2,1,0:T(8,128)(2,1)} fusion(bf16[3072,768]{1,0:T(8,128)(2,1)} %subtract_convert_fusion.1, bf16[3072,768]{1,0:T(8,128)(2,1)} %get-tuple-element.94, pred[]{:T(512)S(6)} %ne.7), kind=kLoop, calls=%fused_computation.4 | loop fusion | flops 14155776 | bytes 14155777 | tf_op jit(solution)/shard_map/broadcast_in_dim | solution.py:303
  570.7 6.6 %fusion.1 = bf16[1,768,3072]{2,1,0:T(8,128)(2,1)} fusion(bf16[768,3072]{1,0:T(8,128)(2,1)S(1)} %copy-done, bf16[768,3072]{1,0:T(8,128)(2,1)} %get-tuple-element.95, pred[]{:T(512)S(6)} %ne.7), kind=kLoop, calls=%fused_computation.5 | loop fusion | flops 14155776 | bytes 14155777 | tf_op jit(solution)/shard_map/broadcast_in_dim | solution.py:303
  (247 shorter events, 106.2 us)
Async XLA Ops:
  7.4 32.5 %copy-start.13 = (bf16[16,2,4,3072]{3,2,1,0:T(4,128)(2,1)}, bf16[16,2,4,3072]{3,2,1,0:T(4,128)(2,1)S(1)}, u32[]{:S(2)}) copy-start(bf16[16,2,4,3072]{3,2,1,0:T(4,128)(2,1)S(1)} %reshape.399) | copy-start | bytes 2359300
  9.5 31.9 %copy-start.22 = (s32[2,3,2,4]{3,2,1,0:T(2,128)S(1)}, s32[2,3,2,4]{3,2,1,0:T(2,128)}, u32[]{:S(2)}) copy-start(s32[2,3,2,4]{3,2,1,0:T(2,128)} %param.23) | copy-start | bytes 580
  40.0 4.8 collective-permute-start.31
  40.7 4.2 collective-permute-start.30
  63.8 36.8 %collective-permute-start.33 = (bf16[1,2,4,3072]{3,2,1,0:T(4,128)(2,1)S(1)}, bf16[1,2,4,3072]{3,2,1,0:T(4,128)(2,1)S(1)}, u32[]{:S(2)}, u32[]{:S(2)}) collective-permute-start(bf16[1,2,4,3072]{3,2,1,0:T(4,128)(2,1)S(1)} %add_convert_fusion.1), channel_id=1, source_target_pairs={{32,80},{48,64},{33,81},{49,65},{34,82},{50,66},{35,83},{51,67},{3... | collective-permute-start | bytes 147464 | tf_op jit(solution)/shard_map/ppermute | solution.py:202
  65.1 37.6 %collective-permute-start.32 = (bf16[1,2,4,3072]{3,2,1,0:T(4,128)(2,1)S(1)}, bf16[1,2,4,3072]{3,2,1,0:T(4,128)(2,1)S(1)}, u32[]{:S(2)}, u32[]{:S(2)}) collective-permute-start(bf16[1,2,4,3072]{3,2,1,0:T(4,128)(2,1)S(1)} %add_convert_fusion.1), channel_id=1, source_target_pairs={{32,64},{48,80},{33,65},{49,81},{34,66},{50,82},{35,67},{51,83},{3... | collective-permute-start | bytes 147464 | tf_op jit(solution)/shard_map/ppermute | solution.py:202
  66.5 34.1 %copy-start.26 = (pred[2,1,4]{2,0,1:T(4,128)(4,1)}, pred[2,1,4]{2,0,1:T(4,128)(4,1)S(1)}, u32[]{:S(2)}) copy-start(pred[2,1,4]{2,0,1:T(4,128)(4,1)S(1)} %copy.132) | copy-start | bytes 28
  129.7 31.0 %copy-start.1 = (bf16[16,16,1536]{2,1,0:T(8,128)(2,1)S(1)}, bf16[16,16,1536]{2,1,0:T(8,128)(2,1)}, u32[]{:S(2)}) copy-start(bf16[16,16,1536]{2,1,0:T(8,128)(2,1)} %shard_map.77) | copy-start | bytes 2359300
  129.7 31.0 %copy-start.2 = (bf16[16,16,1536]{2,1,0:T(8,128)(2,1)S(1)}, bf16[16,16,1536]{2,1,0:T(8,128)(2,1)}, u32[]{:S(2)}) copy-start(bf16[16,16,1536]{2,1,0:T(8,128)(2,1)} %shard_map.79) | copy-start | bytes 2359300
  129.7 31.0 %copy-start.3 = (bf16[16,16,1536]{2,1,0:T(8,128)(2,1)S(1)}, bf16[16,16,1536]{2,1,0:T(8,128)(2,1)}, u32[]{:S(2)}) copy-start(bf16[16,16,1536]{2,1,0:T(8,128)(2,1)} %shard_map.81) | copy-start | bytes 2359300
  147.6 7.4 %collective-permute-start.35 = (bf16[1,2,4,3072]{3,2,1,0:T(4,128)(2,1)S(1)}, bf16[1,2,4,3072]{3,2,1,0:T(4,128)(2,1)S(1)}, u32[]{:S(2)}, u32[]{:S(2)}) collective-permute-start(bf16[1,2,4,3072]{3,2,1,0:T(4,128)(2,1)S(1)} %add_convert_fusion), channel_id=1, source_target_pairs={{64,112},{80,96},{65,113},{81,97},{66,114},{82,98},{67,115},{83,99... | collective-permute-start | bytes 147464 | tf_op jit(solution)/shard_map/ppermute | solution.py:202
  148.9 6.1 %collective-permute-start.34 = (bf16[1,2,4,3072]{3,2,1,0:T(4,128)(2,1)S(1)}, bf16[1,2,4,3072]{3,2,1,0:T(4,128)(2,1)S(1)}, u32[]{:S(2)}, u32[]{:S(2)}) collective-permute-start(bf16[1,2,4,3072]{3,2,1,0:T(4,128)(2,1)S(1)} %add_convert_fusion), channel_id=1, source_target_pairs={{64,96},{80,112},{65,97},{81,113},{66,98},{82,114},{67,99},{83,115... | collective-permute-start | bytes 147464 | tf_op jit(solution)/shard_map/ppermute | solution.py:202
  166.3 30.4 %copy-start.16 = (bf16[2,4,1,3072]{3,1,2,0:T(4,128)(2,1)S(1)}, bf16[2,4,1,3072]{3,1,2,0:T(4,128)(2,1)}, u32[]{:S(2)}) copy-start(bf16[2,4,1,3072]{3,1,2,0:T(4,128)(2,1)} %param.24) | copy-start | bytes 147460
  166.3 30.3 %copy-start.20 = (f32[2,4]{1,0:T(2,128)S(1)}, f32[2,4]{1,0:T(2,128)}, u32[]{:S(2)}) copy-start(f32[2,4]{1,0:T(2,128)} %fusion.218) | copy-start | bytes 100
  166.3 30.3 %copy-start.27 = (pred[2,1,4]{2,0,1:T(4,128)(4,1)S(1)}, pred[2,1,4]{2,0,1:T(4,128)(4,1)}, u32[]{:S(2)}) copy-start(pred[2,1,4]{2,0,1:T(4,128)(4,1)} %copy-done.26) | copy-start | bytes 28
  196.7 57.2 %copy-start.12 = (bf16[1,2,4,3072]{3,2,1,0:T(4,128)(2,1)}, bf16[1,2,4,3072]{3,2,1,0:T(4,128)(2,1)S(1)}, u32[]{:S(2)}) copy-start(bf16[1,2,4,3072]{3,2,1,0:T(4,128)(2,1)S(1)} %get-tuple-element.97) | copy-start | bytes 147460
  196.8 15.7 %collective-permute-start.37 = (bf16[1,2,4,3072]{3,2,1,0:T(4,128)(2,1)S(1)}, bf16[1,2,4,3072]{3,2,1,0:T(4,128)(2,1)S(1)}, u32[]{:S(2)}, u32[]{:S(2)}) collective-permute-start(bf16[1,2,4,3072]{3,2,1,0:T(4,128)(2,1)S(1)} %subtract_convert_fusion.2), channel_id=1, source_target_pairs={{96,80},{112,64},{97,81},{113,65},{98,82},{114,66},{99,83},{115,67... | collective-permute-start | bytes 147464 | tf_op jit(solution)/shard_map/ppermute | solution.py:202
  198.1 14.4 %collective-permute-start.36 = (bf16[1,2,4,3072]{3,2,1,0:T(4,128)(2,1)S(1)}, bf16[1,2,4,3072]{3,2,1,0:T(4,128)(2,1)S(1)}, u32[]{:S(2)}, u32[]{:S(2)}) collective-permute-start(bf16[1,2,4,3072]{3,2,1,0:T(4,128)(2,1)S(1)} %subtract_convert_fusion.2), channel_id=1, source_target_pairs={{96,64},{112,80},{97,65},{113,81},{98,66},{114,82},{99,67},{115,83... | collective-permute-start | bytes 147464 | tf_op jit(solution)/shard_map/ppermute | solution.py:202
  254.0 3.2 collective-permute-start.39
  255.3 3.0 collective-permute-start.38
  281.8 6.4 %collective-permute-start.41 = (bf16[1,2,4,3072]{3,2,1,0:T(4,128)(2,1)}, bf16[1,2,4,3072]{3,2,1,0:T(4,128)(2,1)}, u32[]{:S(2)}, u32[]{:S(2)}) collective-permute-start(bf16[1,2,4,3072]{3,2,1,0:T(4,128)(2,1)} %fusion.190), channel_id=1, source_target_pairs={{32,16},{48,0},{33,17},{49,1},{34,18},{50,2},{35,19},{51,3},{36,20... | collective-permute-start | bytes 147464 | tf_op jit(solution)/shard_map/ppermute | solution.py:202
  283.1 5.1 collective-permute-start.40
  314.2 146.0 %collective-permute-start.28 = (bf16[3072,768]{1,0:T(8,128)(2,1)}, bf16[3072,768]{1,0:T(8,128)(2,1)}, u32[]{:S(2)}, u32[]{:S(2)}) collective-permute-start(bf16[3072,768]{1,0:T(8,128)(2,1)} %get-tuple-element.88), channel_id=1, source_target_pairs={{0,16},{16,0},{32,48},{48,32},{64,80},{80,64},{96,112},{112,96},{1... | collective-permute-start | bytes 14155784 | tf_op jit(solution)/shard_map/cond/branch_15_fun/ppermute | solution.py:214
  356.1 204.8 %collective-permute-start.29 = (bf16[768,3072]{1,0:T(8,128)(2,1)}, bf16[768,3072]{1,0:T(8,128)(2,1)}, u32[]{:S(2)}, u32[]{:S(2)}) collective-permute-start(bf16[768,3072]{1,0:T(8,128)(2,1)} %get-tuple-element.89), channel_id=1, source_target_pairs={{0,16},{16,0},{32,48},{48,32},{64,80},{80,64},{96,112},{112,96},{1... | collective-permute-start | bytes 14155784 | tf_op jit(solution)/shard_map/cond/branch_15_fun/ppermute | solution.py:214
  (19 other events, 229.4 us)

commit v7 on v6

--- a/solution.py
+++ b/solution.py
@@ -212,6 +212,15 @@
     if not pairs:
         return (jnp.zeros_like(stepped_in), jnp.zeros_like(stepped_out))
     return (lax.ppermute(stepped_in, PAIR, pairs), lax.ppermute(stepped_out, PAIR, pairs))
+
+
+def sent_early(payload, anchor, source, target, replicas, flip):
+    pairs = [
+        (source * replicas + h, target * replicas + (replicas - 1 - h if flip else h))
+        for h in range(replicas)
+    ]
+    tied = lax.optimization_barrier((payload, anchor))[0]
+    return lax.ppermute(tied, PAIR, pairs)
 
 
 def on_device(block_inputs, routes, cotangent, gossip_peer, w_in, w_out):
@@ -229,6 +238,7 @@
     scale_in = model_width ** (-0.5)
     scale_out = (hidden * group_size) ** (-0.5)
     link_list, live_list = route_tables(routes, blocks)
+    weights = jnp.stack([weight_in, weight_out.T])
 
     opening = jnp.concatenate(
         [
@@ -241,6 +251,9 @@
     x_keep = x_cur
     for bound in range(section_count - 1):
         piece = forward_piece(x_cur, weight_in, weight_out, scale_in, scale_out, shard_idx, bound)
+        if bound == 0:
+            early_zero = sent_early(weights, piece, 0, 0, replicas, True)
+            early_one = sent_early(weights, piece, 1, 0, replicas, True)
         straight, crossed = cross_boundary(piece, bound, bound + 1, replicas)
         sources = jnp.stack(
             [jnp.where(replica == h, straight, crossed) for h in range(replicas)]
@@ -259,10 +272,14 @@
     )
     up_full = gather_rows(up_piece, section_count - 1)
     up_keep = up_full
+    last = section_count - 1
     for depth in reversed(range(1, section_count)):
         grad_piece = backward_piece(
             x_keep, up_full, up_piece, weight_in, weight_out, scale_in, scale_out, shard_idx, depth
         )
+        if depth == last:
+            early_last = sent_early(weights, grad_piece, last, last, replicas, True)
+            early_near = sent_early(weights, grad_piece, last - 1, last, replicas, True)
         straight, crossed = cross_boundary(grad_piece, depth, depth - 1, replicas)
         sources = jnp.stack(
             [jnp.where(replica == h, straight, crossed) for h in range(replicas)]
@@ -280,18 +297,24 @@
     stepped_out = (weight_out.astype(jnp.float32) - LEARNING * accum_out).astype(jnp.bfloat16)
     partner = gossip_peer[my_section, replica]
     paired = partner != replica
-    pattern = jnp.sum(
-        (gossip_peer[:, 0] != 0).astype(jnp.int32) << jnp.arange(section_count, dtype=jnp.int32)
-    )
-    other_in, other_out = lax.switch(
-        pattern,
-        [
-            lambda a, b, chosen=chosen: swap_sections(a, b, chosen, section_count, replicas)
-            for chosen in range(2**section_count)
-        ],
-        stepped_in,
-        stepped_out,
-    )
+    relay_pairs = [(h, replicas + h) for h in range(replicas)] + [
+        (last * replicas + h, (last - 1) * replicas + h) for h in range(replicas)
+    ]
+    early_zero, early_one, early_last, early_near, up_keep = lax.optimization_barrier(
+        (early_zero, early_one, early_last, early_near, up_keep)
+    )
+    relayed = lax.ppermute(jnp.where(my_section == 0, early_one, early_near), PAIR, relay_pairs)
+    peer_weights = jnp.where(
+        my_section == 0, early_zero, jnp.where(my_section == last, early_last, relayed)
+    )
+    peer_in = peer_weights[0]
+    peer_out = peer_weights[1].T
+    swap = [(h, replicas - 1 - h) for h in range(replicas)]
+    peer_x = lax.ppermute(x_keep, "half", swap)
+    peer_up = lax.ppermute(up_keep, "half", swap)
+    peer_d_in, peer_d_out = weight_grads(peer_x, peer_up, peer_in, peer_out, scale_in, scale_out)
+    other_in = (peer_in.astype(jnp.float32) - LEARNING * peer_d_in).astype(jnp.bfloat16)
+    other_out = (peer_out.astype(jnp.float32) - LEARNING * peer_d_out).astype(jnp.bfloat16)
     chosen_in = jnp.where(paired, other_in, stepped_in)
     chosen_out = jnp.where(paired, other_out, stepped_out)
     new_in = (0.5 * (stepped_in.astype(jnp.float32) + chosen_in.astype(jnp.float32))).astype(

time: 589 us -> 803 us (1.36)
  the two profiles are of different devices: /device:TPU:16 before, /device:TPU:8 now
where the time goes in v7:
time: 803 us; the launch traced here: 793 us
  waiting for transfers between devices  493 us (61%)
  matrix products  80.3 us (10%)
  Pallas kernels  68.6 us (9%)
  local copies, waits for them, and re-layouts  64.3 us (8%)
  other arithmetic  53.6 us (7%)
  starting transfers between devices  30.6 us (4%)
    ppermute x6, waiting for transfers between devices, cross_boundary(): lax.ppermute(piece, PAIR, straight)  478 us
    pallas_call x14, Pallas kernels, plane_dense(): pl.pallas_call(lambda *refs: plane_kernel(count, spread, active, *refs),...  68.6 us
    dot_general x3, matrix products, backward_piece(): lax.dot_general(d_pre, weight_in, (((1,), (1,)), ((), ())), preferred_ele...  24.6 us
    dot_general x2, matrix products, weight_grads(): lax.dot_general(normed, d_pre, (((0,), (0,)), ((), ())), preferred_elemen...  21.2 us
    dot_general x3, matrix products, forward_piece(): jnp.dot(activated, weight_out, preferred_element_type=jnp.float32)  17.9 us
    unnamed x73, local copies, waits for them, and re-layouts  17.6 us
  transfers between devices with their start and end apart: 19, of which 3 were waited for; matrix products, arithmetic and copies ran while one was open for 17% of the time, Pallas kernels for 5%

profile of v7, /device:TPU:8, one launch (start us, length us, event | category | flops | bytes accessed | tf_op | source)
XLA Modules:
  0.0 792.8 jit_solution(14469641120695049910)
XLA Ops:
  2.0 15.3 %shard_map.77 = bf16[16,16,1536]{2,1,0:T(8,128)(2,1)} custom-call(bf16[1,16,1536]{2,1,0:T(8,128)(2,1)} %reshape_transpose.3.refs_0_), custom_call_target="tpu_custom_call" | custom-call | tf_op jit(solution)/shard_map/pallas_call | solution.py:107
  22.8 5.7 fusion.57
  29.6 14.4 %shard_map.78 = bf16[16,16,1536]{2,1,0:T(8,128)(2,1)} custom-call(bf16[16,16,1536]{2,1,0:T(8,128)(2,1)} %convert_element_type.406.refs_0_), custom_call_target="tpu_custom_call" | custom-call | tf_op jit(solution)/shard_map/pallas_call | solution.py:107
  48.0 6.6 copy.77
  54.6 8.3 %pad_maximum_fusion = bf16[2,3072,768]{2,1,0:T(8,128)(2,1)} fusion(bf16[1,3072,768]{2,1,0:T(8,128)(2,1)} %bitcast.291, bf16[1,3072,768]{2,1,0:T(8,128)(2,1)} %param.10), kind=kLoop, calls=%fused_computation | loop fusion | flops 4718592 | bytes 18874368 | tf_op jit(solution)/shard_map/stack | solution.py:241
  78.5 5.7 fusion.54
  99.2 6.6 fusion.51
  129.2 8.4 %fusion.66 = bf16[128,3072]{1,0:T(8,128)(2,1)} fusion(bf16[1,3072,768]{2,1,0:T(8,128)(2,1)} %param.10, bf16[128,3072]{1,0:T(8,128)(2,1)S(1)} %copy-done.17, bf16[1,768,3072]{2,1,0:T(8,128)(2,1)} %param.11, f32[128,768]{1,0:T(8,128)S(1)} %fusion.23), kind=kOutput, calls=%fused_computation.55 | convolution fusion | flops 1210810368 | bytes 11403264 | tf_op jit(solution)/shard_map/dot_general | solution.py:159
  147.2 4.3 collective-permute-start.14
  151.5 4.3 collective-permute-start.15
  162.2 7.8 fusion.63
  182.7 8.4 %fusion.60 = bf16[128,3072]{1,0:T(8,128)(2,1)} fusion(bf16[1,3072,768]{2,1,0:T(8,128)(2,1)} %param.10, bf16[128,3072]{1,0:T(8,128)(2,1)S(1)} %reshape_reshape.14, bf16[1,768,3072]{2,1,0:T(8,128)(2,1)} %param.11, f32[128,768]{1,0:T(8,128)S(1)} %fusion.23), kind=kOutput, calls=%fused_computation.53 | convolution fusion | flops 1210810368 | bytes 11403264 | tf_op jit(solution)/shard_map/dot_general | solution.py:159
  204.8 477.6 %collective-permute-done.10 = bf16[1,2,4,3072]{3,2,1,0:T(4,128)(2,1)S(1)} collective-permute-done((bf16[1,2,4,3072]{3,2,1,0:T(4,128)(2,1)}, bf16[1,2,4,3072]{3,2,1,0:T(4,128)(2,1)S(1)}, u32[]{:S(2)}, u32[]{:S(2)}) %collective-permute-start.10) | collective-permute-done | bytes 49184 | tf_op jit(solution)/shard_map/ppermute | solution.py:202
  683.7 4.7 collective-permute-done.11
  689.3 14.1 %shard_map.90 = bf16[16,16,1536]{2,1,0:T(8,128)(2,1)} custom-call(bf16[1,16,1536]{2,1,0:T(8,128)(2,1)} %reshape_broadcast_in_dim.23.refs_0_), custom_call_target="tpu_custom_call" | custom-call | tf_op jit(solution)/shard_map/pallas_call | solution.py:107
  706.1 9.5 %broadcast_select_fusion = bf16[2,3072,768]{2,1,0:T(8,128)(2,1)} fusion(bf16[2,3072,768]{2,1,0:T(8,128)(2,1)} %collective-permute-done.13, bf16[2,3072,768]{2,1,0:T(8,128)(2,1)} %collective-permute-done.15, pred[]{:T(512)S(6)} %eq.197), kind=kLoop, calls=%fused_computation.9 | loop fusion | flops 4718592 | bytes 28311552 | tf_op jit(solution)/shard_map/jit(_where)/select_n | solution.py:306
  715.7 5.0 collective-permute-start.16
  727.3 6.8 subtract_convert_fusion
  734.1 9.5 %subtract_convert_fusion.2 = bf16[3072,768]{1,0:T(8,128)(2,1)} fusion(bf16[1,3072,768]{2,1,0:T(8,128)(2,1)} %param.10, f32[128,3072]{1,0:T(8,128)S(1)} %copy-done.10, f32[128]{0:T(128)S(1)} %copy-done.29, bf16[128,3072]{1,0:T(8,128)(2,1)S(1)} %select_n.291, bf16[1,768,3072]{2,1,0:T(8,128)(2,1)} %param.11, f32[128,768]{1,0:T(8,128)S(1)} %fusion.23), kind=kOutput, calls=%fused_computation.8 | convolution fusion | flops 1220247552 | bytes 16908800 | tf_op jit(solution)/shard_map/dot_general | solution.py:193
  746.1 10.5 %collective-permute-done.18 = bf16[16,2,4,3072]{3,2,1,0:T(4,128)(2,1)} collective-permute-done((bf16[16,2,4,3072]{3,2,1,0:T(4,128)(2,1)}, bf16[16,2,4,3072]{3,2,1,0:T(4,128)(2,1)}, u32[]{:S(2)}, u32[]{:S(2)}) %collective-permute-start.18) | collective-permute-done | bytes 786464 | tf_op jit(solution)/shard_map/ppermute | solution.py:314
  758.3 7.8 select_select_fusion
  769.8 4.5 fusion.2
  774.3 6.6 copy.98
  780.9 11.7 %fusion.1 = bf16[1,3072,768]{2,1,0:T(8,128)(2,1)} fusion(bf16[3072,768]{1,0:T(8,128)(2,1)} %subtract_convert_fusion.2, pred[]{:T(512)S(6)} %ne.3, bf16[2,3072,768]{2,1,0:T(8,128)(2,1)} %copy-done.3, bf16[128,3072]{1,0:T(8,128)(2,1)S(1)} %reshape.434, f32[128,3072]{1,0:T(8,128)S(1)} %reshape.437, f32[128]{0:T(128)S(1)} %rsqrt.80, f32[128,768]{1,0:T(8,128)S(1)} %fusion.31), kind=kOutput, calls=%fused_computation.10 | convolution fusion | flops 1234403328 | bytes 21627392 | tf_op jit(solution)/shard_map/dot_general | solution.py:193
  (283 shorter events, 126.2 us)
Async XLA Ops:
  45.4 24.7 %collective-permute-start = (bf16[1,2,4,3072]{3,2,1,0:T(4,128)(2,1)S(1)}, bf16[1,2,4,3072]{3,2,1,0:T(4,128)(2,1)S(1)}, u32[]{:S(2)}, u32[]{:S(2)}) collective-permute-start(bf16[1,2,4,3072]{3,2,1,0:T(4,128)(2,1)S(1)} %add_convert_fusion.2), channel_id=1, source_target_pairs={{0,32},{16,48},{1,33},{17,49},{2,34},{18,50},{3,35},{19,51},{4,36}... | collective-permute-start | bytes 147464 | tf_op jit(solution)/shard_map/ppermute | solution.py:202
  46.7 23.4 %collective-permute-start.1 = (bf16[1,2,4,3072]{3,2,1,0:T(4,128)(2,1)S(1)}, bf16[1,2,4,3072]{3,2,1,0:T(4,128)(2,1)S(1)}, u32[]{:S(2)}, u32[]{:S(2)}) collective-permute-start(bf16[1,2,4,3072]{3,2,1,0:T(4,128)(2,1)S(1)} %add_convert_fusion.2), channel_id=1, source_target_pairs={{0,48},{16,32},{1,49},{17,33},{2,50},{18,34},{3,51},{19,35},{4,52}... | collective-permute-start | bytes 147464 | tf_op jit(solution)/shard_map/ppermute | solution.py:202
  62.9 643.2 %collective-permute-start.12 = (bf16[2,3072,768]{2,1,0:T(8,128)(2,1)}, bf16[2,3072,768]{2,1,0:T(8,128)(2,1)}, u32[]{:S(2)}, u32[]{:S(2)}) collective-permute-start(bf16[2,3072,768]{2,1,0:T(8,128)(2,1)} %pad_maximum_fusion), channel_id=1, source_target_pairs={{0,16},{16,0},{1,17},{17,1},{2,18},{18,2},{3,19},{19,3},{4,20},{20... | collective-permute-start | bytes 28311560 | tf_op jit(solution)/shard_map/ppermute | solution.py:223
  65.3 640.8 %collective-permute-start.13 = (bf16[2,3072,768]{2,1,0:T(8,128)(2,1)}, bf16[2,3072,768]{2,1,0:T(8,128)(2,1)}, u32[]{:S(2)}, u32[]{:S(2)}) collective-permute-start(bf16[2,3072,768]{2,1,0:T(8,128)(2,1)} %pad_maximum_fusion), channel_id=1, source_target_pairs={{32,16},{48,0},{33,17},{49,1},{34,18},{50,2},{35,19},{51,3},{36,20... | collective-permute-start | bytes 28311560 | tf_op jit(solution)/shard_map/ppermute | solution.py:223
  89.2 1.5 collective-permute-start.2
  89.9 0.9 collective-permute-start.3
  111.8 6.2 collective-permute-start.4
  112.4 5.5 collective-permute-start.5
  144.4 57.5 %copy-start.20 = (bf16[16,1,8,3072]{3,2,1,0:T(8,128)(2,1)}, bf16[16,1,8,3072]{3,2,1,0:T(8,128)(2,1)S(1)}, u32[]{:S(2)}) copy-start(bf16[16,1,8,3072]{3,2,1,0:T(8,128)(2,1)S(1)} %select_select_fusion.2) | copy-start | bytes 2359300
  147.2 558.9 %collective-permute-start.14 = (bf16[2,3072,768]{2,1,0:T(8,128)(2,1)}, bf16[2,3072,768]{2,1,0:T(8,128)(2,1)}, u32[]{:S(2)}, u32[]{:S(2)}) collective-permute-start(bf16[2,3072,768]{2,1,0:T(8,128)(2,1)} %pad_maximum_fusion), channel_id=1, source_target_pairs={{96,112},{112,96},{97,113},{113,97},{98,114},{114,98},{99,115},{11... | collective-permute-start | bytes 28311560 | tf_op jit(solution)/shard_map/ppermute | solution.py:223
  151.5 554.6 %collective-permute-start.15 = (bf16[2,3072,768]{2,1,0:T(8,128)(2,1)}, bf16[2,3072,768]{2,1,0:T(8,128)(2,1)}, u32[]{:S(2)}, u32[]{:S(2)}) collective-permute-start(bf16[2,3072,768]{2,1,0:T(8,128)(2,1)} %pad_maximum_fusion), channel_id=1, source_target_pairs={{64,112},{80,96},{65,113},{81,97},{66,114},{82,98},{67,115},{83,99... | collective-permute-start | bytes 28311560 | tf_op jit(solution)/shard_map/ppermute | solution.py:223
  155.8 0.7 collective-permute-start.6
  156.4 1.4 collective-permute-start.7
  175.1 0.7 collective-permute-start.8
  175.8 1.3 collective-permute-start.9
  191.1 497.4 %copy-start.30 = (bf16[2,4,2,4]{3,2,1,0:T(2,128)(2,1)S(1)}, bf16[2,4,2,4]{3,2,1,0:T(2,128)(2,1)}, u32[]{:S(2)}) copy-start(bf16[2,4,2,4]{3,2,1,0:T(2,128)(2,1)} %get-tuple-element.51) | copy-start | bytes 388
  191.1 512.3 %copy-start.4 = (bf16[16,16,1536]{2,1,0:T(8,128)(2,1)S(1)}, bf16[16,16,1536]{2,1,0:T(8,128)(2,1)}, u32[]{:S(2)}) copy-start(bf16[16,16,1536]{2,1,0:T(8,128)(2,1)} %shard_map.84) | copy-start | bytes 2359300
  191.1 512.3 %copy-start.5 = (bf16[16,16,1536]{2,1,0:T(8,128)(2,1)S(1)}, bf16[16,16,1536]{2,1,0:T(8,128)(2,1)}, u32[]{:S(2)}) copy-start(bf16[16,16,1536]{2,1,0:T(8,128)(2,1)} %shard_map.86) | copy-start | bytes 2359300
  191.1 512.3 %copy-start.6 = (bf16[16,16,1536]{2,1,0:T(8,128)(2,1)S(1)}, bf16[16,16,1536]{2,1,0:T(8,128)(2,1)}, u32[]{:S(2)}) copy-start(bf16[16,16,1536]{2,1,0:T(8,128)(2,1)} %shard_map.88) | copy-start | bytes 2359300
  203.5 478.9 %collective-permute-start.10 = (bf16[1,2,4,3072]{3,2,1,0:T(4,128)(2,1)}, bf16[1,2,4,3072]{3,2,1,0:T(4,128)(2,1)S(1)}, u32[]{:S(2)}, u32[]{:S(2)}) collective-permute-start(bf16[1,2,4,3072]{3,2,1,0:T(4,128)(2,1)} %fusion.226), channel_id=1, source_target_pairs={{32,0},{48,16},{33,1},{49,17},{34,2},{50,18},{35,3},{51,19},{36,4}... | collective-permute-start | bytes 147464 | tf_op jit(solution)/shard_map/ppermute | solution.py:202
  682.4 6.0 collective-permute-start.11
  715.7 42.6 %collective-permute-start.16 = (bf16[2,3072,768]{2,1,0:T(8,128)(2,1)}, bf16[2,3072,768]{2,1,0:T(8,128)(2,1)}, u32[]{:S(2)}, u32[]{:S(2)}) collective-permute-start(bf16[2,3072,768]{2,1,0:T(8,128)(2,1)} %broadcast_select_fusion), channel_id=1, source_target_pairs={{0,32},{16,48},{96,64},{112,80},{1,33},{17,49},{97,65},{113,81},{2... | collective-permute-start | bytes 28311560 | tf_op jit(solution)/shard_map/ppermute | solution.py:306
  721.9 21.8 %collective-permute-start.17 = (bf16[16,2,4,3072]{3,2,1,0:T(4,128)(2,1)}, bf16[16,2,4,3072]{3,2,1,0:T(4,128)(2,1)S(1)}, u32[]{:S(2)}, u32[]{:S(2)}) collective-permute-start(bf16[16,2,4,3072]{3,2,1,0:T(4,128)(2,1)} %bitcast.304), channel_id=1, source_target_pairs={{0,16},{16,0},{1,17},{17,1},{2,18},{18,2},{3,19},{19,3},{4,20},{20... | collective-permute-start | bytes 2359304 | tf_op jit(solution)/shard_map/ppermute | solution.py:313
  744.1 12.5 %collective-permute-start.18 = (bf16[16,2,4,3072]{3,2,1,0:T(4,128)(2,1)}, bf16[16,2,4,3072]{3,2,1,0:T(4,128)(2,1)}, u32[]{:S(2)}, u32[]{:S(2)}) collective-permute-start(bf16[16,2,4,3072]{3,2,1,0:T(4,128)(2,1)} %select_n.295), channel_id=1, source_target_pairs={{0,16},{16,0},{1,17},{17,1},{2,18},{18,2},{3,19},{19,3},{4,20},{20... | collective-permute-start | bytes 2359304 | tf_op jit(solution)/shard_map/ppermute | solution.py:314
  (30 other events, 344.6 us)

commit v8 on v7

--- a/solution.py
+++ b/solution.py
@@ -196,10 +196,73 @@
     return (d_in, d_out)
 
 
+def route_kernel(source, target, piece_ref, out_ref, held, send_sem, recv_sem):
+    section = lax.axis_index("section")
+    half = lax.axis_index("half")
+    plane = lax.axis_index("plane")
+    barrier = pltpu.get_barrier_semaphore()
+    mesh_ids = pl.DeviceIdType.MESH
+
+    def transfer(way, far):
+        return pltpu.make_async_remote_copy(
+            src_ref=piece_ref,
+            dst_ref=held.at[way],
+            send_sem=send_sem.at[way],
+            recv_sem=recv_sem.at[way],
+            device_id=(far, lax.select(way == 0, half, 1 - half), plane),
+            device_id_type=mesh_ids,
+        )
+
+    @pl.when(section == source)
+    def _():
+        for way in range(2):
+            pl.semaphore_signal(
+                barrier, inc=1, device_id=(target, lax.select(way == 0, half, 1 - half), plane),
+                device_id_type=mesh_ids,
+            )
+        pl.semaphore_wait(barrier, 2)
+        copies = [transfer(way, target) for way in range(2)]
+        for copy in copies:
+            copy.start()
+        for copy in copies:
+            copy.wait_send()
+        out_ref[...] = jnp.zeros_like(out_ref)
+
+    @pl.when(section == target)
+    def _():
+        for way in range(2):
+            pl.semaphore_signal(
+                barrier, inc=1, device_id=(source, lax.select(way == 0, half, 1 - half), plane),
+                device_id_type=mesh_ids,
+            )
+        pl.semaphore_wait(barrier, 2)
+        for way in range(2):
+            transfer(way, source).wait_recv()
+        out_ref[...] = held[...]
+
+    @pl.when(jnp.logical_and(section != source, section != target))
+    def _():
+        out_ref[...] = jnp.zeros_like(out_ref)
+
+
 def cross_boundary(piece, source, target, replicas):
-    straight = [(source * replicas + h, target * replicas + h) for h in range(replicas)]
-    crossed = [(source * replicas + h, target * replicas + (replicas - 1 - h)) for h in range(replicas)]
-    return (lax.ppermute(piece, PAIR, straight), lax.ppermute(piece, PAIR, crossed))
+    lanes = piece.size // 16
+    dense = piece.reshape(16, lanes)
+    both = pl.pallas_call(
+        lambda *refs: route_kernel(source, target, *refs),
+        out_shape=jax.ShapeDtypeStruct((2, 16, lanes), piece.dtype),
+        in_specs=[pl.BlockSpec(memory_space=pltpu.VMEM)],
+        out_specs=pl.BlockSpec(memory_space=pltpu.VMEM),
+        scratch_shapes=[
+            pltpu.VMEM((2, 16, lanes), piece.dtype),
+            pltpu.SemaphoreType.DMA((2,)),
+            pltpu.SemaphoreType.DMA((2,)),
+        ],
+        compiler_params=pltpu.CompilerParams(
+            collective_id=8 + source * 4 + target, has_side_effects=True
+        ),
+    )(dense)
+    return (both[0].reshape(piece.shape), both[1].reshape(piece.shape))
 
 
 def swap_sections(stepped_in, stepped_out, chosen, section_count, replicas):

time: 803 us -> 662 us (0.82)
  the two profiles are of different devices: /device:TPU:8 before, /device:TPU:0 now
where the time goes in v8:
time: 662 us; the launch traced here: 651 us
  Pallas kernels  409 us (62%)
  matrix products  79.4 us (12%)
  local copies, waits for them, and re-layouts  66.5 us (10%)
  other arithmetic  62.4 us (9%)
  starting transfers between devices  20.7 us (3%)
  waiting for transfers between devices  10.5 us (2%)
    pallas_call x6, Pallas kernels, cross_boundary(): pl.pallas_call(lambda *refs: route_kernel(source, target, *refs), out_sha...  340 us
    pallas_call x14, Pallas kernels, plane_dense(): pl.pallas_call(lambda *refs: plane_kernel(count, spread, active, *refs),...  68.6 us
    dot_general x3, matrix products, backward_piece(): lax.dot_general(d_pre, weight_in, (((1,), (1,)), ((), ())), preferred_ele...  23.6 us
    dot_general x2, matrix products, weight_grads(): lax.dot_general(normed, d_pre, (((0,), (0,)), ((), ())), preferred_elemen...  21.2 us
    unnamed x83, local copies, waits for them, and re-layouts  18.5 us
    dot_general x3, matrix products, forward_piece(): jnp.dot(activated, weight_out, preferred_element_type=jnp.float32)  17.9 us
    ppermute x4, starting transfers between devices, sent_early(): return lax.ppermute(tied, PAIR, pairs)  13.4 us
  transfers between devices with their start and end apart: 7, of which 1 were waited for; matrix products, arithmetic and copies ran while one was open for 9% of the time, Pallas kernels for 55%

profile of v8, /device:TPU:0, one launch (start us, length us, event | category | flops | bytes accessed | tf_op | source)
XLA Modules:
  0.0 650.9 jit_solution(691862721786461020)
XLA Ops:
  2.0 15.4 %shard_map.77 = bf16[16,16,1536]{2,1,0:T(8,128)(2,1)} custom-call(bf16[1,16,1536]{2,1,0:T(8,128)(2,1)} %reshape_transpose.3.refs_0_), custom_call_target="tpu_custom_call" | custom-call | tf_op jit(solution)/shard_map/pallas_call | solution.py:107
  26.8 5.7 fusion.57
  33.7 14.4 %shard_map.78 = bf16[16,16,1536]{2,1,0:T(8,128)(2,1)} custom-call(bf16[16,16,1536]{2,1,0:T(8,128)(2,1)} %convert_element_type.406.refs_0_), custom_call_target="tpu_custom_call" | custom-call | tf_op jit(solution)/shard_map/pallas_call | solution.py:107
  62.7 5.7 fusion.54
  84.8 6.6 %fusion.51 = bf16[128,3072]{1,0:T(8,128)(2,1)} fusion(bf16[1,768,3072]{2,1,0:T(8,128)(2,1)} %param.11, bf16[128,3072]{1,0:T(8,128)(2,1)S(1)} %convert_element_type.423, bf16[1,3072,768]{2,1,0:T(8,128)(2,1)} %param.10), kind=kOutput, calls=%fused_computation.50 | convolution fusion | flops 1209729024 | bytes 11010048 | tf_op jit(solution)/shard_map/dot_general | solution.py:139
  109.9 6.6 %copy.89 = bf16[1,768,3072]{1,2,0:T(8,128)(2,1)} copy(bf16[1,768,3072]{2,1,0:T(8,128)(2,1)} %param.11) | data formatting | bytes 9437184 | tf_op args[5]
  126.1 8.4 %fusion.66 = bf16[128,3072]{1,0:T(8,128)(2,1)} fusion(bf16[1,3072,768]{2,1,0:T(8,128)(2,1)} %param.10, bf16[128,3072]{1,0:T(8,128)(2,1)S(1)} %reshape_reshape.12, bf16[1,768,3072]{2,1,0:T(8,128)(2,1)} %param.11, f32[128,768]{1,0:T(8,128)S(1)} %fusion.23), kind=kOutput, calls=%fused_computation.55 | convolution fusion | flops 1210810368 | bytes 11403264 | tf_op jit(solution)/shard_map/dot_general | solution.py:159
  145.3 8.4 %pad_maximum_fusion = bf16[2,3072,768]{2,1,0:T(8,128)(2,1)} fusion(bf16[1,3072,768]{2,1,0:T(8,128)(2,1)} %bitcast.272, bf16[1,3072,768]{2,1,0:T(8,128)(2,1)} %param.10), kind=kLoop, calls=%fused_computation | loop fusion | flops 4718592 | bytes 18874368 | tf_op jit(solution)/shard_map/stack | solution.py:304
  154.7 4.3 collective-permute-start.2
  159.0 4.3 collective-permute-start.3
  163.3 3.5 collective-permute-start
  175.4 7.8 %fusion.63 = bf16[128,3072]{1,0:T(8,128)(2,1)S(1)} fusion(bf16[1,3072,768]{2,1,0:T(8,128)(2,1)} %param.10, bf16[128,3072]{1,0:T(8,128)(2,1)S(1)} %reshape_reshape.13, bf16[1,768,3072]{2,1,0:T(8,128)(2,1)} %param.11, f32[128,768]{1,0:T(8,128)S(1)} %fusion.23), kind=kOutput, calls=%fused_computation.54 | convolution fusion | flops 1210810368 | bytes 11403264 | tf_op jit(solution)/shard_map/dot_general | solution.py:159
  199.2 7.5 %fusion.60 = bf16[128,3072]{1,0:T(8,128)(2,1)S(1)} fusion(bf16[1,3072,768]{2,1,0:T(8,128)(2,1)} %param.10, bf16[128,3072]{1,0:T(8,128)(2,1)S(1)} %reshape_reshape.14, bf16[1,768,3072]{2,1,0:T(8,128)(2,1)} %param.11, f32[128,768]{1,0:T(8,128)S(1)} %fusion.23), kind=kOutput, calls=%fused_computation.53 | convolution fusion | flops 1210810368 | bytes 11403264 | tf_op jit(solution)/shard_map/dot_general | solution.py:159
  214.2 331.0 %shard_map.95 = bf16[2,16,1536]{2,1,0:T(8,128)(2,1)} custom-call(bf16[16,1536]{1,0:T(8,128)(2,1)} %reshape.745.refs_0_), custom_call_target="tpu_custom_call" | custom-call | tf_op jit(solution)/shard_map/pallas_call | solution.py:251
  547.0 14.1 %shard_map.96 = bf16[16,16,1536]{2,1,0:T(8,128)(2,1)} custom-call(bf16[1,16,1536]{2,1,0:T(8,128)(2,1)} %reshape_broadcast_in_dim.23.refs_0_), custom_call_target="tpu_custom_call" | custom-call | tf_op jit(solution)/shard_map/pallas_call | solution.py:107
  563.8 9.5 %broadcast_select_fusion = bf16[2,3072,768]{2,1,0:T(8,128)(2,1)} fusion(bf16[2,3072,768]{2,1,0:T(8,128)(2,1)} %collective-permute-done.1, bf16[2,3072,768]{2,1,0:T(8,128)(2,1)} %collective-permute-done.3, pred[]{:T(512)S(6)} %eq.197), kind=kLoop, calls=%fused_computation.9 | loop fusion | flops 4718592 | bytes 28311552 | tf_op jit(solution)/shard_map/jit(_where)/select_n | solution.py:369
  573.3 5.1 collective-permute-start.4
  585.4 6.8 %subtract_convert_fusion = bf16[768,3072]{0,1:T(8,128)(2,1)} fusion(bf16[1,768,3072]{1,2,0:T(8,128)(2,1)} %copy.89, bf16[128,3072]{1,0:T(8,128)(2,1)} %reshape.747, bf16[128,3072]{1,0:T(8,128)(2,1)} %copy-done.21, bf16[128,3072]{1,0:T(8,128)(2,1)} %copy-done.20, bf16[128,3072]{1,0:T(8,128)(2,1)} %copy-done.19, pred[]{:T(512)S(6)} %eq.195, pred[]{:T(512)S(6)} %eq.196, ...), kind=kOutput, calls=%fused_computation.4 | convolution fusion | flops 615579648 | bytes 12976131 | tf_op jit(solution)/shard_map/dot_general | solution.py:184
  592.2 9.5 %subtract_convert_fusion.2 = bf16[3072,768]{1,0:T(8,128)(2,1)} fusion(bf16[1,3072,768]{2,1,0:T(8,128)(2,1)} %param.10, f32[128,3072]{1,0:T(8,128)S(1)} %copy-done.10, f32[128]{0:T(128)S(1)} %copy-done.32, bf16[128,3072]{1,0:T(8,128)(2,1)S(1)} %copy-done.17, bf16[1,768,3072]{2,1,0:T(8,128)(2,1)} %param.11, f32[128,768]{1,0:T(8,128)S(1)} %fusion.23), kind=kOutput, calls=%fused_computation.8 | convolution fusion | flops 1220247552 | bytes 16908800 | tf_op jit(solution)/shard_map/dot_general | solution.py:193
  604.2 10.5 %collective-permute-done.6 = bf16[16,2,4,3072]{3,2,1,0:T(4,128)(2,1)} collective-permute-done((bf16[16,2,4,3072]{3,2,1,0:T(4,128)(2,1)}, bf16[16,2,4,3072]{3,2,1,0:T(4,128)(2,1)}, u32[]{:S(2)}, u32[]{:S(2)}) %collective-permute-start.6) | collective-permute-done | bytes 786464 | tf_op jit(solution)/shard_map/ppermute | solution.py:377
  616.4 7.8 %select_select_fusion = bf16[2,3072,768]{2,1,0:T(8,128)(2,1)S(1)} fusion(bf16[2,3072,768]{2,1,0:T(8,128)(2,1)} %collective-permute-done, bf16[2,3072,768]{2,1,0:T(8,128)(2,1)} %collective-permute-done.2, bf16[2,3072,768]{2,1,0:T(8,128)(2,1)} %collective-permute-done.4, pred[]{:T(512)S(6)} %eq.162, pred[]{:T(512)S(6)} %eq.197), kind=kLoop, calls=%fused_computation.7 | loop fusion | flops 9437184 | bytes 37748736 | tf_op jit(solution)/shard_map/jit(_where)/select_n | solution.py:370
  627.9 4.5 fusion.2
  632.4 6.6 %copy.116 = bf16[1,768,3072]{2,1,0:T(8,128)(2,1)} copy(bf16[1,768,3072]{1,2,0:T(8,128)(2,1)} %fusion.2) | data formatting | bytes 9437184
  639.0 11.7 %fusion.1 = bf16[1,3072,768]{2,1,0:T(8,128)(2,1)} fusion(bf16[3072,768]{1,0:T(8,128)(2,1)} %subtract_convert_fusion.2, pred[]{:T(512)S(6)} %ne.3, bf16[2,3072,768]{2,1,0:T(8,128)(2,1)} %copy-done.3, bf16[128,3072]{1,0:T(8,128)(2,1)S(1)} %reshape.746, f32[128,3072]{1,0:T(8,128)S(1)} %reshape.749, f32[128]{0:T(128)S(1)} %rsqrt.80, f32[128,768]{1,0:T(8,128)S(1)} %fusion.31), kind=kOutput, calls=%fused_computation.10 | convolution fusion | flops 1234403328 | bytes 21627392 | tf_op jit(solution)/shard_map/dot_general | solution.py:193
  (293 shorter events, 132.7 us)
Async XLA Ops:
  20.8 28.6 %copy-start.11 = (bf16[16,2,4,3072]{3,2,1,0:T(4,128)(2,1)}, bf16[16,2,4,3072]{3,2,1,0:T(4,128)(2,1)S(1)}, u32[]{:S(2)}) copy-start(bf16[16,2,4,3072]{3,2,1,0:T(4,128)(2,1)S(1)} %reshape.736) | copy-start | bytes 2359300
  60.6 12.6 %copy-start.13 = (bf16[16,2,4,3072]{3,2,1,0:T(4,128)(2,1)}, bf16[16,2,4,3072]{3,2,1,0:T(4,128)(2,1)S(1)}, u32[]{:S(2)}) copy-start(bf16[16,2,4,3072]{3,2,1,0:T(4,128)(2,1)S(1)} %reshape.738) | copy-start | bytes 2359300
  82.7 14.6 %copy-start.15 = (bf16[16,2,4,3072]{3,2,1,0:T(4,128)(2,1)}, bf16[16,2,4,3072]{3,2,1,0:T(4,128)(2,1)S(1)}, u32[]{:S(2)}) copy-start(bf16[16,2,4,3072]{3,2,1,0:T(4,128)(2,1)S(1)} %reshape.740) | copy-start | bytes 2359300
  91.4 16.9 %copy-start = (bf16[16,16,1536]{2,1,0:T(8,128)(2,1)S(1)}, bf16[16,16,1536]{2,1,0:T(8,128)(2,1)}, u32[]{:S(2)}) copy-start(bf16[16,16,1536]{2,1,0:T(8,128)(2,1)} %shard_map.77) | copy-start | bytes 2359300
  91.4 16.9 %copy-start.1 = (bf16[16,16,1536]{2,1,0:T(8,128)(2,1)S(1)}, bf16[16,16,1536]{2,1,0:T(8,128)(2,1)}, u32[]{:S(2)}) copy-start(bf16[16,16,1536]{2,1,0:T(8,128)(2,1)} %shard_map.80) | copy-start | bytes 2359300
  91.4 16.9 %copy-start.2 = (bf16[16,16,1536]{2,1,0:T(8,128)(2,1)S(1)}, bf16[16,16,1536]{2,1,0:T(8,128)(2,1)}, u32[]{:S(2)}) copy-start(bf16[16,16,1536]{2,1,0:T(8,128)(2,1)} %shard_map.83) | copy-start | bytes 2359300
  145.3 43.7 %copy-start.29 = (f32[2,4]{1,0:T(2,128)}, f32[2,4]{1,0:T(2,128)S(1)}, u32[]{:S(2)}) copy-start(f32[2,4]{1,0:T(2,128)S(1)} %fusion.259) | copy-start | bytes 100
  154.7 409.1 %collective-permute-start.2 = (bf16[2,3072,768]{2,1,0:T(8,128)(2,1)}, bf16[2,3072,768]{2,1,0:T(8,128)(2,1)}, u32[]{:S(2)}, u32[]{:S(2)}) collective-permute-start(bf16[2,3072,768]{2,1,0:T(8,128)(2,1)} %pad_maximum_fusion), channel_id=1, source_target_pairs={{96,112},{112,96},{97,113},{113,97},{98,114},{114,98},{99,115},{11... | collective-permute-start | bytes 28311560 | tf_op jit(solution)/shard_map/ppermute | solution.py:286
  159.0 404.8 %collective-permute-start.3 = (bf16[2,3072,768]{2,1,0:T(8,128)(2,1)}, bf16[2,3072,768]{2,1,0:T(8,128)(2,1)}, u32[]{:S(2)}, u32[]{:S(2)}) collective-permute-start(bf16[2,3072,768]{2,1,0:T(8,128)(2,1)} %pad_maximum_fusion), channel_id=1, source_target_pairs={{64,112},{80,96},{65,113},{81,97},{66,114},{82,98},{67,115},{83,99... | collective-permute-start | bytes 28311560 | tf_op jit(solution)/shard_map/ppermute | solution.py:286
  163.3 400.5 %collective-permute-start = (bf16[2,3072,768]{2,1,0:T(8,128)(2,1)}, bf16[2,3072,768]{2,1,0:T(8,128)(2,1)}, u32[]{:S(2)}, u32[]{:S(2)}) collective-permute-start(bf16[2,3072,768]{2,1,0:T(8,128)(2,1)} %pad_maximum_fusion), channel_id=1, source_target_pairs={{0,16},{16,0},{1,17},{17,1},{2,18},{18,2},{3,19},{19,3},{4,20},{20... | collective-permute-start | bytes 28311560 | tf_op jit(solution)/shard_map/ppermute | solution.py:286
  166.7 397.0 %collective-permute-start.1 = (bf16[2,3072,768]{2,1,0:T(8,128)(2,1)}, bf16[2,3072,768]{2,1,0:T(8,128)(2,1)}, u32[]{:S(2)}, u32[]{:S(2)}) collective-permute-start(bf16[2,3072,768]{2,1,0:T(8,128)(2,1)} %pad_maximum_fusion), channel_id=1, source_target_pairs={{32,16},{48,0},{33,17},{49,1},{34,18},{50,2},{35,19},{51,3},{36,20... | collective-permute-start | bytes 28311560 | tf_op jit(solution)/shard_map/ppermute | solution.py:286
  199.2 13.4 %copy-start.30 = (f32[2,4]{1,0:T(2,128)S(1)}, f32[2,4]{1,0:T(2,128)}, u32[]{:S(2)}) copy-start(f32[2,4]{1,0:T(2,128)} %copy-done.29) | copy-start | bytes 100
  206.7 339.4 %copy-start.34 = (bf16[2,4,2,4]{3,2,1,0:T(2,128)(2,1)S(1)}, bf16[2,4,2,4]{3,2,1,0:T(2,128)(2,1)}, u32[]{:S(2)}) copy-start(bf16[2,4,2,4]{3,2,1,0:T(2,128)(2,1)} %get-tuple-element.51) | copy-start | bytes 388
  206.7 354.4 %copy-start.4 = (bf16[16,16,1536]{2,1,0:T(8,128)(2,1)S(1)}, bf16[16,16,1536]{2,1,0:T(8,128)(2,1)}, u32[]{:S(2)}) copy-start(bf16[16,16,1536]{2,1,0:T(8,128)(2,1)} %shard_map.87) | copy-start | bytes 2359300
  206.7 354.4 %copy-start.5 = (bf16[16,16,1536]{2,1,0:T(8,128)(2,1)S(1)}, bf16[16,16,1536]{2,1,0:T(8,128)(2,1)}, u32[]{:S(2)}) copy-start(bf16[16,16,1536]{2,1,0:T(8,128)(2,1)} %shard_map.90) | copy-start | bytes 2359300
  206.7 354.4 %copy-start.6 = (bf16[16,16,1536]{2,1,0:T(8,128)(2,1)S(1)}, bf16[16,16,1536]{2,1,0:T(8,128)(2,1)}, u32[]{:S(2)}) copy-start(bf16[16,16,1536]{2,1,0:T(8,128)(2,1)} %shard_map.93) | copy-start | bytes 2359300
  563.8 16.6 %copy-start.7 = (bf16[16,16,1536]{2,1,0:T(8,128)(2,1)S(1)}, bf16[16,16,1536]{2,1,0:T(8,128)(2,1)}, u32[]{:S(2)}) copy-start(bf16[16,16,1536]{2,1,0:T(8,128)(2,1)} %shard_map.96) | copy-start | bytes 2359300
  563.8 18.9 %copy-start.9 = (bf16[16,16,1536]{2,1,0:T(8,128)(2,1)S(1)}, bf16[16,16,1536]{2,1,0:T(8,128)(2,1)}, u32[]{:S(2)}) copy-start(bf16[16,16,1536]{2,1,0:T(8,128)(2,1)} %copy-done.8) | copy-start | bytes 2359300
  573.3 10.8 %copy-start.37 = (s32[4,2]{0,1:T(2,128)S(1)}, s32[4,2]{0,1:T(2,128)}, u32[]{:S(2)}) copy-start(s32[4,2]{0,1:T(2,128)} %param.9) | copy-start | bytes 100
  573.3 43.1 %collective-permute-start.4 = (bf16[2,3072,768]{2,1,0:T(8,128)(2,1)}, bf16[2,3072,768]{2,1,0:T(8,128)(2,1)}, u32[]{:S(2)}, u32[]{:S(2)}) collective-permute-start(bf16[2,3072,768]{2,1,0:T(8,128)(2,1)} %broadcast_select_fusion), channel_id=1, source_target_pairs={{0,32},{16,48},{96,64},{112,80},{1,33},{17,49},{97,65},{113,81},{2... | collective-permute-start | bytes 28311560 | tf_op jit(solution)/shard_map/ppermute | solution.py:369
  578.3 23.4 %collective-permute-start.5 = (bf16[16,2,4,3072]{3,2,1,0:T(4,128)(2,1)}, bf16[16,2,4,3072]{3,2,1,0:T(4,128)(2,1)S(1)}, u32[]{:S(2)}, u32[]{:S(2)}) collective-permute-start(bf16[16,2,4,3072]{3,2,1,0:T(4,128)(2,1)} %bitcast.271), channel_id=1, source_target_pairs={{0,16},{16,0},{1,17},{17,1},{2,18},{18,2},{3,19},{19,3},{4,20},{20... | collective-permute-start | bytes 2359304 | tf_op jit(solution)/shard_map/ppermute | solution.py:376
  602.2 12.5 %collective-permute-start.6 = (bf16[16,2,4,3072]{3,2,1,0:T(4,128)(2,1)}, bf16[16,2,4,3072]{3,2,1,0:T(4,128)(2,1)}, u32[]{:S(2)}, u32[]{:S(2)}) collective-permute-start(bf16[16,2,4,3072]{3,2,1,0:T(4,128)(2,1)} %select_n.451), channel_id=1, source_target_pairs={{0,16},{16,0},{1,17},{17,1},{2,18},{18,2},{3,19},{19,3},{4,20},{20... | collective-permute-start | bytes 2359304 | tf_op jit(solution)/shard_map/ppermute | solution.py:377
  614.7 13.1 %slice-start = ((s8[4718592]{0:T(1024)(128)(4,1)}), s8[524288]{0:T(1024)(128)(4,1)S(1)}, s32[]{:S(2)}) async-start(s8[4718592]{0:T(1024)(128)(4,1)} %bitcast.273), calls=%async_computation | async-start | bytes 1048576
  616.4 11.5 %slice-start.1 = ((s8[4718592]{0:T(1024)(128)(4,1)}), s8[4194304]{0:T(1024)(128)(4,1)S(1)}, s32[]{:S(2)}) async-start(s8[4718592]{0:T(1024)(128)(4,1)} %bitcast.273), calls=%async_computation.1 | async-start | bytes 8388608
  (23 other events, 136.6 us)

commit v9 on v6

--- a/solution.py
+++ b/solution.py
@@ -230,15 +230,12 @@
     scale_out = (hidden * group_size) ** (-0.5)
     link_list, live_list = route_tables(routes, blocks)
 
-    opening = jnp.concatenate(
-        [
-            block_inputs,
-            jnp.zeros((micro_count, capacity - blocks, piece_rows, model_width), jnp.bfloat16),
-        ],
-        axis=1,
-    ).transpose(2, 0, 1, 3)
-    x_cur = gather_rows(opening, 0)
-    x_keep = x_cur
+    def padded(full):
+        filler = jnp.zeros(full.shape[:2] + (capacity - full.shape[2],) + full.shape[3:], full.dtype)
+        return jnp.concatenate([full, filler], axis=2)
+
+    x_cur = gather_rows(block_inputs.transpose(2, 0, 1, 3), 0)
+    x_keep = padded(x_cur)
     for bound in range(section_count - 1):
         piece = forward_piece(x_cur, weight_in, weight_out, scale_in, scale_out, shard_idx, bound)
         straight, crossed = cross_boundary(piece, bound, bound + 1, replicas)
@@ -246,6 +243,7 @@
             [jnp.where(replica == h, straight, crossed) for h in range(replicas)]
         )[:, 0]
         mine = lax.dynamic_index_in_dim(link_list[bound], replica, 3, keepdims=False)
+        mine = mine[:, :, : piece.shape[2], :]
         routed = jnp.einsum(
             "mqjk,qmjd->mkd", mine.astype(jnp.bfloat16), sources,
             preferred_element_type=jnp.float32,
@@ -268,12 +266,14 @@
             [jnp.where(replica == h, straight, crossed) for h in range(replicas)]
         )[:, 0]
         mine = lax.dynamic_index_in_dim(link_list[depth - 1], replica, 1, keepdims=False)
+        if depth == 1:
+            mine = mine[:, :blocks]
         up_piece = jnp.einsum(
             "mjdk,dmkD->mjD", mine.astype(jnp.bfloat16), sources,
             preferred_element_type=jnp.float32,
         ).astype(jnp.bfloat16)[None]
         up_full = gather_rows(up_piece, depth - 1)
-        up_keep = jnp.where(my_section == depth - 1, up_full, up_keep)
+        up_keep = jnp.where(my_section == depth - 1, padded(up_full), up_keep)
 
     accum_in, accum_out = weight_grads(x_keep, up_keep, weight_in, weight_out, scale_in, scale_out)
     stepped_in = (weight_in.astype(jnp.float32) - LEARNING * accum_in).astype(jnp.bfloat16)

time: 589 us -> 570 us (0.968)
  waiting for transfers between devices: 246 us -> 239 us
  transfers between devices with their start and end apart: 14 -> 14, of which waited for: 6 -> 5; matrix products, arithmetic and copies ran while one was open for 2% -> 2% of each run, Pallas kernels for 0% -> 0%
where the time goes in v9:
time: 570 us; the launch traced here: 561 us
  waiting for transfers between devices  239 us (42%)
  Pallas kernels  112 us (20%)
  starting transfers between devices  63.1 us (11%)
  matrix products  60.7 us (11%)
  other arithmetic  43.1 us (8%)
  local copies, waits for them, and re-layouts  39.1 us (7%)
    pallas_call x14, Pallas kernels, plane_dense(): pl.pallas_call(lambda *refs: plane_kernel(count, spread, active, *refs),...  112 us
    ppermute x1, waiting for transfers between devices, swap_sections(): lax.ppermute(stepped_out, PAIR, pairs)  101 us
    ppermute x1, waiting for transfers between devices, swap_sections(): lax.ppermute(stepped_in, PAIR, pairs)  93.9 us
    ppermute x6, waiting for transfers between devices, cross_boundary(): lax.ppermute(piece, PAIR, crossed)  43 us
    ppermute x1, starting transfers between devices, swap_sections(): lax.ppermute(stepped_in, PAIR, pairs)  38.4 us
    dot_general x3, matrix products, backward_piece(): lax.dot_general(d_pre, weight_in, (((1,), (1,)), ((), ())), preferred_ele...  23.4 us
    dot_general x3, matrix products, forward_piece(): jnp.dot(activated, weight_out, preferred_element_type=jnp.float32)  17.2 us
    broadcast_in_dim x2, other arithmetic, on_device(): return (new_in[None], new_out[None])  16.1 us
  transfers between devices with their start and end apart: 14, of which 5 were waited for; matrix products, arithmetic and copies ran while one was open for 2% of the time, Pallas kernels for 0%

profile of v9, /device:TPU:16, one launch (start us, length us, event | category | flops | bytes accessed | tf_op | source)
XLA Modules:
  0.0 560.5 jit_solution(4848239214233362573)
XLA Ops:
  8.0 5.9 %fusion.63 = bf16[64,3072]{1,0:T(8,128)(2,1)S(1)} fusion(bf16[1,768,3072]{2,1,0:T(8,128)(2,1)} %param.27, bf16[64,3072]{1,0:T(8,128)(2,1)S(1)} %convert_element_type.358, bf16[1,3072,768]{2,1,0:T(8,128)(2,1)} %param.26), kind=kOutput, calls=%fused_computation.45 | convolution fusion | flops 604864512 | bytes 10223616 | tf_op jit(solution)/shard_map/dot_general | solution.py:139
  14.8 19.5 %shard_map.78 = bf16[16,16,768]{2,1,0:T(8,128)(2,1)} custom-call(bf16[16,16,768]{2,1,0:T(8,128)(2,1)} %convert_element_type.361.refs_0_), custom_call_target="tpu_custom_call" | custom-call | tf_op jit(solution)/shard_map/pallas_call | solution.py:107
  49.7 5.7 %fusion.48 = bf16[128,3072]{1,0:T(8,128)(2,1)S(1)} fusion(bf16[1,768,3072]{2,1,0:T(8,128)(2,1)} %param.27, bf16[128,3072]{1,0:T(8,128)(2,1)S(1)} %convert_element_type.368, bf16[1,3072,768]{2,1,0:T(8,128)(2,1)} %param.26), kind=kOutput, calls=%fused_computation.40 | convolution fusion | flops 1209729024 | bytes 11010048 | tf_op jit(solution)/shard_map/dot_general | solution.py:139
  62.8 30.6 %collective-permute-done.33 = bf16[1,2,4,3072]{3,2,1,0:T(4,128)(2,1)S(1)} collective-permute-done((bf16[1,2,4,3072]{3,2,1,0:T(4,128)(2,1)S(1)}, bf16[1,2,4,3072]{3,2,1,0:T(4,128)(2,1)S(1)}, u32[]{:S(2)}, u32[]{:S(2)}) %collective-permute-start.33) | collective-permute-done | bytes 49184 | tf_op jit(solution)/shard_map/ppermute | solution.py:202
  96.2 14.4 %shard_map.81 = bf16[16,16,1536]{2,1,0:T(8,128)(2,1)} custom-call(bf16[1,16,1536]{2,1,0:T(8,128)(2,1)} %reshape_broadcast_in_dim.19.refs_0_), custom_call_target="tpu_custom_call" | custom-call | tf_op jit(solution)/shard_map/pallas_call | solution.py:107
  116.1 5.7 %fusion.45 = bf16[128,3072]{1,0:T(8,128)(2,1)S(1)} fusion(bf16[1,768,3072]{2,1,0:T(8,128)(2,1)} %param.27, bf16[128,3072]{1,0:T(8,128)(2,1)S(1)} %convert_element_type.378, bf16[1,3072,768]{2,1,0:T(8,128)(2,1)} %param.26), kind=kOutput, calls=%fused_computation.39 | convolution fusion | flops 1209729024 | bytes 11010048 | tf_op jit(solution)/shard_map/dot_general | solution.py:139
  122.9 14.4 %shard_map.82 = bf16[16,16,1536]{2,1,0:T(8,128)(2,1)} custom-call(bf16[16,16,1536]{2,1,0:T(8,128)(2,1)} %convert_element_type.381.refs_0_), custom_call_target="tpu_custom_call" | custom-call | tf_op jit(solution)/shard_map/pallas_call | solution.py:107
  153.7 3.1 fusion.22
  156.9 7.5 %fusion.57 = bf16[128,3072]{1,0:T(8,128)(2,1)S(1)} fusion(bf16[1,3072,768]{2,1,0:T(8,128)(2,1)} %param.26, bf16[128,3072]{1,0:T(8,128)(2,1)S(1)} %copy-done.5, bf16[1,768,3072]{2,1,0:T(8,128)(2,1)} %param.27, f32[128,768]{1,0:T(8,128)S(1)} %fusion.22), kind=kOutput, calls=%fused_computation.43 | convolution fusion | flops 1210810368 | bytes 11403264 | tf_op jit(solution)/shard_map/dot_general | solution.py:159
  165.5 18.4 %shard_map.85 = bf16[16,16,1536]{2,1,0:T(8,128)(2,1)} custom-call(bf16[16,16,1536]{2,1,0:T(8,128)(2,1)} %convert_element_type.398.refs_0_), custom_call_target="tpu_custom_call" | custom-call | tf_op jit(solution)/shard_map/pallas_call | solution.py:107
  188.8 12.4 %collective-permute-done.37 = bf16[1,2,4,3072]{3,2,1,0:T(4,128)(2,1)S(1)} collective-permute-done((bf16[1,2,4,3072]{3,2,1,0:T(4,128)(2,1)S(1)}, bf16[1,2,4,3072]{3,2,1,0:T(4,128)(2,1)S(1)}, u32[]{:S(2)}, u32[]{:S(2)}) %collective-permute-start.37) | collective-permute-done | bytes 49184 | tf_op jit(solution)/shard_map/ppermute | solution.py:202
  202.1 14.1 %shard_map.86 = bf16[16,16,1536]{2,1,0:T(8,128)(2,1)} custom-call(bf16[1,16,1536]{2,1,0:T(8,128)(2,1)} %reshape_broadcast_in_dim.21.refs_0_), custom_call_target="tpu_custom_call" | custom-call | tf_op jit(solution)/shard_map/pallas_call | solution.py:107
  217.6 7.5 %fusion.54 = bf16[128,3072]{1,0:T(8,128)(2,1)S(1)} fusion(bf16[1,3072,768]{2,1,0:T(8,128)(2,1)} %param.26, bf16[128,3072]{1,0:T(8,128)(2,1)S(1)} %reshape_reshape.13, bf16[1,768,3072]{2,1,0:T(8,128)(2,1)} %param.27, f32[128,768]{1,0:T(8,128)S(1)} %fusion.22), kind=kOutput, calls=%fused_computation.42 | convolution fusion | flops 1210810368 | bytes 11403264 | tf_op jit(solution)/shard_map/dot_general | solution.py:159
  226.3 14.5 %shard_map.87 = bf16[16,16,1536]{2,1,0:T(8,128)(2,1)} custom-call(bf16[16,16,1536]{2,1,0:T(8,128)(2,1)} %convert_element_type.406.refs_0_), custom_call_target="tpu_custom_call" | custom-call | tf_op jit(solution)/shard_map/pallas_call | solution.py:107
  253.7 8.4 %fusion.51 = bf16[128,3072]{1,0:T(8,128)(2,1)} fusion(bf16[1,3072,768]{2,1,0:T(8,128)(2,1)} %param.26, bf16[128,3072]{1,0:T(8,128)(2,1)S(1)} %reshape_reshape.14, bf16[1,768,3072]{2,1,0:T(8,128)(2,1)} %param.27, f32[128,768]{1,0:T(8,128)S(1)} %fusion.22), kind=kOutput, calls=%fused_computation.41 | convolution fusion | flops 1210810368 | bytes 11403264 | tf_op jit(solution)/shard_map/dot_general | solution.py:159
  285.4 6.0 %subtract_convert_fusion = bf16[768,3072]{1,0:T(8,128)(2,1)} fusion(bf16[128,3072]{1,0:T(8,128)(2,1)S(1)} %reshape.397, bf16[1,768,3072]{2,1,0:T(8,128)(2,1)} %param.27, f32[128,768]{1,0:T(8,128)S(1)} %fusion.22), kind=kOutput, calls=%fused_computation.2 | convolution fusion | flops 614400000 | bytes 10616832 | tf_op jit(solution)/shard_map/dot_general | solution.py:184
  291.4 9.5 %subtract_convert_fusion.1 = bf16[3072,768]{1,0:T(8,128)(2,1)} fusion(bf16[1,3072,768]{2,1,0:T(8,128)(2,1)} %param.26, f32[128,3072]{1,0:T(8,128)S(1)} %copy-done.4, f32[128]{0:T(128)S(1)} %copy-done.19, bf16[128,3072]{1,0:T(8,128)(2,1)S(1)} %reshape.397, bf16[1,768,3072]{2,1,0:T(8,128)(2,1)} %param.27, f32[128,768]{1,0:T(8,128)S(1)} %fusion.22), kind=kOutput, calls=%fused_computation.3 | convolution fusion | flops 1220247552 | bytes 16908800 | tf_op jit(solution)/shard_map/dot_general | solution.py:193
  300.9 243.3 %conditional.1 = (bf16[3072,768]{1,0:T(8,128)(2,1)}, bf16[768,3072]{1,0:T(8,128)(2,1)}) conditional(s32[]{:T(128)} %clamp.3, () %tuple.72, (bf16[3072,768]{1,0:T(8,128)(2,1)}, bf16[768,3072]{1,0:T(8,128)(2,1)}) %tuple.73, (bf16[3072,768]{1,0:T(8,128)(2,1)}, bf16[768,3072]{1,0:T(8,128)(2,1)}) %tuple.73, ...), branch_computations={%region_26.27_spmd, %region_27.28_spmd, %region_28.29_spmd, %regio... | conditional | bytes 37748832 | solution.py:286
  301.1 38.4 %collective-permute-start.24 = (bf16[3072,768]{1,0:T(8,128)(2,1)}, bf16[3072,768]{1,0:T(8,128)(2,1)}, u32[]{:S(2)}, u32[]{:S(2)}) collective-permute-start(bf16[3072,768]{1,0:T(8,128)(2,1)} %get-tuple-element.84), channel_id=1, source_target_pairs={{0,16},{16,0},{64,80},{80,64},{96,112},{112,96},{1,17},{17,1},{65,... | collective-permute-start | bytes 14155784 | tf_op jit(solution)/shard_map/cond/branch_13_fun/ppermute | solution.py:214
  339.5 10.2 %collective-permute-start.25 = (bf16[768,3072]{1,0:T(8,128)(2,1)}, bf16[768,3072]{1,0:T(8,128)(2,1)}, u32[]{:S(2)}, u32[]{:S(2)}) collective-permute-start(bf16[768,3072]{1,0:T(8,128)(2,1)} %get-tuple-element.85), channel_id=1, source_target_pairs={{0,16},{16,0},{64,80},{80,64},{96,112},{112,96},{1,17},{17,1},{65,... | collective-permute-start | bytes 14155784 | tf_op jit(solution)/shard_map/cond/branch_13_fun/ppermute | solution.py:214
  349.7 93.9 %collective-permute-done.24 = bf16[3072,768]{1,0:T(8,128)(2,1)} collective-permute-done((bf16[3072,768]{1,0:T(8,128)(2,1)}, bf16[3072,768]{1,0:T(8,128)(2,1)}, u32[]{:S(2)}, u32[]{:S(2)}) %collective-permute-start.24) | collective-permute-done | bytes 4718624 | tf_op jit(solution)/shard_map/cond/branch_13_fun/ppermute | solution.py:214
  443.6 100.6 %collective-permute-done.25 = bf16[768,3072]{1,0:T(8,128)(2,1)} collective-permute-done((bf16[768,3072]{1,0:T(8,128)(2,1)}, bf16[768,3072]{1,0:T(8,128)(2,1)}, u32[]{:S(2)}, u32[]{:S(2)}) %collective-permute-start.25) | collective-permute-done | bytes 4718624 | tf_op jit(solution)/shard_map/cond/branch_13_fun/ppermute | solution.py:214
  544.2 9.5 %fusion = bf16[1,3072,768]{2,1,0:T(8,128)(2,1)} fusion(bf16[3072,768]{1,0:T(8,128)(2,1)} %subtract_convert_fusion.1, bf16[3072,768]{1,0:T(8,128)(2,1)} %get-tuple-element.94, pred[]{:T(512)S(6)} %ne.7), kind=kLoop, calls=%fused_computation.4 | loop fusion | flops 14155776 | bytes 14155777 | tf_op jit(solution)/shard_map/broadcast_in_dim | solution.py:303
  553.7 6.6 %fusion.1 = bf16[1,768,3072]{2,1,0:T(8,128)(2,1)} fusion(bf16[768,3072]{1,0:T(8,128)(2,1)S(1)} %copy-done, bf16[768,3072]{1,0:T(8,128)(2,1)} %get-tuple-element.95, pred[]{:T(512)S(6)} %ne.7), kind=kLoop, calls=%fused_computation.5 | loop fusion | flops 14155776 | bytes 14155777 | tf_op jit(solution)/shard_map/broadcast_in_dim | solution.py:303
  (238 shorter events, 100.3 us)
Async XLA Ops:
  7.9 28.9 %copy-start.14 = (s32[2,3,2,4]{3,2,1,0:T(2,128)S(1)}, s32[2,3,2,4]{3,2,1,0:T(2,128)}, u32[]{:S(2)}) copy-start(s32[2,3,2,4]{3,2,1,0:T(2,128)} %param.23) | copy-start | bytes 580
  8.0 31.9 %copy-start.6 = (bf16[2,4,1,3072]{3,1,2,0:T(4,128)(2,1)S(1)}, bf16[2,4,1,3072]{3,1,2,0:T(4,128)(2,1)}, u32[]{:S(2)}) copy-start(bf16[2,4,1,3072]{3,1,2,0:T(4,128)(2,1)} %param.24) | copy-start | bytes 147460
  35.5 5.6 %collective-permute-start.31 = (bf16[1,2,2,3072]{3,2,1,0:T(2,128)(2,1)S(1)}, bf16[1,2,2,3072]{3,2,1,0:T(2,128)(2,1)S(1)}, u32[]{:S(2)}, u32[]{:S(2)}) collective-permute-start(bf16[1,2,2,3072]{3,2,1,0:T(2,128)(2,1)S(1)} %add_convert_fusion.2), channel_id=1, source_target_pairs={{0,48},{16,32},{1,49},{17,33},{2,50},{18,34},{3,51},{19,35},{4,52}... | collective-permute-start | bytes 73736 | tf_op jit(solution)/shard_map/ppermute | solution.py:202
  36.2 5.0 collective-permute-start.30
  60.2 33.2 %collective-permute-start.33 = (bf16[1,2,4,3072]{3,2,1,0:T(4,128)(2,1)S(1)}, bf16[1,2,4,3072]{3,2,1,0:T(4,128)(2,1)S(1)}, u32[]{:S(2)}, u32[]{:S(2)}) collective-permute-start(bf16[1,2,4,3072]{3,2,1,0:T(4,128)(2,1)S(1)} %add_convert_fusion.1), channel_id=1, source_target_pairs={{32,80},{48,64},{33,81},{49,65},{34,82},{50,66},{35,83},{51,67},{3... | collective-permute-start | bytes 147464 | tf_op jit(solution)/shard_map/ppermute | solution.py:202
  61.5 33.8 %collective-permute-start.32 = (bf16[1,2,4,3072]{3,2,1,0:T(4,128)(2,1)S(1)}, bf16[1,2,4,3072]{3,2,1,0:T(4,128)(2,1)S(1)}, u32[]{:S(2)}, u32[]{:S(2)}) collective-permute-start(bf16[1,2,4,3072]{3,2,1,0:T(4,128)(2,1)S(1)} %add_convert_fusion.1), channel_id=1, source_target_pairs={{32,64},{48,80},{33,65},{49,81},{34,66},{50,82},{35,67},{51,83},{3... | collective-permute-start | bytes 147464 | tf_op jit(solution)/shard_map/ppermute | solution.py:202
  121.8 24.3 %copy-start.16 = (bf16[2,2,4,1,4]{4,3,2,0,1:T(2,128)(2,1)S(1)}, bf16[2,2,4,1,4]{4,3,2,0,1:T(2,128)(2,1)}, u32[]{:S(2)}) copy-start(bf16[2,2,4,1,4]{4,3,2,0,1:T(2,128)(2,1)} %get-tuple-element.124) | copy-start | bytes 388
  138.7 7.3 %collective-permute-start.35 = (bf16[1,2,4,3072]{3,2,1,0:T(4,128)(2,1)S(1)}, bf16[1,2,4,3072]{3,2,1,0:T(4,128)(2,1)S(1)}, u32[]{:S(2)}, u32[]{:S(2)}) collective-permute-start(bf16[1,2,4,3072]{3,2,1,0:T(4,128)(2,1)S(1)} %add_convert_fusion), channel_id=1, source_target_pairs={{64,112},{80,96},{65,113},{81,97},{66,114},{82,98},{67,115},{83,99... | collective-permute-start | bytes 147464 | tf_op jit(solution)/shard_map/ppermute | solution.py:202
  140.0 6.1 %collective-permute-start.34 = (bf16[1,2,4,3072]{3,2,1,0:T(4,128)(2,1)S(1)}, bf16[1,2,4,3072]{3,2,1,0:T(4,128)(2,1)S(1)}, u32[]{:S(2)}, u32[]{:S(2)}) collective-permute-start(bf16[1,2,4,3072]{3,2,1,0:T(4,128)(2,1)S(1)} %add_convert_fusion), channel_id=1, source_target_pairs={{64,96},{80,112},{65,97},{81,113},{66,98},{82,114},{67,99},{83,115... | collective-permute-start | bytes 147464 | tf_op jit(solution)/shard_map/ppermute | solution.py:202
  156.9 28.6 %copy-start.7 = (bf16[2,4,1,3072]{3,1,2,0:T(4,128)(2,1)S(1)}, bf16[2,4,1,3072]{3,1,2,0:T(4,128)(2,1)}, u32[]{:S(2)}) copy-start(bf16[2,4,1,3072]{3,1,2,0:T(4,128)(2,1)} %param.24) | copy-start | bytes 147460
  156.9 28.6 %copy-start.11 = (f32[2,4]{1,0:T(2,128)S(1)}, f32[2,4]{1,0:T(2,128)}, u32[]{:S(2)}) copy-start(f32[2,4]{1,0:T(2,128)} %fusion.214) | copy-start | bytes 100
  156.9 28.6 %copy-start.21 = (pred[2,1,4]{2,0,1:T(4,128)(4,1)S(1)}, pred[2,1,4]{2,0,1:T(4,128)(4,1)}, u32[]{:S(2)}) copy-start(pred[2,1,4]{2,0,1:T(4,128)(4,1)} %copy-done.20) | copy-start | bytes 28
  156.9 31.3 %copy-start.22 = (s32[4,2]{0,1:T(2,128)S(1)}, s32[4,2]{0,1:T(2,128)}, u32[]{:S(2)}) copy-start(s32[4,2]{0,1:T(2,128)} %param.25) | copy-start | bytes 100
  164.4 36.9 %copy-start.18 = (bf16[2,4,2,4]{3,2,1,0:T(2,128)(2,1)S(1)}, bf16[2,4,2,4]{3,2,1,0:T(2,128)(2,1)}, u32[]{:S(2)}) copy-start(bf16[2,4,2,4]{3,2,1,0:T(2,128)(2,1)} %get-tuple-element.126) | copy-start | bytes 388
  185.6 15.6 %collective-permute-start.37 = (bf16[1,2,4,3072]{3,2,1,0:T(4,128)(2,1)S(1)}, bf16[1,2,4,3072]{3,2,1,0:T(4,128)(2,1)S(1)}, u32[]{:S(2)}, u32[]{:S(2)}) collective-permute-start(bf16[1,2,4,3072]{3,2,1,0:T(4,128)(2,1)S(1)} %subtract_convert_fusion.2), channel_id=1, source_target_pairs={{96,80},{112,64},{97,81},{113,65},{98,82},{114,66},{99,83},{115,67... | collective-permute-start | bytes 147464 | tf_op jit(solution)/shard_map/ppermute | solution.py:202
  186.9 14.3 %collective-permute-start.36 = (bf16[1,2,4,3072]{3,2,1,0:T(4,128)(2,1)S(1)}, bf16[1,2,4,3072]{3,2,1,0:T(4,128)(2,1)S(1)}, u32[]{:S(2)}, u32[]{:S(2)}) collective-permute-start(bf16[1,2,4,3072]{3,2,1,0:T(4,128)(2,1)S(1)} %subtract_convert_fusion.2), channel_id=1, source_target_pairs={{96,64},{112,80},{97,65},{113,81},{98,66},{114,82},{99,67},{115,83... | collective-permute-start | bytes 147464 | tf_op jit(solution)/shard_map/ppermute | solution.py:202
  217.6 24.7 %copy-start.12 = (f32[2,4]{1,0:T(2,128)S(1)}, f32[2,4]{1,0:T(2,128)}, u32[]{:S(2)}) copy-start(f32[2,4]{1,0:T(2,128)} %fusion.214) | copy-start | bytes 100
  225.1 24.3 %copy-start.17 = (bf16[2,4,2,4]{3,2,1,0:T(2,128)(2,1)S(1)}, bf16[2,4,2,4]{3,2,1,0:T(2,128)(2,1)}, u32[]{:S(2)}) copy-start(bf16[2,4,2,4]{3,2,1,0:T(2,128)(2,1)} %get-tuple-element.125) | copy-start | bytes 388
  242.5 6.9 %collective-permute-start.39 = (bf16[1,2,4,3072]{3,2,1,0:T(4,128)(2,1)S(1)}, bf16[1,2,4,3072]{3,2,1,0:T(4,128)(2,1)S(1)}, u32[]{:S(2)}, u32[]{:S(2)}) collective-permute-start(bf16[1,2,4,3072]{3,2,1,0:T(4,128)(2,1)S(1)} %fusion.180), channel_id=1, source_target_pairs={{64,48},{80,32},{65,49},{81,33},{66,50},{82,34},{67,51},{83,35},{6... | collective-permute-start | bytes 147464 | tf_op jit(solution)/shard_map/ppermute | solution.py:202
  244.2 5.2 collective-permute-start.38
  274.4 5.5 collective-permute-start.41
  275.7 4.3 collective-permute-start.40
  301.1 142.5 %collective-permute-start.24 = (bf16[3072,768]{1,0:T(8,128)(2,1)}, bf16[3072,768]{1,0:T(8,128)(2,1)}, u32[]{:S(2)}, u32[]{:S(2)}) collective-permute-start(bf16[3072,768]{1,0:T(8,128)(2,1)} %get-tuple-element.84), channel_id=1, source_target_pairs={{0,16},{16,0},{64,80},{80,64},{96,112},{112,96},{1,17},{17,1},{65,... | collective-permute-start | bytes 14155784 | tf_op jit(solution)/shard_map/cond/branch_13_fun/ppermute | solution.py:214
  339.5 204.7 %collective-permute-start.25 = (bf16[768,3072]{1,0:T(8,128)(2,1)}, bf16[768,3072]{1,0:T(8,128)(2,1)}, u32[]{:S(2)}, u32[]{:S(2)}) collective-permute-start(bf16[768,3072]{1,0:T(8,128)(2,1)} %get-tuple-element.85), channel_id=1, source_target_pairs={{0,16},{16,0},{64,80},{80,64},{96,112},{112,96},{1,17},{17,1},{65,... | collective-permute-start | bytes 14155784 | tf_op jit(solution)/shard_map/cond/branch_13_fun/ppermute | solution.py:214
  (15 other events, 165.0 us)

commit v10 on v9

--- a/solution.py
+++ b/solution.py
@@ -234,7 +234,13 @@
         filler = jnp.zeros(full.shape[:2] + (capacity - full.shape[2],) + full.shape[3:], full.dtype)
         return jnp.concatenate([full, filler], axis=2)
 
+    last_live = lax.dynamic_index_in_dim(live_list[section_count - 1], replica, 1, keepdims=False)
+    up_piece = jnp.where(
+        last_live[None, :, :, None], cotangent.transpose(2, 0, 1, 3), jnp.zeros((), jnp.bfloat16)
+    )
+    up_full = gather_rows(up_piece, section_count - 1)
     x_cur = gather_rows(block_inputs.transpose(2, 0, 1, 3), 0)
+    x_cur, up_full = lax.optimization_barrier((x_cur, up_full))
     x_keep = padded(x_cur)
     for bound in range(section_count - 1):
         piece = forward_piece(x_cur, weight_in, weight_out, scale_in, scale_out, shard_idx, bound)
@@ -251,11 +257,6 @@
         x_cur = gather_rows(routed, bound + 1)
         x_keep = jnp.where(my_section == bound + 1, x_cur, x_keep)
 
-    last_live = lax.dynamic_index_in_dim(live_list[section_count - 1], replica, 1, keepdims=False)
-    up_piece = jnp.where(
-        last_live[None, :, :, None], cotangent.transpose(2, 0, 1, 3), jnp.zeros((), jnp.bfloat16)
-    )
-    up_full = gather_rows(up_piece, section_count - 1)
     up_keep = up_full
     for depth in reversed(range(1, section_count)):
         grad_piece = backward_piece(

time: 570 us -> 595 us (1.044)
  local copies, waits for them, and re-layouts: 39.1 us -> 47.7 us
  Pallas kernels: 112 us -> 118 us
    pallas_call x14, Pallas kernels: 112 us -> 118 us  [plane_dense(): pl.pallas_call(lambda *refs: plane_kernel(count, spread, active, *refs),...]
    reshape x5 -> x8, local copies, waits for them, and re-layouts: 8.26 us -> 12.7 us  [plane_call(): return dense.reshape((count,) + value.shape[1:])]
  transfers between devices with their start and end apart: 14 -> 14, of which waited for: 5 -> 6; matrix products, arithmetic and copies ran while one was open for 2% -> 1% of each run, Pallas kernels for 0% -> 0%
where the time goes in v10:
time: 595 us; the launch traced here: 584 us
  waiting for transfers between devices  244 us (41%)
  Pallas kernels  118 us (20%)
  matrix products  62.1 us (10%)
  starting transfers between devices  61.8 us (10%)
  other arithmetic  47.7 us (8%)
  local copies, waits for them, and re-layouts  47.7 us (8%)
    pallas_call x14, Pallas kernels, plane_dense(): pl.pallas_call(lambda *refs: plane_kernel(count, spread, active, *refs),...  118 us
    ppermute x1, waiting for transfers between devices, swap_sections(): lax.ppermute(stepped_out, PAIR, pairs)  101 us
    ppermute x1, waiting for transfers between devices, swap_sections(): lax.ppermute(stepped_in, PAIR, pairs)  93.9 us
    ppermute x6, waiting for transfers between devices, cross_boundary(): lax.ppermute(piece, PAIR, crossed)  46.4 us
    ppermute x1, starting transfers between devices, swap_sections(): lax.ppermute(stepped_in, PAIR, pairs)  36.8 us
    dot_general x3, matrix products, backward_piece(): lax.dot_general(d_pre, weight_in, (((1,), (1,)), ((), ())), preferred_ele...  23.4 us
    dot_general x3, matrix products, forward_piece(): jnp.dot(activated, weight_out, preferred_element_type=jnp.float32)  18.5 us
    broadcast_in_dim x2, other arithmetic, on_device(): return (new_in[None], new_out[None])  16.1 us
  transfers between devices with their start and end apart: 14, of which 6 were waited for; matrix products, arithmetic and copies ran while one was open for 1% of the time, Pallas kernels for 0%

profile of v10, /device:TPU:16, one launch (start us, length us, event | category | flops | bytes accessed | tf_op | source)
XLA Modules:
  0.0 584.0 jit_solution(13226581773589442079)
XLA Ops:
  17.8 5.9 %fusion.63 = bf16[64,3072]{1,0:T(8,128)(2,1)S(1)} fusion(bf16[1,768,3072]{2,1,0:T(8,128)(2,1)} %param.27, bf16[64,3072]{1,0:T(8,128)(2,1)S(1)} %convert_element_type.358, bf16[1,3072,768]{2,1,0:T(8,128)(2,1)} %param.26), kind=kOutput, calls=%fused_computation.45 | convolution fusion | flops 604864512 | bytes 10223616 | tf_op jit(solution)/shard_map/dot_general | solution.py:139
  24.7 21.9 %shard_map.79 = bf16[16,16,768]{2,1,0:T(8,128)(2,1)} custom-call(bf16[16,16,768]{2,1,0:T(8,128)(2,1)} %convert_element_type.361.refs_0_), custom_call_target="tpu_custom_call" | custom-call | tf_op jit(solution)/shard_map/pallas_call | solution.py:107
  58.6 5.9 %fusion.48 = bf16[128,3072]{1,0:T(8,128)(2,1)S(1)} fusion(bf16[1,768,3072]{2,1,0:T(8,128)(2,1)} %param.27, bf16[128,3072]{1,0:T(8,128)(2,1)} %convert_element_type.368, bf16[1,3072,768]{2,1,0:T(8,128)(2,1)} %param.26), kind=kOutput, calls=%fused_computation.40 | convolution fusion | flops 1209729024 | bytes 11010048 | tf_op jit(solution)/shard_map/dot_general | solution.py:139
  72.1 34.6 %collective-permute-done.33 = bf16[1,2,4,3072]{3,2,1,0:T(4,128)(2,1)S(1)} collective-permute-done((bf16[1,2,4,3072]{3,2,1,0:T(4,128)(2,1)S(1)}, bf16[1,2,4,3072]{3,2,1,0:T(4,128)(2,1)S(1)}, u32[]{:S(2)}, u32[]{:S(2)}) %collective-permute-start.33) | collective-permute-done | bytes 49184 | tf_op jit(solution)/shard_map/ppermute | solution.py:202
  109.6 14.3 %shard_map.82 = bf16[16,16,1536]{2,1,0:T(8,128)(2,1)} custom-call(bf16[1,16,1536]{2,1,0:T(8,128)(2,1)} %reshape_broadcast_in_dim.19.refs_0_), custom_call_target="tpu_custom_call" | custom-call | tf_op jit(solution)/shard_map/pallas_call | solution.py:107
  132.0 6.8 %fusion.45 = bf16[128,3072]{1,0:T(8,128)(2,1)} fusion(bf16[1,768,3072]{2,1,0:T(8,128)(2,1)} %param.27, bf16[128,3072]{1,0:T(8,128)(2,1)} %convert_element_type.378, bf16[1,3072,768]{2,1,0:T(8,128)(2,1)} %param.26), kind=kOutput, calls=%fused_computation.39 | convolution fusion | flops 1209729024 | bytes 11010048 | tf_op jit(solution)/shard_map/dot_general | solution.py:139
  140.9 14.4 %shard_map.83 = bf16[16,16,1536]{2,1,0:T(8,128)(2,1)} custom-call(bf16[16,16,1536]{2,1,0:T(8,128)(2,1)} %convert_element_type.381.refs_0_), custom_call_target="tpu_custom_call" | custom-call | tf_op jit(solution)/shard_map/pallas_call | solution.py:107
  169.8 3.2 fusion.22
  173.1 7.5 %fusion.57 = bf16[128,3072]{1,0:T(8,128)(2,1)S(1)} fusion(bf16[1,3072,768]{2,1,0:T(8,128)(2,1)} %param.26, bf16[128,3072]{1,0:T(8,128)(2,1)S(1)} %copy-done.5, bf16[1,768,3072]{2,1,0:T(8,128)(2,1)} %param.27, f32[128,768]{1,0:T(8,128)S(1)} %fusion.22), kind=kOutput, calls=%fused_computation.43 | convolution fusion | flops 1210810368 | bytes 11403264 | tf_op jit(solution)/shard_map/dot_general | solution.py:159
  181.7 22.1 %shard_map.85 = bf16[16,16,1536]{2,1,0:T(8,128)(2,1)} custom-call(bf16[16,16,1536]{2,1,0:T(8,128)(2,1)} %convert_element_type.398.refs_0_), custom_call_target="tpu_custom_call" | custom-call | tf_op jit(solution)/shard_map/pallas_call | solution.py:107
  210.1 11.7 %collective-permute-done.37 = bf16[1,2,4,3072]{3,2,1,0:T(4,128)(2,1)S(1)} collective-permute-done((bf16[1,2,4,3072]{3,2,1,0:T(4,128)(2,1)S(1)}, bf16[1,2,4,3072]{3,2,1,0:T(4,128)(2,1)S(1)}, u32[]{:S(2)}, u32[]{:S(2)}) %collective-permute-start.37) | collective-permute-done | bytes 49184 | tf_op jit(solution)/shard_map/ppermute | solution.py:202
  222.7 14.1 %shard_map.86 = bf16[16,16,1536]{2,1,0:T(8,128)(2,1)} custom-call(bf16[1,16,1536]{2,1,0:T(8,128)(2,1)} %reshape_broadcast_in_dim.21.refs_0_), custom_call_target="tpu_custom_call" | custom-call | tf_op jit(solution)/shard_map/pallas_call | solution.py:107
  238.2 7.5 %fusion.54 = bf16[128,3072]{1,0:T(8,128)(2,1)S(1)} fusion(bf16[1,3072,768]{2,1,0:T(8,128)(2,1)} %param.26, bf16[128,3072]{1,0:T(8,128)(2,1)S(1)} %reshape_reshape.8, bf16[1,768,3072]{2,1,0:T(8,128)(2,1)} %param.27, f32[128,768]{1,0:T(8,128)S(1)} %fusion.22), kind=kOutput, calls=%fused_computation.42 | convolution fusion | flops 1210810368 | bytes 11403264 | tf_op jit(solution)/shard_map/dot_general | solution.py:159
  246.8 14.6 %shard_map.87 = bf16[16,16,1536]{2,1,0:T(8,128)(2,1)} custom-call(bf16[16,16,1536]{2,1,0:T(8,128)(2,1)} %convert_element_type.406.refs_0_), custom_call_target="tpu_custom_call" | custom-call | tf_op jit(solution)/shard_map/pallas_call | solution.py:107
  272.9 8.4 %fusion.51 = bf16[128,3072]{1,0:T(8,128)(2,1)} fusion(bf16[1,3072,768]{2,1,0:T(8,128)(2,1)} %param.26, bf16[128,3072]{1,0:T(8,128)(2,1)S(1)} %reshape_reshape.9, bf16[1,768,3072]{2,1,0:T(8,128)(2,1)} %param.27, f32[128,768]{1,0:T(8,128)S(1)} %fusion.22), kind=kOutput, calls=%fused_computation.41 | convolution fusion | flops 1210810368 | bytes 11403264 | tf_op jit(solution)/shard_map/dot_general | solution.py:159
  310.5 6.0 %subtract_convert_fusion = bf16[768,3072]{1,0:T(8,128)(2,1)} fusion(bf16[128,3072]{1,0:T(8,128)(2,1)S(1)} %reshape.405, bf16[1,768,3072]{2,1,0:T(8,128)(2,1)} %param.27, f32[128,768]{1,0:T(8,128)S(1)} %fusion.22), kind=kOutput, calls=%fused_computation.2 | convolution fusion | flops 614400000 | bytes 10616832 | tf_op jit(solution)/shard_map/dot_general | solution.py:184
  316.5 9.5 %subtract_convert_fusion.1 = bf16[3072,768]{1,0:T(8,128)(2,1)} fusion(bf16[1,3072,768]{2,1,0:T(8,128)(2,1)} %param.26, f32[128,3072]{1,0:T(8,128)S(1)} %copy-done.3, f32[128]{0:T(128)S(1)} %copy-done.12, bf16[128,3072]{1,0:T(8,128)(2,1)S(1)} %reshape.405, bf16[1,768,3072]{2,1,0:T(8,128)(2,1)} %param.27, f32[128,768]{1,0:T(8,128)S(1)} %fusion.22), kind=kOutput, calls=%fused_computation.3 | convolution fusion | flops 1220247552 | bytes 16908800 | tf_op jit(solution)/shard_map/dot_general | solution.py:193
  326.0 241.7 %conditional.1 = (bf16[3072,768]{1,0:T(8,128)(2,1)}, bf16[768,3072]{1,0:T(8,128)(2,1)}) conditional(s32[]{:T(128)} %clamp.3, () %tuple.74, (bf16[3072,768]{1,0:T(8,128)(2,1)}, bf16[768,3072]{1,0:T(8,128)(2,1)}) %tuple.75, (bf16[3072,768]{1,0:T(8,128)(2,1)}, bf16[768,3072]{1,0:T(8,128)(2,1)}) %tuple.75, ...), branch_computations={%region_25.26_spmd, %region_26.27_spmd, %region_27.28_spmd, %regio... | conditional | bytes 37748832 | solution.py:287
  326.2 36.8 %collective-permute-start.26 = (bf16[3072,768]{1,0:T(8,128)(2,1)}, bf16[3072,768]{1,0:T(8,128)(2,1)}, u32[]{:S(2)}, u32[]{:S(2)}) collective-permute-start(bf16[3072,768]{1,0:T(8,128)(2,1)} %get-tuple-element.86), channel_id=1, source_target_pairs={{32,48},{48,32},{64,80},{80,64},{96,112},{112,96},{33,49},{49,33},... | collective-permute-start | bytes 14155784 | tf_op jit(solution)/shard_map/cond/branch_14_fun/ppermute | solution.py:214
  363.0 10.2 %collective-permute-start.27 = (bf16[768,3072]{1,0:T(8,128)(2,1)}, bf16[768,3072]{1,0:T(8,128)(2,1)}, u32[]{:S(2)}, u32[]{:S(2)}) collective-permute-start(bf16[768,3072]{1,0:T(8,128)(2,1)} %get-tuple-element.87), channel_id=1, source_target_pairs={{32,48},{48,32},{64,80},{80,64},{96,112},{112,96},{33,49},{49,33},... | collective-permute-start | bytes 14155784 | tf_op jit(solution)/shard_map/cond/branch_14_fun/ppermute | solution.py:214
  373.2 93.9 %collective-permute-done.26 = bf16[3072,768]{1,0:T(8,128)(2,1)} collective-permute-done((bf16[3072,768]{1,0:T(8,128)(2,1)}, bf16[3072,768]{1,0:T(8,128)(2,1)}, u32[]{:S(2)}, u32[]{:S(2)}) %collective-permute-start.26) | collective-permute-done | bytes 4718624 | tf_op jit(solution)/shard_map/cond/branch_14_fun/ppermute | solution.py:214
  467.1 100.6 %collective-permute-done.27 = bf16[768,3072]{1,0:T(8,128)(2,1)} collective-permute-done((bf16[768,3072]{1,0:T(8,128)(2,1)}, bf16[768,3072]{1,0:T(8,128)(2,1)}, u32[]{:S(2)}, u32[]{:S(2)}) %collective-permute-start.27) | collective-permute-done | bytes 4718624 | tf_op jit(solution)/shard_map/cond/branch_14_fun/ppermute | solution.py:214
  567.7 9.5 %fusion = bf16[1,3072,768]{2,1,0:T(8,128)(2,1)} fusion(bf16[3072,768]{1,0:T(8,128)(2,1)} %subtract_convert_fusion.1, bf16[3072,768]{1,0:T(8,128)(2,1)} %get-tuple-element.98, pred[]{:T(512)S(6)} %ne.7), kind=kLoop, calls=%fused_computation.4 | loop fusion | flops 14155776 | bytes 14155777 | tf_op jit(solution)/shard_map/broadcast_in_dim | solution.py:304
  577.2 6.6 %fusion.1 = bf16[1,768,3072]{2,1,0:T(8,128)(2,1)} fusion(bf16[768,3072]{1,0:T(8,128)(2,1)S(1)} %copy-done, bf16[768,3072]{1,0:T(8,128)(2,1)} %get-tuple-element.99, pred[]{:T(512)S(6)} %ne.7), kind=kLoop, calls=%fused_computation.5 | loop fusion | flops 14155776 | bytes 14155777 | tf_op jit(solution)/shard_map/broadcast_in_dim | solution.py:304
  (217 shorter events, 115.0 us)
Async XLA Ops:
  3.1 46.0 %copy-start.9 = (bf16[2,2,4,2,4]{4,3,2,0,1:T(2,128)(2,1)}, bf16[2,2,4,2,4]{4,3,2,0,1:T(2,128)(2,1)S(1)}, u32[]{:S(2)}) copy-start(bf16[2,2,4,2,4]{4,3,2,0,1:T(2,128)(2,1)S(1)} %get-tuple-element.122) | copy-start | bytes 772
  4.7 67.4 %copy-start.8 = (bf16[2,2,4,2,4]{4,3,2,0,1:T(2,128)(2,1)}, bf16[2,2,4,2,4]{4,3,2,0,1:T(2,128)(2,1)S(1)}, u32[]{:S(2)}) copy-start(bf16[2,2,4,2,4]{4,3,2,0,1:T(2,128)(2,1)S(1)} %get-tuple-element.120) | copy-start | bytes 772
  6.2 42.9 %copy-start.10 = (bf16[2,2,4,2,4]{4,3,2,0,1:T(2,128)(2,1)}, bf16[2,2,4,2,4]{4,3,2,0,1:T(2,128)(2,1)S(1)}, u32[]{:S(2)}) copy-start(bf16[2,2,4,2,4]{4,3,2,0,1:T(2,128)(2,1)S(1)} %get-tuple-element.118) | copy-start | bytes 772
  47.7 1.4 collective-permute-start.31
  48.4 0.8 collective-permute-start.30
  69.3 37.4 %collective-permute-start.33 = (bf16[1,2,4,3072]{3,2,1,0:T(4,128)(2,1)S(1)}, bf16[1,2,4,3072]{3,2,1,0:T(4,128)(2,1)S(1)}, u32[]{:S(2)}, u32[]{:S(2)}) collective-permute-start(bf16[1,2,4,3072]{3,2,1,0:T(4,128)(2,1)S(1)} %add_convert_fusion.1), channel_id=1, source_target_pairs={{32,80},{48,64},{33,81},{49,65},{34,82},{50,66},{35,83},{51,67},{3... | collective-permute-start | bytes 147464 | tf_op jit(solution)/shard_map/ppermute | solution.py:202
  70.6 38.0 %collective-permute-start.32 = (bf16[1,2,4,3072]{3,2,1,0:T(4,128)(2,1)S(1)}, bf16[1,2,4,3072]{3,2,1,0:T(4,128)(2,1)S(1)}, u32[]{:S(2)}, u32[]{:S(2)}) collective-permute-start(bf16[1,2,4,3072]{3,2,1,0:T(4,128)(2,1)S(1)} %add_convert_fusion.1), channel_id=1, source_target_pairs={{32,64},{48,80},{33,65},{49,81},{34,66},{50,82},{35,67},{51,83},{3... | collective-permute-start | bytes 147464 | tf_op jit(solution)/shard_map/ppermute | solution.py:202
  127.2 29.4 %copy-start.4 = (bf16[16,2,4,3072]{3,2,1,0:T(4,128)(2,1)}, bf16[16,2,4,3072]{3,2,1,0:T(4,128)(2,1)S(1)}, u32[]{:S(2)}) copy-start(bf16[16,2,4,3072]{3,2,1,0:T(4,128)(2,1)S(1)} %reshape.399) | copy-start | bytes 2359300
  156.7 3.7 collective-permute-start.35
  158.0 2.4 collective-permute-start.34
  206.2 15.6 %collective-permute-start.37 = (bf16[1,2,4,3072]{3,2,1,0:T(4,128)(2,1)S(1)}, bf16[1,2,4,3072]{3,2,1,0:T(4,128)(2,1)S(1)}, u32[]{:S(2)}, u32[]{:S(2)}) collective-permute-start(bf16[1,2,4,3072]{3,2,1,0:T(4,128)(2,1)S(1)} %subtract_convert_fusion.2), channel_id=1, source_target_pairs={{96,80},{112,64},{97,81},{113,65},{98,82},{114,66},{99,83},{115,67... | collective-permute-start | bytes 147464 | tf_op jit(solution)/shard_map/ppermute | solution.py:202
  207.5 14.3 %collective-permute-start.36 = (bf16[1,2,4,3072]{3,2,1,0:T(4,128)(2,1)S(1)}, bf16[1,2,4,3072]{3,2,1,0:T(4,128)(2,1)S(1)}, u32[]{:S(2)}, u32[]{:S(2)}) collective-permute-start(bf16[1,2,4,3072]{3,2,1,0:T(4,128)(2,1)S(1)} %subtract_convert_fusion.2), channel_id=1, source_target_pairs={{96,64},{112,80},{97,65},{113,81},{98,66},{114,82},{99,67},{115,83... | collective-permute-start | bytes 147464 | tf_op jit(solution)/shard_map/ppermute | solution.py:202
  222.1 14.7 %copy-start.7 = (bf16[2,4,3072]{2,1,0:T(4,128)(2,1)}, bf16[2,4,3072]{2,1,0:T(4,128)(2,1)S(1)}, u32[]{:S(2)}) copy-start(bf16[2,4,3072]{2,1,0:T(4,128)(2,1)S(1)} %fusion.68) | copy-start | bytes 147460
  245.7 21.2 %copy-start.14 = (s32[4,2]{0,1:T(2,128)S(1)}, s32[4,2]{0,1:T(2,128)}, u32[]{:S(2)}) copy-start(s32[4,2]{0,1:T(2,128)} %param.25) | copy-start | bytes 100
  245.7 22.9 %copy-start.11 = (bf16[2,4,2,4]{3,2,1,0:T(2,128)(2,1)S(1)}, bf16[2,4,2,4]{3,2,1,0:T(2,128)(2,1)}, u32[]{:S(2)}) copy-start(bf16[2,4,2,4]{3,2,1,0:T(2,128)(2,1)} %get-tuple-element.129) | copy-start | bytes 388
  263.8 3.6 collective-permute-start.39
  265.5 3.0 collective-permute-start.38
  281.3 20.6 %copy-start.1 = (bf16[16,16,1536]{2,1,0:T(8,128)(2,1)S(1)}, bf16[16,16,1536]{2,1,0:T(8,128)(2,1)}, u32[]{:S(2)}) copy-start(bf16[16,16,1536]{2,1,0:T(8,128)(2,1)} %shard_map.86) | copy-start | bytes 2359300
  281.3 21.1 %copy-start.2 = (bf16[16,16,1536]{2,1,0:T(8,128)(2,1)S(1)}, bf16[16,16,1536]{2,1,0:T(8,128)(2,1)}, u32[]{:S(2)}) copy-start(bf16[16,16,1536]{2,1,0:T(8,128)(2,1)} %shard_map.88) | copy-start | bytes 2359300
  293.6 9.2 %collective-permute-start.41 = (bf16[1,2,4,3072]{3,2,1,0:T(4,128)(2,1)}, bf16[1,2,4,3072]{3,2,1,0:T(4,128)(2,1)}, u32[]{:S(2)}, u32[]{:S(2)}) collective-permute-start(bf16[1,2,4,3072]{3,2,1,0:T(4,128)(2,1)} %fusion.179), channel_id=1, source_target_pairs={{32,16},{48,0},{33,17},{49,1},{34,18},{50,2},{35,19},{51,3},{36,20... | collective-permute-start | bytes 147464 | tf_op jit(solution)/shard_map/ppermute | solution.py:202
  294.9 8.0 %collective-permute-start.40 = (bf16[1,2,4,3072]{3,2,1,0:T(4,128)(2,1)}, bf16[1,2,4,3072]{3,2,1,0:T(4,128)(2,1)}, u32[]{:S(2)}, u32[]{:S(2)}) collective-permute-start(bf16[1,2,4,3072]{3,2,1,0:T(4,128)(2,1)} %fusion.179), channel_id=1, source_target_pairs={{32,0},{48,16},{33,1},{49,17},{34,2},{50,18},{35,3},{51,19},{36,4}... | collective-permute-start | bytes 147464 | tf_op jit(solution)/shard_map/ppermute | solution.py:202
  326.2 140.9 %collective-permute-start.26 = (bf16[3072,768]{1,0:T(8,128)(2,1)}, bf16[3072,768]{1,0:T(8,128)(2,1)}, u32[]{:S(2)}, u32[]{:S(2)}) collective-permute-start(bf16[3072,768]{1,0:T(8,128)(2,1)} %get-tuple-element.86), channel_id=1, source_target_pairs={{32,48},{48,32},{64,80},{80,64},{96,112},{112,96},{33,49},{49,33},... | collective-permute-start | bytes 14155784 | tf_op jit(solution)/shard_map/cond/branch_14_fun/ppermute | solution.py:214
  363.0 204.7 %collective-permute-start.27 = (bf16[768,3072]{1,0:T(8,128)(2,1)}, bf16[768,3072]{1,0:T(8,128)(2,1)}, u32[]{:S(2)}, u32[]{:S(2)}) collective-permute-start(bf16[768,3072]{1,0:T(8,128)(2,1)} %get-tuple-element.87), channel_id=1, source_target_pairs={{32,48},{48,32},{64,80},{80,64},{96,112},{112,96},{33,49},{49,33},... | collective-permute-start | bytes 14155784 | tf_op jit(solution)/shard_map/cond/branch_14_fun/ppermute | solution.py:214
  567.7 9.5 %copy-start = (bf16[768,3072]{1,0:T(8,128)(2,1)S(1)}, bf16[768,3072]{1,0:T(8,128)(2,1)}, u32[]{:S(2)}) copy-start(bf16[768,3072]{1,0:T(8,128)(2,1)} %subtract_convert_fusion) | copy-start | bytes 14155780
  (6 other events, 19.6 us)
